TPU v7x, 128 devices: a whole 4x4x4 slice. The times are simulated.
128 devices in a mesh: seq: 32 (over x, z, core), feat: 4 (over y).
Axes of the slice: x: 4, y: 4, z: 4, core: 2. Of those that a mesh axis runs over, the one named last changes fastest.
Arguments:
- hidden: bfloat16 [16384, 1536], P('seq', 'feat'), may hold values from -24 to 24
- lengths: int32 [8], replicated, may hold values from 1 to 8192, 16384 in all
- page_table: int32 [64], replicated, may hold values from 0 to 63, each once
- first_gain: float32 [1536], replicated, may hold values from 0.5 to 1.5
- query_weight: bfloat16 [1536, 1536], P(None, 'feat'), may hold values from -0.15625 to 0.15625
- keyvalue_weight: bfloat16 [1536, 256], P(None, 'feat'), may hold values from -0.15625 to 0.15625
- output_weight: bfloat16 [1536, 1536], P('feat'), may hold values from -0.15625 to 0.15625
- second_gain: float32 [1536], replicated, may hold values from 0.5 to 1.5
- gate_weight: bfloat16 [1536, 4608], P(None, 'feat'), may hold values from -0.15625 to 0.15625
- up_weight: bfloat16 [1536, 4608], P(None, 'feat'), may hold values from -0.15625 to 0.15625
- down_weight: bfloat16 [4608, 1536], P('feat'), may hold values from -0.09375 to 0.09375
Outputs:
- output: bfloat16 [16384, 1536], P('seq', 'feat')
- cache: bfloat16 [64, 128, 256], P('seq', 'feat')
Inputs may be any that keep to these rules, and one draw needn't show every extreme that they name: `lengths`: the 8 prompts fill the pack in order and sum to 16384 tokens; the longest has exactly 8192. A permutation of the 64 pages; cache block b of prompt r is page_table[r * 8 + b], and page p is held by seq index p // 2.
All inputs are finite; a program needn't handle non-finite values.
Results may differ from a plain program's by a relative error of at most 0.007.
Values may be sent and summed in bfloat16 or wider, within the bound.
No kernel may reach another device: no remote copies, remote signals or barrier semaphores. Data moves between devices by JAX's collectives and lax.ppermute only.
A program may use at most 128 MiB of HBM per device.

v0:
```python
import math

import jax
import jax.numpy as jnp
from jax import lax
from jax.sharding import PartitionSpec as P

HD = 128
WIN = 1024
BLK = 128


epsilon = 1e-06


def passed_along(block, axis, distance):
    devices = range(lax.axis_size(axis))
    route = [(i - distance, i) for i in devices if i - distance in devices]
    return lax.ppermute(block, axis, route)


def locate(places, lengths):
    offsets = jnp.cumsum(lengths) - lengths
    numbers = jnp.arange(lengths.shape[0], dtype=jnp.int32)
    segment = jnp.sum((places[:, None] >= offsets[None, :]).astype(jnp.int32), axis=1) - 1
    member = (segment[:, None] == numbers[None, :]).astype(jnp.int32)
    begin = jnp.sum(member * offsets[None, :], axis=1)
    length = jnp.sum(member * lengths[None, :], axis=1)
    return (segment, places - begin, length, begin)


def rotate(values, inner):
    half = values.shape[-1] // 2
    freq = jnp.exp(
        jnp.arange(half, dtype=jnp.float32) * (-2.0 * math.log(10000.0) / values.shape[-1])
    )
    angle = inner.astype(jnp.float32)[:, None] * freq[None, :]
    cosine = jnp.cos(angle)[:, None, :]
    sine = jnp.sin(angle)[:, None, :]
    first = values[..., :half]
    second = values[..., half:]
    return jnp.concatenate(
        [first * cosine - second * sine, second * cosine + first * sine], axis=-1
    )


def normalize(values, gain):
    square = jnp.sum(values * values, axis=-1, keepdims=True) / values.shape[-1]
    return (values * lax.rsqrt(square + epsilon) * gain).astype(jnp.bfloat16)


def window_attention(block_query, block_kv, query_seg, key_seg):
    query_count = block_query.shape[0]
    key_count = block_kv.shape[0]
    head_size = block_kv.shape[1] // 2
    window = key_count - query_count
    offset = (
        jnp.arange(key_count, dtype=jnp.int32)[None, :]
        - jnp.arange(query_count, dtype=jnp.int32)[:, None]
    )
    allowed = (offset > 0) & (offset <= window) & (query_seg[:, None] == key_seg[None, :])
    scores = jnp.einsum(
        "qhd,kd->hqk", block_query, block_kv[:, :head_size], preferred_element_type=jnp.float32
    )
    scores = scores * head_size ** (-0.5)
    weights = jnp.where(allowed[None], jnp.exp(scores), 0.0)
    probs = (weights / jnp.sum(weights, axis=-1, keepdims=True)).astype(jnp.bfloat16)
    mixed = jnp.einsum(
        "hqk,kd->qhd", probs, block_kv[:, head_size:], preferred_element_type=jnp.float32
    )
    return mixed.astype(jnp.bfloat16).reshape(query_count, -1)


def place(rows, places, extra, lengths, page_table, feat_index, part_rows):
    segment, inner, length, begin = locate(places, lengths)
    keep = (segment >= 0) & (inner >= length - WIN) & extra
    slot = jnp.where(keep, inner % WIN, 0)
    entry = jnp.where(keep, segment * (WIN // BLK) + slot // BLK, 0)
    pages = page_table.shape[0]
    page = jnp.sum(
        jnp.where(
            entry[:, None] == jnp.arange(pages, dtype=jnp.int32)[None, :], page_table[None, :], 0
        ),
        axis=1,
    )
    within = slot % BLK
    mine = keep & (within // part_rows == feat_index)
    target = jnp.where(mine, page * part_rows + within % part_rows, -1)
    onehot = (jnp.arange(pages * part_rows, dtype=jnp.int32)[:, None] == target[None, :]).astype(
        jnp.bfloat16
    )
    image = jnp.dot(onehot, rows, preferred_element_type=jnp.float32)
    return image.reshape(pages, part_rows, rows.shape[1])


def shards(
    hidden,
    lengths,
    page_table,
    first_gain,
    query_weight,
    keyvalue_weight,
    output_weight,
    second_gain,
    gate_weight,
    up_weight,
    down_weight,
):
    tokens_here = hidden.shape[0]
    width_here = hidden.shape[1]
    feat_count = lax.axis_size("feat")
    seq_index = lax.axis_index("seq")
    feat_index = lax.axis_index("feat")
    full_width = width_here * feat_count
    local_heads = query_weight.shape[1] // HD
    gathered = lax.all_gather(hidden, "feat", axis=1, tiled=True)
    normed = normalize(gathered.astype(jnp.float32), first_gain)
    start = seq_index * tokens_here
    places = start + jnp.arange(tokens_here, dtype=jnp.int32)
    segment, inner, length, begin = locate(places, lengths)
    queries = jnp.dot(normed, query_weight, preferred_element_type=jnp.float32).reshape(
        tokens_here, local_heads, HD
    )
    queries = rotate(queries, inner).astype(jnp.bfloat16)
    keyvalue_part = jnp.dot(normed, keyvalue_weight, preferred_element_type=jnp.float32).astype(
        jnp.bfloat16
    )
    keyvalue = lax.all_gather(keyvalue_part, "feat", axis=1, tiled=True)
    keys = rotate(keyvalue[:, None, :HD].astype(jnp.float32), inner)[:, 0, :].astype(jnp.bfloat16)
    rotated = jnp.concatenate([keys, keyvalue[:, HD:]], axis=1)
    earlier = max(1, WIN // tokens_here)
    pieces = []
    for distance in range(earlier, 0, -1):
        pieces.append(passed_along(rotated, "seq", distance))
    window_rows = jnp.concatenate(pieces + [rotated], axis=0)
    window_places = (
        start - earlier * tokens_here + jnp.arange((earlier + 1) * tokens_here, dtype=jnp.int32)
    )
    window_seg, window_inner, window_length, window_begin = locate(window_places, lengths)
    block_rows = min(tokens_here, 512)

    def attend(index):
        return window_attention(queries, window_rows, segment, window_seg)

    attended = lax.map(attend, jnp.arange(tokens_here // block_rows, dtype=jnp.int32))
    attended = attended.reshape(tokens_here, local_heads * HD)
    partial_sums = jnp.dot(attended, output_weight, preferred_element_type=jnp.float32)
    head_share = lax.psum_scatter(partial_sums, "feat", scatter_dimension=1, tiled=True)
    residual = hidden.astype(jnp.float32) + head_share
    squares = lax.psum(jnp.sum(residual * residual, axis=1), "feat")
    gain_here = lax.dynamic_slice_in_dim(second_gain, feat_index * width_here, width_here, 0)
    normed_part = (
        residual * lax.rsqrt(squares[:, None] / full_width + epsilon) * gain_here
    ).astype(jnp.bfloat16)
    normed2 = lax.all_gather(normed_part, "feat", axis=1, tiled=True)
    gate = jnp.dot(normed2, gate_weight, preferred_element_type=jnp.float32)
    upper = jnp.dot(normed2, up_weight, preferred_element_type=jnp.float32)
    activated = (jax.nn.gelu(gate, approximate=True) * upper).astype(jnp.bfloat16)
    down_terms = jnp.dot(activated, down_weight, preferred_element_type=jnp.float32)
    feed_share = lax.psum_scatter(down_terms, "feat", scatter_dimension=1, tiled=True)
    output = (residual + feed_share).astype(jnp.bfloat16)
    part_rows = BLK // feat_count
    image = place(
        rotated, places, jnp.ones((tokens_here,), bool), lengths, page_table, feat_index, part_rows
    )
    cache = lax.psum_scatter(image.astype(jnp.bfloat16), "seq", scatter_dimension=0, tiled=True)
    return (output, cache)


def solution(mesh):
    placed = (
        P("seq", "feat"),
        P(),
        P(),
        P(),
        P(None, "feat"),
        P(None, "feat"),
        P("feat", None),
        P(),
        P(None, "feat"),
        P(None, "feat"),
        P("feat", None),
    )
    return jax.shard_map(
        shards,
        mesh=mesh,
        in_specs=placed,
        out_specs=(P("seq", "feat"), P("seq", "feat", None)),
        check_vma=False,
    )
```

profile of v0, /device:TPU:6, one launch (start us, length us, event | category | flops | bytes accessed | tf_op | source)
XLA Modules:
  0.0 298.4 jit_solution(2308352064949406638)
XLA Ops:
  12.6 1.8 multiply_cosine_fusion
  14.4 2.1 fusion.9
  16.4 22.2 %all-gather.3.cloned.1.call-done = bf16[512,1536]{1,0:T(8,128)(2,1)} async-done(((bf16[512,384]{1,0:T(8,128)(2,1)}), bf16[512,1536]{1,0:T(8,128)(2,1)}) %all-gather.3.cloned.1.call-update) | async-done | bytes 1572880 | tf_op jit(solution)/shard_map/all_gather | solution.py:116
  40.4 2.2 convolution_convert_fusion
  42.7 12.5 %all_gather.10 = bf16[512,256]{0,1:T(8,128)(2,1)S(1)} all-gather(bf16[512,64]{0,1:T(8,128)(2,1)S(1)} %convolution_convert_fusion), channel_id=1, replica_groups=mesh['seq'=32,'feat'=4] {'feat'}, dimensions={1}, use_global_device_ids=true | all-gather | bytes 327680 | tf_op jit(solution)/shard_map/all_gather | solution.py:128
  56.6 1.9 collective-permute-start.1
  58.5 3.5 %collective-permute-start = (bf16[512,256]{0,1:T(8,128)(2,1)}, bf16[512,256]{0,1:T(8,128)(2,1)}, u32[]{:S(2)}, u32[]{:S(2)}) collective-permute-start(bf16[512,256]{0,1:T(8,128)(2,1)} %pad_maximum_fusion), channel_id=1, source_target_pairs={{0,8},{4,12},{8,16},{12,20},{16,24},{20,28},{24,32},{28,36},{32,40... | collective-permute-start | bytes 786440 | tf_op jit(solution)/shard_map/ppermute | solution.py:19
  63.9 2.1 copy.25
  66.0 2.2 copy.24
  68.2 1.8 subtract_convert_fusion
  70.0 1.9 collective-permute-done
  73.1 2.8 fusion
  75.8 2.9 fusion.20
  78.8 2.7 fusion.58
  82.3 35.8 %reduce-scatter.4.cloned.1.call-done = f32[512,384]{1,0:T(8,128)} async-done(((f32[512,1536]{1,0:T(8,128)}), f32[512,384]{1,0:T(8,128)}) %reduce-scatter.4.cloned.1.call-update) | async-done | bytes 786448 | tf_op jit(solution)/shard_map/reduce_scatter | solution.py:148
  119.5 8.6 %psum.7 = f32[512]{0:T(512)S(1)} all-reduce(f32[512]{0:T(512)S(1)} %multiply_reduce_fusion), channel_id=1, replica_groups=mesh['seq'=32,'feat'=4] {'feat'}, use_global_device_ids=true, to_apply=%region_8.9 | all-reduce | flops 512 | bytes 4096 | tf_op jit(solution)/shard_map/psum | solution.py:150
  128.1 2.1 multiply_convert_fusion
  130.5 25.9 %all-gather.5.cloned.1.call-done = bf16[512,1536]{1,0:T(8,128)(2,1)} async-done(((bf16[512,384]{1,0:T(8,128)(2,1)}), bf16[512,1536]{1,0:T(8,128)(2,1)}) %all-gather.5.cloned.1.call-update) | async-done | bytes 1572880 | tf_op jit(solution)/shard_map/all_gather | solution.py:155
  156.4 6.1 %fusion.59 = f32[512,1152]{1,0:T(8,128)} fusion(bf16[512,1536]{1,0:T(8,128)(2,1)} %all-gather.5.cloned.1.call-done, bf16[1536,1152]{1,0:T(8,128)(2,1)} %param.19), kind=kOutput, calls=%fused_computation.114 | convolution fusion | flops 1811939328 | bytes 7471104 | tf_op jit(solution)/shard_map/dot_general | solution.py:156
  162.5 9.9 %fusion.21 = f32[512,1536]{1,0:T(8,128)} fusion(bf16[1152,1536]{1,0:T(8,128)(2,1)S(1)} %copy-done, bf16[512,1536]{1,0:T(8,128)(2,1)} %all-gather.5.cloned.1.call-done, bf16[1536,1152]{1,0:T(8,128)(2,1)} %param.20, f32[512,1152]{1,0:T(8,128)} %fusion.59), kind=kOutput, calls=%fused_computation.37 | convolution fusion | flops 3629776896 | bytes 14155776 | tf_op jit(solution)/shard_map/dot_general | solution.py:159
  173.1 2.8 fusion.11
  175.9 35.0 %reduce-scatter.6.cloned.1.call-done = f32[512,384]{1,0:T(8,128)} async-done(((f32[512,1536]{1,0:T(8,128)}), f32[512,384]{1,0:T(8,128)}) %reduce-scatter.6.cloned.1.call-update) | async-done | bytes 786448 | tf_op jit(solution)/shard_map/reduce_scatter | solution.py:160
  210.9 2.3 add_convert_fusion
  213.2 78.7 %reduce-scatter.8.cloned.1.call-done = bf16[2,32,256]{2,1,0:T(8,128)(2,1)} async-done(((bf16[64,32,256]{2,1,0:T(8,128)(2,1)}), bf16[2,32,256]{2,1,0:T(8,128)(2,1)}) %reduce-scatter.8.cloned.1.call-update) | async-done | bytes 32784 | tf_op jit(solution)/shard_map/reduce_scatter | solution.py:166
  (58 shorter events, 14.7 us)
Async XLA Ops:
  7.2 155.3 %copy-start = (bf16[1152,1536]{1,0:T(8,128)(2,1)S(1)}, bf16[1152,1536]{1,0:T(8,128)(2,1)}, u32[]{:S(2)}) copy-start(bf16[1152,1536]{1,0:T(8,128)(2,1)} %param.21) | copy-start | bytes 10616836
  7.2 31.4 %all-gather.3.cloned.1.call-start = ((), (), s32[]{:S(2)}) async-start(), calls=%async_computation.3 | async-start | bytes 1966080 | tf_op jit(solution)/shard_map/all_gather | solution.py:116
  7.9 110.2 %reduce-scatter.4.cloned.1.call-start = ((), (), s32[]{:S(2)}) async-start(), calls=%async_computation.4 | async-start | bytes 3932160 | tf_op jit(solution)/shard_map/reduce_scatter | solution.py:148
  40.4 21.6 %copy-start.1 = (bf16[512,1536]{1,0:T(8,128)(2,1)S(1)}, bf16[512,1536]{1,0:T(8,128)(2,1)}, u32[]{:S(2)}) copy-start(bf16[512,1536]{1,0:T(8,128)(2,1)} %all-gather.3.cloned.1.call-done) | copy-start | bytes 4718596
  40.4 21.6 %copy-start.9 = (bf16[1536,384]{1,0:T(8,128)(2,1)S(1)}, bf16[1536,384]{1,0:T(8,128)(2,1)}, u32[]{:S(2)}) copy-start(bf16[1536,384]{1,0:T(8,128)(2,1)} %param.15) | copy-start | bytes 3538948
  40.4 21.6 %copy-start.10 = (f32[1536]{0:T(1024)S(1)}, f32[1536]{0:T(1024)}, u32[]{:S(2)}) copy-start(f32[1536]{0:T(1024)} %param.14) | copy-start | bytes 18436
  55.2 0.6 copy-start.3
  55.8 0.8 copy-start.5
  56.6 13.4 %collective-permute-start.1 = (bf16[512,256]{0,1:T(8,128)(2,1)}, bf16[512,256]{0,1:T(8,128)(2,1)}, u32[]{:S(2)}, u32[]{:S(2)}) collective-permute-start(bf16[512,256]{0,1:T(8,128)(2,1)} %pad_maximum_fusion), channel_id=1, source_target_pairs={{0,4},{4,8},{8,12},{12,16},{16,20},{20,24},{24,28},{28,32},{32,36}... | collective-permute-start | bytes 786440 | tf_op jit(solution)/shard_map/ppermute | solution.py:19
  58.5 13.5 %collective-permute-start = (bf16[512,256]{0,1:T(8,128)(2,1)}, bf16[512,256]{0,1:T(8,128)(2,1)}, u32[]{:S(2)}, u32[]{:S(2)}) collective-permute-start(bf16[512,256]{0,1:T(8,128)(2,1)} %pad_maximum_fusion), channel_id=1, source_target_pairs={{0,8},{4,12},{8,16},{12,20},{16,24},{20,28},{24,32},{28,36},{32,40... | collective-permute-start | bytes 786440 | tf_op jit(solution)/shard_map/ppermute | solution.py:19
  68.2 3.8 %copy-start.4 = (bf16[512,128]{0,1:T(8,128)(2,1)S(1)}, bf16[512,128]{0,1:T(8,128)(2,1)}, u32[]{:S(2)}) copy-start(bf16[512,128]{0,1:T(8,128)(2,1)} %copy-done.3) | copy-start | bytes 393220
  68.2 3.8 %copy-start.6 = (bf16[512,128]{0,1:T(8,128)(2,1)S(1)}, bf16[512,128]{0,1:T(8,128)(2,1)}, u32[]{:S(2)}) copy-start(bf16[512,128]{0,1:T(8,128)(2,1)} %copy-done.5) | copy-start | bytes 393220
  68.2 4.8 %copy-start.7 = (pred[512,1536]{0,1:T(8,128)(4,1)S(1)}, pred[512,1536]{0,1:T(8,128)(4,1)}, u32[]{:S(2)}) copy-start(pred[512,1536]{0,1:T(8,128)(4,1)} %fusion.9) | copy-start | bytes 2359300
  75.8 2.9 copy-start.2
  81.4 74.9 %all-gather.5.cloned.1.call-start = ((), (), s32[]{:S(2)}) async-start(), calls=%async_computation.5 | async-start | bytes 1966080 | tf_op jit(solution)/shard_map/all_gather | solution.py:155
  130.2 80.6 %reduce-scatter.6.cloned.1.call-start = ((), (), s32[]{:S(2)}) async-start(), calls=%async_computation.6 | async-start | bytes 3932160 | tf_op jit(solution)/shard_map/reduce_scatter | solution.py:160
  172.4 0.7 copy-start.8
  172.4 119.5 %reduce-scatter.8.cloned.1.call-start = ((), (), s32[]{:S(2)}) async-start(), calls=%async_computation.7 | async-start | bytes 1081344 | tf_op jit(solution)/shard_map/reduce_scatter | solution.py:166
Sparse Core Ops, SparseCore 0:
  9.7 28.8 all-gather.2
  81.6 36.4 reduce-scatter.3
  130.4 25.9 all-gather.4
  172.6 38.2 reduce-scatter.5
  214.8 77.0 reduce-scatter.7
where the time goes:
time: 299 us; the launch traced here: 298 us
  waiting for transfers between devices  200 us (67%)
  matrix products  30.3 us (10%)
  blocking collectives  21.1 us (7%)
  other arithmetic  20.3 us (7%)
  between operations  14 us (5%)
  local copies, waits for them, and re-layouts  6.7 us (2%)
  starting transfers between devices  5.75 us (2%)
    reduce_scatter x1, waiting for transfers between devices, shards(): lax.psum_scatter(image.astype(jnp.bfloat16), 'seq', scatter_dimension=0,...  78.7 us
    reduce_scatter x1, waiting for transfers between devices, shards(): lax.psum_scatter(partial_sums, 'feat', scatter_dimension=1, tiled=True)  35.8 us
    reduce_scatter x1, waiting for transfers between devices, shards(): lax.psum_scatter(down_terms, 'feat', scatter_dimension=1, tiled=True)  35 us
    all_gather x1, waiting for transfers between devices, shards(): normed2 = lax.all_gather(normed_part, 'feat', axis=1, tiled=True)  25.9 us
    all_gather x1, waiting for transfers between devices, shards(): gathered = lax.all_gather(hidden, 'feat', axis=1, tiled=True)  22.2 us
    all_gather x1, blocking collectives, shards(): keyvalue = lax.all_gather(keyvalue_part, 'feat', axis=1, tiled=True)  12.5 us
    dot_general x1, matrix products, shards(): jnp.dot(activated, down_weight, preferred_element_type=jnp.float32)  9.91 us
    psum x1, blocking collectives, shards(): squares = lax.psum(jnp.sum(residual * residual, axis=1), 'feat')  8.59 us
  transfers between devices with their start and end apart: 7, of which 6 were waited for; matrix products, arithmetic and copies ran while one was open for 7% of the time, Pallas kernels for 0%

commit v1 on v0

v1 whole, which is shorter than its diff:
```python
import functools
import math

import jax
import jax.numpy as jnp
from jax import lax
from jax.experimental import pallas as pl
from jax.experimental.pallas import tpu as pltpu
from jax.sharding import PartitionSpec as P

HD = 128
WIN = 1024
BLK = 128
epsilon = 1e-06
bf16 = jnp.bfloat16
f32 = jnp.float32
VM = pl.BlockSpec(memory_space=pltpu.VMEM)
SM = pl.BlockSpec(memory_space=pltpu.SMEM)


def from_peer(block, distance):
    n = lax.axis_size("feat")
    return lax.ppermute(block, "feat", [(i, (i - distance) % n) for i in range(n)])


def from_earlier(block, distance):
    n = lax.axis_size("seq")
    return lax.ppermute(block, "seq", [(i - distance, i) for i in range(distance, n)])


def run(body, outs, name, scalars, arrays, scratch=(), vmem=60 << 20):
    many = isinstance(outs, (list, tuple))
    return pl.pallas_call(
        body,
        out_shape=outs,
        in_specs=[SM] * len(scalars) + [VM] * len(arrays),
        out_specs=[VM] * len(outs) if many else VM,
        scratch_shapes=list(scratch),
        compiler_params=pltpu.CompilerParams(vmem_limit_bytes=vmem),
        name=name,
    )(*scalars, *arrays)


def dot(a, b):
    return jnp.dot(a, b, preferred_element_type=f32)


def norm_kv_body(place, x0, x1, x2, x3, gain, wkv, n_out, kv_out):
    f = place[0]
    xs = (x0, x1, x2, x3)
    tokens, width = x0.shape
    step = 128
    for r in range(tokens // step):
        rows = pl.ds(r * step, step)
        total = None
        for x in xs:
            v = x[rows, :].astype(f32)
            part = jnp.sum(v * v, axis=1, keepdims=True)
            total = part if total is None else total + part
        scale = lax.rsqrt(total / (width * 4) + epsilon)
        for d, x in enumerate(xs):
            g = lax.rem(f + d, 4)
            v = x[rows, :].astype(f32) * scale * gain[pl.ds(g, 1), :]
            n_out[d, rows, :] = v.astype(bf16)
    acc = None
    for d in range(4):
        g = lax.rem(f + d, 4)
        start = pl.multiple_of(g * width, 128)
        part = dot(n_out[d], wkv[pl.ds(start, width), :])
        acc = part if acc is None else acc + part
    kv = acc.astype(bf16)
    half = tokens // 2
    kv_out[...] = jnp.concatenate([kv[:half], kv[half:]], axis=1)


def query_body(place, n_in, wq, cosine, sine, q_out):
    f = place[0]
    width = n_in.shape[2]
    acc = None
    for d in range(4):
        g = lax.rem(f + d, 4)
        start = pl.multiple_of(g * width, 128)
        part = dot(n_in[d], wq[pl.ds(start, width), :])
        acc = part if acc is None else acc + part
    c = cosine[...]
    s = sine[...]
    for h in range(acc.shape[1] // HD):
        v = acc[:, h * HD : (h + 1) * HD]
        q_out[:, h * HD : (h + 1) * HD] = (v * c + pltpu.roll(v, HD // 2, 1) * s).astype(bf16)


def rotate_body(place, y0, y1, y2, y3, cosine, sine, out, hold):
    f = place[0]
    half = y0.shape[0]
    for d, y in enumerate((y0, y1, y2, y3)):
        hold[lax.rem(f + d, 4)] = y[...].astype(f32)
    for part in range(2):
        rows = pl.ds(part * half, half)
        lanes = slice(part * 64, part * 64 + 64)
        k = jnp.concatenate([hold[0][:, lanes], hold[1][:, lanes]], axis=1)
        v = jnp.concatenate([hold[2][:, lanes], hold[3][:, lanes]], axis=1)
        k = k * cosine[rows, :] + pltpu.roll(k, HD // 2, 1) * sine[rows, :]
        out[rows, :HD] = k.astype(bf16)
        out[rows, HD:] = v.astype(bf16)


def attend_body(d, place, offsets, q, far, near, own, wo, out, win, att):
    f = place[0]
    first = place[1]
    tokens = own.shape[0]
    win[pl.ds(0, tokens), :] = far[...]
    win[pl.ds(tokens, tokens), :] = near[...]
    win[pl.ds(2 * tokens, tokens), :] = own[...]
    step = 128
    b = lax.rem(f + d, 4)
    row0 = pl.multiple_of(b * step, step)
    keys = WIN + step
    k = win[pl.ds(row0, keys), :HD]
    v = win[pl.ds(row0, keys), HD:]
    pos = first + row0 + lax.broadcasted_iota(jnp.int32, (step, 1), 0)
    begin = jnp.zeros((step, 1), jnp.int32)
    for r in range(offsets.shape[0]):
        begin = jnp.where(pos >= offsets[r], offsets[r], begin)
    low = jnp.maximum(pos - (WIN - 1), begin)
    kpos = first + row0 - WIN + lax.broadcasted_iota(jnp.int32, (step, keys), 1)
    allowed = (kpos >= low) & (kpos <= pos)
    factor = HD**-0.5 * math.log2(math.e)
    for h in range(q.shape[1] // HD):
        qh = q[pl.ds(row0, step), h * HD : (h + 1) * HD]
        s = lax.dot_general(qh, k, (((1,), (1,)), ((), ())), preferred_element_type=f32)
        p = jnp.where(allowed, jnp.exp2(s * factor), 0.0)
        total = jnp.sum(p, axis=1, keepdims=True)
        mixed = dot(p.astype(bf16), v)
        att[:, h * HD : (h + 1) * HD] = (mixed / total).astype(bf16)
    out[...] = dot(att[...], wo[...]).astype(out.dtype)


def residual_body(place, x0, x1, x2, x3, p0, p1, p2, p3, gain, res_out, n_out):
    f = place[0]
    step, width = p0.shape[0], x0.shape[1]
    rows = pl.ds(pl.multiple_of(f * step, step), step)
    for d, x in enumerate((x0, x1, x2, x3)):
        res_out[lax.rem(f + d, 4)] = x[rows, :].astype(f32)
    total = None
    for g in range(4):
        cols = slice(g * width, (g + 1) * width)
        v = res_out[g] + p0[:, cols]
        v = v + p1[:, cols].astype(f32)
        v = v + p2[:, cols].astype(f32)
        v = v + p3[:, cols].astype(f32)
        res_out[g] = v
        part = jnp.sum(v * v, axis=1, keepdims=True)
        total = part if total is None else total + part
    scale = lax.rsqrt(total / (width * 4) + epsilon)
    for g in range(4):
        cols = slice(g * width, (g + 1) * width)
        n_out[:, cols] = (res_out[g] * scale * gain[:, cols]).astype(bf16)


def gelu(x):
    inner = math.sqrt(2 / math.pi) * (x + 0.044715 * (x * x * x))
    return x * (0.5 * (1.0 + jnp.tanh(inner)))


def gate_body(*refs):
    ins, (wg, wu, out) = refs[:-3], refs[-3:]
    n = jnp.concatenate([r[...] for r in ins], axis=0) if len(ins) > 1 else ins[0][...]
    chunk = 384
    for c in range(wg.shape[1] // chunk):
        cols = slice(c * chunk, (c + 1) * chunk)
        out[:, cols] = (gelu(dot(n, wg[:, cols])) * dot(n, wu[:, cols])).astype(bf16)


def down_body(d, place, a0, a13, a2, res, wd, out):
    f = place[0]
    width = out.shape[1]
    step = res.shape[1]
    g = lax.rem(f + d, 4)
    w = wd[:, pl.ds(pl.multiple_of(g * width, 128), width)]

    def rows(e):
        return pl.ds(pl.multiple_of(lax.rem(f + e, 4) * step, step), step)

    out[rows(0), :] = (dot(a0[...], w) + res[g]).astype(out.dtype)
    both = dot(a13[...], w)
    out[rows(1), :] = both[:step].astype(out.dtype)
    out[rows(3), :] = both[step:].astype(out.dtype)
    out[rows(2), :] = dot(a2[...], w).astype(out.dtype)


def image_body(target, rows, out):
    count = out.shape[0]
    step = 512
    for r in range(count // step):
        index = r * step + lax.broadcasted_iota(jnp.int32, (step, target.shape[1]), 0)
        hot = jnp.where(index == target[...], 1.0, 0.0).astype(bf16)
        out[pl.ds(r * step, step), :] = dot(hot, rows[...]).astype(bf16)


def shards(
    hidden,
    lengths,
    page_table,
    first_gain,
    query_weight,
    keyvalue_weight,
    output_weight,
    second_gain,
    gate_weight,
    up_weight,
    down_weight,
):
    tokens, width = hidden.shape
    full = width * 4
    seq_index = lax.axis_index("seq")
    f = lax.axis_index("feat")
    first = seq_index * tokens
    place = jnp.stack([f, first]).astype(jnp.int32)
    sds = jax.ShapeDtypeStruct

    x0 = hidden
    x2 = from_peer(hidden, 2)
    x1 = from_peer(hidden, 1)
    x3 = from_peer(hidden, 3)

    offsets = jnp.cumsum(lengths) - lengths
    places = first + jnp.arange(tokens, dtype=jnp.int32)
    numbers = jnp.arange(lengths.shape[0], dtype=jnp.int32)
    segment = jnp.sum((places[:, None] >= offsets[None, :]).astype(jnp.int32), axis=1) - 1
    member = (segment[:, None] == numbers[None, :]).astype(jnp.int32)
    inner = places - jnp.sum(member * offsets[None, :], axis=1)
    length = jnp.sum(member * lengths[None, :], axis=1)
    half = HD // 2
    freq = jnp.exp(jnp.arange(half, dtype=f32) * (-2.0 * math.log(10000.0) / HD))
    angle = inner.astype(f32)[:, None] * freq[None, :]
    cosine = jnp.cos(angle)
    sine = jnp.sin(angle)
    cosine = jnp.concatenate([cosine, cosine], axis=1)
    sine = jnp.concatenate([-sine, sine], axis=1)

    pages = page_table.shape[0]
    part_rows = BLK // 4
    keep = inner >= length - WIN
    slot = inner % WIN
    entry = segment * (WIN // BLK) + slot // BLK
    page = jnp.sum(
        jnp.where(
            entry[:, None] == jnp.arange(pages, dtype=jnp.int32)[None, :], page_table[None, :], 0
        ),
        axis=1,
    )
    within = slot % BLK
    mine = keep & (within // part_rows == f)
    target = jnp.where(mine, page * part_rows + within % part_rows, -1)[None, :]

    normed, kv_part = run(
        norm_kv_body,
        (sds((4, tokens, width), bf16), sds((tokens // 2, 128), bf16)),
        "norm_kv",
        [place],
        [x0, x1, x2, x3, first_gain.reshape(4, width), keyvalue_weight],
    )
    y2 = from_peer(kv_part, 2)
    y1 = from_peer(kv_part, 1)
    y3 = from_peer(kv_part, 3)
    queries = run(
        query_body,
        sds((tokens, query_weight.shape[1]), bf16),
        "queries",
        [place],
        [normed, query_weight, cosine, sine],
    )
    rotated = run(
        rotate_body,
        sds((tokens, 2 * HD), bf16),
        "rotate",
        [place],
        [kv_part, y1, y2, y3, cosine, sine],
        [pltpu.VMEM((4, tokens // 2, 128), f32)],
    )
    far = from_earlier(rotated, 2)
    near = from_earlier(rotated, 1)

    step = tokens // 4

    def attend(d, kind):
        return run(
            functools.partial(attend_body, d),
            sds((step, full), kind),
            f"attend{d}",
            [place, offsets],
            [queries, far, near, rotated, output_weight],
            [
                pltpu.VMEM((3 * tokens, 2 * HD), bf16),
                pltpu.VMEM((step, query_weight.shape[1]), bf16),
            ],
        )

    p2 = from_peer(attend(2, bf16), 2)
    p1 = from_peer(attend(1, bf16), 3)
    p3 = from_peer(attend(3, bf16), 1)
    p0 = attend(0, f32)

    image = run(image_body, sds((pages * part_rows, 2 * HD), bf16), "image", [], [target, rotated])
    image = image.reshape(32, pages // 32 * part_rows, 2 * HD)
    landed = lax.all_to_all(image, "seq", 0, 0, tiled=False)
    cache = jnp.sum(landed.astype(f32), axis=0).astype(bf16)
    cache = cache.reshape(pages // 32, part_rows, 2 * HD)

    residual, normed2 = run(
        residual_body,
        (sds((4, step, width), f32), sds((step, full), bf16)),
        "residual",
        [place],
        [x0, x1, x2, x3, p0, p1, p2, p3, second_gain.reshape(1, full)],
    )
    m1 = from_peer(normed2, 1)
    m3 = from_peer(normed2, 3)
    m2 = from_peer(normed2, 2)

    def gated(*blocks):
        return run(
            gate_body,
            sds((step * len(blocks), gate_weight.shape[1]), bf16),
            f"gate{len(blocks)}",
            [],
            [*blocks, gate_weight, up_weight],
        )

    a0 = gated(normed2)
    a13 = gated(m1, m3)
    a2 = gated(m2)

    def down(d, kind):
        return run(
            functools.partial(down_body, d),
            sds((tokens, width), kind),
            f"down{d}",
            [place],
            [a0, a13, a2, residual, down_weight],
        )

    o2 = from_peer(down(2, bf16), 2)
    o1 = from_peer(down(1, bf16), 3)
    o3 = from_peer(down(3, bf16), 1)
    o0 = down(0, f32)
    output = (o0 + o1.astype(f32) + o2.astype(f32) + o3.astype(f32)).astype(bf16)
    return (output, cache)


def solution(mesh):
    placed = (
        P("seq", "feat"),
        P(),
        P(),
        P(),
        P(None, "feat"),
        P(None, "feat"),
        P("feat", None),
        P(),
        P(None, "feat"),
        P(None, "feat"),
        P("feat", None),
    )
    return jax.shard_map(
        shards,
        mesh=mesh,
        in_specs=placed,
        out_specs=(P("seq", "feat"), P("seq", "feat", None)),
        check_vma=False,
    )
```

time: 299 us -> 155 us (0.52)
  waiting for transfers between devices: 200 us -> 32.8 us
  Pallas kernels: 0 us -> 65.1 us
  starting transfers between devices: 5.75 us -> 36.3 us
  matrix products: 30.3 us -> 0 us
  blocking collectives: 21.1 us -> 0 us
  between operations: 14 us -> 0.76 us
  other arithmetic: 20.3 us -> 9.16 us
  local copies, waits for them, and re-layouts: 6.7 us -> 10.5 us
    reduce_scatter x3 -> x0, waiting for transfers between devices: 149 us -> none  [the longest x1 78.7 us: shards(): lax.psum_scatter(image.astype(jnp.bfloat16), 'seq', scatter_dimension=0,...]
    pallas_call x0 -> x16, Pallas kernels: none -> 65.1 us  [run(): pl.pallas_call(body, out_shape=outs, in_specs=[SM] * len(scalars) + [VM]...]
    all_gather x2 -> x0, waiting for transfers between devices: 48.1 us -> none  [the longest x1 25.9 us: shards(): normed2 = lax.all_gather(normed_part, 'feat', axis=1, tiled=True)]
    ppermute x2 -> x17, waiting for transfers between devices: 1.94 us -> 32.8 us  [the longest x15 27.6 us: from_peer(): lax.ppermute(block, 'feat', [(i, (i - distance) % n) for i in range(n)])]
    dot_general x8 -> x0, matrix products: 30.3 us -> none  [the longest x1 9.91 us: shards(): jnp.dot(activated, down_weight, preferred_element_type=jnp.float32)]
    ppermute x2 -> x17, starting transfers between devices: 5.37 us -> 29.5 us  [the longest x15 23.8 us: from_peer(): lax.ppermute(block, 'feat', [(i, (i - distance) % n) for i in range(n)])]
    all_gather x1 -> x0, blocking collectives: 12.5 us -> none  [shards(): keyvalue = lax.all_gather(keyvalue_part, 'feat', axis=1, tiled=True)]
    psum x1 -> x0, blocking collectives: 8.59 us -> none  [shards(): squares = lax.psum(jnp.sum(residual * residual, axis=1), 'feat')]
  transfers between devices with their start and end apart: 7 -> 18, of which waited for: 6 -> 9; matrix products, arithmetic and copies ran while one was open for 7% -> 7% of each run, Pallas kernels for 0% -> 36%
where the time goes in v1:
time: 155 us
  Pallas kernels  65.1 us (42%)
  starting transfers between devices  36.3 us (23%)
  waiting for transfers between devices  32.8 us (21%)
  local copies, waits for them, and re-layouts  10.5 us (7%)
  other arithmetic  9.16 us (6%)
    pallas_call x16, Pallas kernels, run(): pl.pallas_call(body, out_shape=outs, in_specs=[SM] * len(scalars) + [VM]...  65.1 us
    ppermute x15, waiting for transfers between devices, from_peer(): lax.ppermute(block, 'feat', [(i, (i - distance) % n) for i in range(n)])  27.6 us
    ppermute x15, starting transfers between devices, from_peer(): lax.ppermute(block, 'feat', [(i, (i - distance) % n) for i in range(n)])  23.8 us
    unnamed x39, local copies, waits for them, and re-layouts  8.59 us
    all_to_all x1, starting transfers between devices, shards(): landed = lax.all_to_all(image, 'seq', 0, 0, tiled=False)  6.83 us
    ppermute x2, starting transfers between devices, from_earlier(): lax.ppermute(block, 'seq', [(i - distance, i) for i in range(distance, n)])  5.73 us
    ppermute x2, waiting for transfers between devices, from_earlier(): lax.ppermute(block, 'seq', [(i - distance, i) for i in range(distance, n)])  5.15 us
  transfers between devices with their start and end apart: 18, of which 9 were waited for; matrix products, arithmetic and copies ran while one was open for 7% of the time, Pallas kernels for 36%

profile of v1, /device:TPU:6, one launch (start us, length us, event | category | flops | bytes accessed | tf_op | source)
XLA Modules:
  0.0 154.7 jit_solution(12435622502956141573)
XLA Ops:
  2.3 2.9 %collective-permute-start.1 = (bf16[512,384]{1,0:T(8,128)(2,1)}, bf16[512,384]{1,0:T(8,128)(2,1)S(1)}, u32[]{:S(2)}, u32[]{:S(2)}) collective-permute-start(bf16[512,384]{1,0:T(8,128)(2,1)} %x0.3), channel_id=1, source_target_pairs={{0,2},{1,3},{2,0},{3,1},{4,6},{5,7},{6,4},{7,5},{8,10},{9,11},{10,... | collective-permute-start | bytes 1179656 | tf_op jit(solution)/shard_map/ppermute | solution.py:23
  14.5 8.1 %collective-permute-done.1.x2 = bf16[512,384]{1,0:T(8,128)(2,1)S(1)} collective-permute-done((bf16[512,384]{1,0:T(8,128)(2,1)}, bf16[512,384]{1,0:T(8,128)(2,1)S(1)}, u32[]{:S(2)}, u32[]{:S(2)}) %collective-permute-start.1) | collective-permute-done | bytes 393248 | tf_op jit(solution)/shard_map/ppermute | solution.py:23
  24.2 3.6 %norm_kv.1 = (bf16[4,512,384]{2,1,0:T(8,128)(2,1)}, bf16[256,128]{1,0:T(8,128)(2,1)}) custom-call(s32[2]{0:T(128)} %pad_add_fusion.place, bf16[512,384]{1,0:T(8,128)(2,1)} %x0.3, bf16[512,384]{1,0:T(8,128)(2,1)} %copy-done.4, bf16[512,384]{1,0:T(8,128)(2,1)} %copy-done.3, bf16[512,384]{1,0:T(8,128)(2,1)} %copy-done.2, f32[4,384]{1,0:T(4,128)} %reshape.276.gain, ...), custom_call_target="tpu_custom_call" | custom-call | tf_op jit(solution)/shard_map/norm_kv/pallas_call | solution.py:33
  39.8 3.8 %collective-permute-start.6 = (bf16[512,256]{1,0:T(8,128)(2,1)}, bf16[512,256]{1,0:T(8,128)(2,1)S(1)}, u32[]{:S(2)}, u32[]{:S(2)}) collective-permute-start(bf16[512,256]{1,0:T(8,128)(2,1)} %rotate.1.own.rows), channel_id=1, source_target_pairs={{0,8},{4,12},{8,16},{12,20},{16,24},{20,28},{24,32},{28,36},{32,40... | collective-permute-start | bytes 786440 | tf_op jit(solution)/shard_map/ppermute | solution.py:28
  43.8 3.9 %queries.1.q = bf16[512,384]{1,0:T(8,128)(2,1)} custom-call(s32[2]{0:T(128)} %pad_add_fusion.place, bf16[4,512,384]{2,1,0:T(8,128)(2,1)} %get-tuple-element.6.n_in, bf16[1536,384]{1,0:T(8,128)(2,1)} %wq.1, f32[512,128]{1,0:T(8,128)} %pad_maximum_fusion.cosine, f32[512,128]{1,0:T(8,128)} %pad_maximum_fusion.1.sine), custom_call_target="tpu_custom_call" | custom-call | tf_op jit(solution)/shard_map/queries/pallas_call | solution.py:33
  48.0 4.8 %collective-permute-done.6.far = bf16[512,256]{1,0:T(8,128)(2,1)S(1)} collective-permute-done((bf16[512,256]{1,0:T(8,128)(2,1)}, bf16[512,256]{1,0:T(8,128)(2,1)S(1)}, u32[]{:S(2)}, u32[]{:S(2)}) %collective-permute-start.6) | collective-permute-done | bytes 262176 | tf_op jit(solution)/shard_map/ppermute | solution.py:28
  53.5 3.7 %attend1.1 = bf16[128,1536]{1,0:T(8,128)(2,1)} custom-call(s32[2]{0:T(128)} %pad_add_fusion.place, s32[8]{0:T(128)} %copy-done.16, bf16[512,384]{1,0:T(8,128)(2,1)} %queries.1.q, bf16[512,256]{1,0:T(8,128)(2,1)} %copy-done.1, bf16[512,256]{1,0:T(8,128)(2,1)} %copy-done, bf16[512,256]{1,0:T(8,128)(2,1)} %rotate.1.own.rows, bf16[384,1536]{1,0:T(8,128)(2,1)} %wo.7), custom_call_target="tpu_custom_call" | custom-call | tf_op jit(solution)/shard_map/attend1/pallas_call | solution.py:33
  58.5 3.8 %attend2.1 = bf16[128,1536]{1,0:T(8,128)(2,1)} custom-call(s32[2]{0:T(128)} %pad_add_fusion.place, s32[8]{0:T(128)} %copy-done.16, bf16[512,384]{1,0:T(8,128)(2,1)} %queries.1.q, bf16[512,256]{1,0:T(8,128)(2,1)} %copy-done.1, bf16[512,256]{1,0:T(8,128)(2,1)} %copy-done, bf16[512,256]{1,0:T(8,128)(2,1)} %rotate.1.own.rows, bf16[384,1536]{1,0:T(8,128)(2,1)} %wo.7), custom_call_target="tpu_custom_call" | custom-call | tf_op jit(solution)/shard_map/attend2/pallas_call | solution.py:33
  62.2 3.0 %collective-permute-start.9 = (bf16[128,1536]{1,0:T(8,128)(2,1)}, bf16[128,1536]{1,0:T(8,128)(2,1)S(1)}, u32[]{:S(2)}, u32[]{:S(2)}) collective-permute-start(bf16[128,1536]{1,0:T(8,128)(2,1)} %attend2.1), channel_id=1, source_target_pairs={{0,2},{1,3},{2,0},{3,1},{4,6},{5,7},{6,4},{7,5},{8,10},{9,11},{10,... | collective-permute-start | bytes 1179656 | tf_op jit(solution)/shard_map/ppermute | solution.py:23
  65.3 3.8 %attend3.1 = bf16[128,1536]{1,0:T(8,128)(2,1)} custom-call(s32[2]{0:T(128)} %pad_add_fusion.place, s32[8]{0:T(128)} %copy-done.16, bf16[512,384]{1,0:T(8,128)(2,1)} %queries.1.q, bf16[512,256]{1,0:T(8,128)(2,1)} %copy-done.1, bf16[512,256]{1,0:T(8,128)(2,1)} %copy-done, bf16[512,256]{1,0:T(8,128)(2,1)} %rotate.1.own.rows, bf16[384,1536]{1,0:T(8,128)(2,1)} %wo.7), custom_call_target="tpu_custom_call" | custom-call | tf_op jit(solution)/shard_map/attend3/pallas_call | solution.py:33
  70.1 2.7 %image.1 = bf16[2048,256]{1,0:T(8,128)(2,1)} custom-call(s32[1,512]{1,0:T(1,128)} %and_select_fusion.1.target, bf16[512,256]{1,0:T(8,128)(2,1)} %rotate.1.own.rows), custom_call_target="tpu_custom_call" | custom-call | tf_op jit(solution)/shard_map/image/pallas_call | solution.py:33
  72.8 6.8 %all-to-all-start = ((bf16[32,64,256]{2,1,0:T(8,128)(2,1)}), bf16[32,64,256]{2,1,0:T(8,128)(2,1)S(1)}, u32[]{:S(2)}, u32[]{:S(2)}) async-start(bf16[32,64,256]{2,1,0:T(8,128)(2,1)} %bitcast.10), calls=%async_computation | async-start | bytes 2097152 | tf_op jit(solution)/shard_map/all_to_all | solution.py:306
  80.3 3.9 %attend0.1.p0 = f32[128,1536]{1,0:T(8,128)} custom-call(s32[2]{0:T(128)} %pad_add_fusion.place, s32[8]{0:T(128)} %copy-done.16, bf16[512,384]{1,0:T(8,128)(2,1)} %queries.1.q, bf16[512,256]{1,0:T(8,128)(2,1)} %copy-done.1, bf16[512,256]{1,0:T(8,128)(2,1)} %copy-done, bf16[512,256]{1,0:T(8,128)(2,1)} %rotate.1.own.rows, bf16[384,1536]{1,0:T(8,128)(2,1)} %wo.7), custom_call_target="tpu_custom_call" | custom-call | tf_op jit(solution)/shard_map/attend0/pallas_call | solution.py:33
  85.8 3.3 %residual.1 = (f32[4,128,384]{2,1,0:T(8,128)}, bf16[128,1536]{1,0:T(8,128)(2,1)}) custom-call(s32[2]{0:T(128)} %pad_add_fusion.place, bf16[512,384]{1,0:T(8,128)(2,1)} %x0.3, bf16[512,384]{1,0:T(8,128)(2,1)} %copy-done.4, bf16[512,384]{1,0:T(8,128)(2,1)} %copy-done.3, bf16[512,384]{1,0:T(8,128)(2,1)} %copy-done.2, f32[128,1536]{1,0:T(8,128)} %attend0.1.p0, ...), custom_call_target="tpu_custom_call" | custom-call | tf_op jit(solution)/shard_map/residual/pallas_call | solution.py:33
  90.6 3.1 %collective-permute-start.11 = (bf16[128,1536]{1,0:T(8,128)(2,1)}, bf16[128,1536]{1,0:T(8,128)(2,1)S(1)}, u32[]{:S(2)}, u32[]{:S(2)}) collective-permute-start(bf16[128,1536]{1,0:T(8,128)(2,1)} %get-tuple-element.8.refs_0_), channel_id=1, source_target_pairs={{0,3},{1,0},{2,1},{3,2},{4,7},{5,4},{6,5},{7,6},{8,11},{9,8},{10,9... | collective-permute-start | bytes 1179656 | tf_op jit(solution)/shard_map/ppermute | solution.py:23
  93.7 5.3 %gate1.2.a0 = bf16[128,1152]{1,0:T(8,128)(2,1)} custom-call(bf16[128,1536]{1,0:T(8,128)(2,1)} %get-tuple-element.8.refs_0_, bf16[1536,1152]{1,0:T(8,128)(2,1)} %refs_1_.3, bf16[1536,1152]{1,0:T(8,128)(2,1)} %refs_2_.5), custom_call_target="tpu_custom_call" | custom-call | tf_op jit(solution)/shard_map/gate1/pallas_call | solution.py:33
  99.0 3.8 %collective-permute-done.13.refs_0_ = bf16[128,1536]{1,0:T(8,128)(2,1)S(1)} collective-permute-done((bf16[128,1536]{1,0:T(8,128)(2,1)}, bf16[128,1536]{1,0:T(8,128)(2,1)S(1)}, u32[]{:S(2)}, u32[]{:S(2)}) %collective-permute-start.13) | collective-permute-done | bytes 393248 | tf_op jit(solution)/shard_map/ppermute | solution.py:23
  103.5 5.3 %gate1.3.a2 = bf16[128,1152]{1,0:T(8,128)(2,1)} custom-call(bf16[128,1536]{1,0:T(8,128)(2,1)} %copy-done.12, bf16[1536,1152]{1,0:T(8,128)(2,1)} %refs_1_.3, bf16[1536,1152]{1,0:T(8,128)(2,1)} %refs_2_.5), custom_call_target="tpu_custom_call" | custom-call | tf_op jit(solution)/shard_map/gate1/pallas_call | solution.py:33
  111.8 6.8 %gate2.1.a13 = bf16[256,1152]{1,0:T(8,128)(2,1)} custom-call(bf16[128,1536]{1,0:T(8,128)(2,1)} %copy-done.6, bf16[128,1536]{1,0:T(8,128)(2,1)} %copy-done.5, bf16[1536,1152]{1,0:T(8,128)(2,1)} %refs_1_.3, bf16[1536,1152]{1,0:T(8,128)(2,1)} %refs_2_.5), custom_call_target="tpu_custom_call" | custom-call | tf_op jit(solution)/shard_map/gate2/pallas_call | solution.py:33
  118.6 4.2 %down3.1 = bf16[512,384]{1,0:T(8,128)(2,1)} custom-call(s32[2]{0:T(128)} %pad_add_fusion.place, bf16[128,1152]{1,0:T(8,128)(2,1)} %gate1.2.a0, bf16[256,1152]{1,0:T(8,128)(2,1)} %gate2.1.a13, bf16[128,1152]{1,0:T(8,128)(2,1)} %gate1.3.a2, f32[4,128,384]{2,1,0:T(8,128)} %get-tuple-element.9.res, bf16[1152,1536]{1,0:T(8,128)(2,1)} %wd.7), custom_call_target="tpu_custom_call" | custom-call | tf_op jit(solution)/shard_map/down3/pallas_call | solution.py:33
  122.8 4.2 %down2.1 = bf16[512,384]{1,0:T(8,128)(2,1)} custom-call(s32[2]{0:T(128)} %pad_add_fusion.place, bf16[128,1152]{1,0:T(8,128)(2,1)} %gate1.2.a0, bf16[256,1152]{1,0:T(8,128)(2,1)} %gate2.1.a13, bf16[128,1152]{1,0:T(8,128)(2,1)} %gate1.3.a2, f32[4,128,384]{2,1,0:T(8,128)} %get-tuple-element.9.res, bf16[1152,1536]{1,0:T(8,128)(2,1)} %wd.7), custom_call_target="tpu_custom_call" | custom-call | tf_op jit(solution)/shard_map/down2/pallas_call | solution.py:33
  127.0 4.3 %down1.1 = bf16[512,384]{1,0:T(8,128)(2,1)} custom-call(s32[2]{0:T(128)} %pad_add_fusion.place, bf16[128,1152]{1,0:T(8,128)(2,1)} %gate1.2.a0, bf16[256,1152]{1,0:T(8,128)(2,1)} %gate2.1.a13, bf16[128,1152]{1,0:T(8,128)(2,1)} %gate1.3.a2, f32[4,128,384]{2,1,0:T(8,128)} %get-tuple-element.9.res, bf16[1152,1536]{1,0:T(8,128)(2,1)} %wd.7), custom_call_target="tpu_custom_call" | custom-call | tf_op jit(solution)/shard_map/down1/pallas_call | solution.py:33
  136.1 4.3 %down0.1 = f32[512,384]{1,0:T(8,128)} custom-call(s32[2]{0:T(128)} %pad_add_fusion.place, bf16[128,1152]{1,0:T(8,128)(2,1)} %gate1.2.a0, bf16[256,1152]{1,0:T(8,128)(2,1)} %gate2.1.a13, bf16[128,1152]{1,0:T(8,128)(2,1)} %gate1.3.a2, f32[4,128,384]{2,1,0:T(8,128)} %get-tuple-element.9.res, bf16[1152,1536]{1,0:T(8,128)(2,1)} %wd.7), custom_call_target="tpu_custom_call" | custom-call | tf_op jit(solution)/shard_map/down0/pallas_call | solution.py:33
  140.5 11.7 %collective-permute-done.14 = bf16[512,384]{1,0:T(8,128)(2,1)S(1)} collective-permute-done((bf16[512,384]{1,0:T(8,128)(2,1)}, bf16[512,384]{1,0:T(8,128)(2,1)S(1)}, u32[]{:S(2)}, u32[]{:S(2)}) %collective-permute-start.14) | collective-permute-done | bytes 393248 | tf_op jit(solution)/shard_map/ppermute | solution.py:23
  (86 shorter events, 42.9 us)
Async XLA Ops:
  0.6 43.0 %copy-start.18 = (s32[64]{0:T(128)S(1)}, s32[64]{0:T(128)}, u32[]{:S(2)}) copy-start(s32[64]{0:T(128)} %param.13) | copy-start | bytes 772
  0.6 13.9 %collective-permute-start.2 = (bf16[512,384]{1,0:T(8,128)(2,1)}, bf16[512,384]{1,0:T(8,128)(2,1)S(1)}, u32[]{:S(2)}, u32[]{:S(2)}) collective-permute-start(bf16[512,384]{1,0:T(8,128)(2,1)} %x0.3), channel_id=1, source_target_pairs={{0,1},{1,2},{2,3},{3,0},{4,5},{5,6},{6,7},{7,4},{8,9},{9,10},{10,1... | collective-permute-start | bytes 1179656 | tf_op jit(solution)/shard_map/ppermute | solution.py:23
  2.3 20.4 %collective-permute-start.1 = (bf16[512,384]{1,0:T(8,128)(2,1)}, bf16[512,384]{1,0:T(8,128)(2,1)S(1)}, u32[]{:S(2)}, u32[]{:S(2)}) collective-permute-start(bf16[512,384]{1,0:T(8,128)(2,1)} %x0.3), channel_id=1, source_target_pairs={{0,2},{1,3},{2,0},{3,1},{4,6},{5,7},{6,4},{7,5},{8,10},{9,11},{10,... | collective-permute-start | bytes 1179656 | tf_op jit(solution)/shard_map/ppermute | solution.py:23
  5.2 17.5 %collective-permute-start = (bf16[512,384]{1,0:T(8,128)(2,1)}, bf16[512,384]{1,0:T(8,128)(2,1)S(1)}, u32[]{:S(2)}, u32[]{:S(2)}) collective-permute-start(bf16[512,384]{1,0:T(8,128)(2,1)} %x0.3), channel_id=1, source_target_pairs={{0,3},{1,0},{2,1},{3,2},{4,7},{5,4},{6,5},{7,6},{8,11},{9,8},{10,9... | collective-permute-start | bytes 1179656 | tf_op jit(solution)/shard_map/ppermute | solution.py:23
  8.0 39.6 %copy-start.16 = (s32[8]{0:T(128)}, s32[8]{0:T(128)S(1)}, u32[]{:S(2)}) copy-start(s32[8]{0:T(128)S(1)} %bitcast_subtract_fusion.offsets) | copy-start | bytes 100
  14.5 8.1 %copy-start.2 = (bf16[512,384]{1,0:T(8,128)(2,1)}, bf16[512,384]{1,0:T(8,128)(2,1)S(1)}, u32[]{:S(2)}) copy-start(bf16[512,384]{1,0:T(8,128)(2,1)S(1)} %collective-permute-done.2.x3) | copy-start | bytes 1179652
  27.7 6.7 %collective-permute-start.5 = (bf16[256,128]{1,0:T(8,128)(2,1)}, bf16[256,128]{1,0:T(8,128)(2,1)S(1)}, u32[]{:S(2)}, u32[]{:S(2)}) collective-permute-start(bf16[256,128]{1,0:T(8,128)(2,1)} %get-tuple-element.7.y0), channel_id=1, source_target_pairs={{0,1},{1,2},{2,3},{3,0},{4,5},{5,6},{6,7},{7,4},{8,9},{9,10},{10,1... | collective-permute-start | bytes 196616 | tf_op jit(solution)/shard_map/ppermute | solution.py:23
  28.2 6.2 %collective-permute-start.4 = (bf16[256,128]{1,0:T(8,128)(2,1)}, bf16[256,128]{1,0:T(8,128)(2,1)S(1)}, u32[]{:S(2)}, u32[]{:S(2)}) collective-permute-start(bf16[256,128]{1,0:T(8,128)(2,1)} %get-tuple-element.7.y0), channel_id=1, source_target_pairs={{0,2},{1,3},{2,0},{3,1},{4,6},{5,7},{6,4},{7,5},{8,10},{9,11},{10,... | collective-permute-start | bytes 196616 | tf_op jit(solution)/shard_map/ppermute | solution.py:23
  30.6 4.5 %collective-permute-start.3 = (bf16[256,128]{1,0:T(8,128)(2,1)}, bf16[256,128]{1,0:T(8,128)(2,1)S(1)}, u32[]{:S(2)}, u32[]{:S(2)}) collective-permute-start(bf16[256,128]{1,0:T(8,128)(2,1)} %get-tuple-element.7.y0), channel_id=1, source_target_pairs={{0,3},{1,0},{2,1},{3,2},{4,7},{5,4},{6,5},{7,6},{8,11},{9,8},{10,9... | collective-permute-start | bytes 196616 | tf_op jit(solution)/shard_map/ppermute | solution.py:23
  37.9 10.1 %collective-permute-start.7 = (bf16[512,256]{1,0:T(8,128)(2,1)}, bf16[512,256]{1,0:T(8,128)(2,1)S(1)}, u32[]{:S(2)}, u32[]{:S(2)}) collective-permute-start(bf16[512,256]{1,0:T(8,128)(2,1)} %rotate.1.own.rows), channel_id=1, source_target_pairs={{0,4},{4,8},{8,12},{12,16},{16,20},{20,24},{24,28},{28,32},{32,36}... | collective-permute-start | bytes 786440 | tf_op jit(solution)/shard_map/ppermute | solution.py:28
  39.8 13.0 %collective-permute-start.6 = (bf16[512,256]{1,0:T(8,128)(2,1)}, bf16[512,256]{1,0:T(8,128)(2,1)S(1)}, u32[]{:S(2)}, u32[]{:S(2)}) collective-permute-start(bf16[512,256]{1,0:T(8,128)(2,1)} %rotate.1.own.rows), channel_id=1, source_target_pairs={{0,8},{4,12},{8,16},{12,20},{16,24},{20,28},{24,32},{28,36},{32,40... | collective-permute-start | bytes 786440 | tf_op jit(solution)/shard_map/ppermute | solution.py:28
  57.3 26.9 %collective-permute-start.8 = (bf16[128,1536]{1,0:T(8,128)(2,1)}, bf16[128,1536]{1,0:T(8,128)(2,1)S(1)}, u32[]{:S(2)}, u32[]{:S(2)}) collective-permute-start(bf16[128,1536]{1,0:T(8,128)(2,1)} %attend1.1), channel_id=1, source_target_pairs={{0,1},{1,2},{2,3},{3,0},{4,5},{5,6},{6,7},{7,4},{8,9},{9,10},{10,1... | collective-permute-start | bytes 1179656 | tf_op jit(solution)/shard_map/ppermute | solution.py:23
  62.2 17.4 %copy-start.17 = (f32[1536]{0:T(1024)S(1)}, f32[1536]{0:T(1024)}, u32[]{:S(2)}) copy-start(f32[1536]{0:T(1024)} %param.18) | copy-start | bytes 18436
  62.2 21.9 %collective-permute-start.9 = (bf16[128,1536]{1,0:T(8,128)(2,1)}, bf16[128,1536]{1,0:T(8,128)(2,1)S(1)}, u32[]{:S(2)}, u32[]{:S(2)}) collective-permute-start(bf16[128,1536]{1,0:T(8,128)(2,1)} %attend2.1), channel_id=1, source_target_pairs={{0,2},{1,3},{2,0},{3,1},{4,6},{5,7},{6,4},{7,5},{8,10},{9,11},{10,... | collective-permute-start | bytes 1179656 | tf_op jit(solution)/shard_map/ppermute | solution.py:23
  69.0 15.1 %collective-permute-start.10 = (bf16[128,1536]{1,0:T(8,128)(2,1)}, bf16[128,1536]{1,0:T(8,128)(2,1)S(1)}, u32[]{:S(2)}, u32[]{:S(2)}) collective-permute-start(bf16[128,1536]{1,0:T(8,128)(2,1)} %attend3.1), channel_id=1, source_target_pairs={{0,3},{1,0},{2,1},{3,2},{4,7},{5,4},{6,5},{7,6},{8,11},{9,8},{10,9... | collective-permute-start | bytes 1179656 | tf_op jit(solution)/shard_map/ppermute | solution.py:23
  72.8 62.6 %all-to-all-start = ((bf16[32,64,256]{2,1,0:T(8,128)(2,1)}), bf16[32,64,256]{2,1,0:T(8,128)(2,1)S(1)}, u32[]{:S(2)}, u32[]{:S(2)}) async-start(bf16[32,64,256]{2,1,0:T(8,128)(2,1)} %bitcast.10), calls=%async_computation | async-start | bytes 2097152 | tf_op jit(solution)/shard_map/all_to_all | solution.py:306
  89.0 13.7 %collective-permute-start.13 = (bf16[128,1536]{1,0:T(8,128)(2,1)}, bf16[128,1536]{1,0:T(8,128)(2,1)S(1)}, u32[]{:S(2)}, u32[]{:S(2)}) collective-permute-start(bf16[128,1536]{1,0:T(8,128)(2,1)} %get-tuple-element.8.refs_0_), channel_id=1, source_target_pairs={{0,2},{1,3},{2,0},{3,1},{4,6},{5,7},{6,4},{7,5},{8,10},{9,11},{10,... | collective-permute-start | bytes 1179656 | tf_op jit(solution)/shard_map/ppermute | solution.py:23
  90.4 19.9 %collective-permute-start.12 = (bf16[128,1536]{1,0:T(8,128)(2,1)}, bf16[128,1536]{1,0:T(8,128)(2,1)S(1)}, u32[]{:S(2)}, u32[]{:S(2)}) collective-permute-start(bf16[128,1536]{1,0:T(8,128)(2,1)} %get-tuple-element.8.refs_0_), channel_id=1, source_target_pairs={{0,1},{1,2},{2,3},{3,0},{4,5},{5,6},{6,7},{7,4},{8,9},{9,10},{10,1... | collective-permute-start | bytes 1179656 | tf_op jit(solution)/shard_map/ppermute | solution.py:23
  90.6 19.8 %collective-permute-start.11 = (bf16[128,1536]{1,0:T(8,128)(2,1)}, bf16[128,1536]{1,0:T(8,128)(2,1)S(1)}, u32[]{:S(2)}, u32[]{:S(2)}) collective-permute-start(bf16[128,1536]{1,0:T(8,128)(2,1)} %get-tuple-element.8.refs_0_), channel_id=1, source_target_pairs={{0,3},{1,0},{2,1},{3,2},{4,7},{5,4},{6,5},{7,6},{8,11},{9,8},{10,9... | collective-permute-start | bytes 1179656 | tf_op jit(solution)/shard_map/ppermute | solution.py:23
  127.0 5.1 %copy-start.8 = (bf16[512,384]{1,0:T(8,128)(2,1)S(1)}, bf16[512,384]{1,0:T(8,128)(2,1)}, u32[]{:S(2)}) copy-start(bf16[512,384]{1,0:T(8,128)(2,1)} %down2.1) | copy-start | bytes 1179652
  127.0 6.3 %copy-start.7 = (bf16[512,384]{1,0:T(8,128)(2,1)S(1)}, bf16[512,384]{1,0:T(8,128)(2,1)}, u32[]{:S(2)}) copy-start(bf16[512,384]{1,0:T(8,128)(2,1)} %down3.1) | copy-start | bytes 1179652
  131.3 20.9 %collective-permute-start.14 = (bf16[512,384]{1,0:T(8,128)(2,1)}, bf16[512,384]{1,0:T(8,128)(2,1)S(1)}, u32[]{:S(2)}, u32[]{:S(2)}) collective-permute-start(bf16[512,384]{1,0:T(8,128)(2,1)} %down1.1), channel_id=1, source_target_pairs={{0,1},{1,2},{2,3},{3,0},{4,5},{5,6},{6,7},{7,4},{8,9},{9,10},{10,1... | collective-permute-start | bytes 1179656 | tf_op jit(solution)/shard_map/ppermute | solution.py:23
  132.1 20.1 %collective-permute-start.15 = (bf16[512,384]{1,0:T(8,128)(2,1)S(1)}, bf16[512,384]{1,0:T(8,128)(2,1)S(1)}, u32[]{:S(2)}, u32[]{:S(2)}) collective-permute-start(bf16[512,384]{1,0:T(8,128)(2,1)S(1)} %copy-done.8), channel_id=1, source_target_pairs={{0,2},{1,3},{2,0},{3,1},{4,6},{5,7},{6,4},{7,5},{8,10},{9,11},{10,... | collective-permute-start | bytes 1179656 | tf_op jit(solution)/shard_map/ppermute | solution.py:23
  133.4 19.2 %collective-permute-start.16 = (bf16[512,384]{1,0:T(8,128)(2,1)S(1)}, bf16[512,384]{1,0:T(8,128)(2,1)S(1)}, u32[]{:S(2)}, u32[]{:S(2)}) collective-permute-start(bf16[512,384]{1,0:T(8,128)(2,1)S(1)} %copy-done.7), channel_id=1, source_target_pairs={{0,3},{1,0},{2,1},{3,2},{4,7},{5,4},{6,5},{7,6},{8,11},{9,8},{10,9... | collective-permute-start | bytes 1179656 | tf_op jit(solution)/shard_map/ppermute | solution.py:23
  (13 other events, 13.6 us)

commit v2 on v1

v2 whole, which is shorter than its diff:
```python
import functools
import math

import jax
import jax.numpy as jnp
from jax import lax
from jax.experimental import pallas as pl
from jax.experimental.pallas import tpu as pltpu
from jax.sharding import PartitionSpec as P

HD = 128
WIN = 1024
BLK = 128
epsilon = 1e-06
bf16 = jnp.bfloat16
f32 = jnp.float32
VM = pl.BlockSpec(memory_space=pltpu.VMEM)
SM = pl.BlockSpec(memory_space=pltpu.SMEM)


def from_peer(block, distance):
    n = lax.axis_size("feat")
    return lax.ppermute(block, "feat", [(i, (i - distance) % n) for i in range(n)])


def from_earlier(block, distance):
    n = lax.axis_size("seq")
    return lax.ppermute(block, "seq", [(i - distance, i) for i in range(distance, n)])


def from_partner(block, bits):
    n = lax.axis_size("seq")
    return lax.ppermute(block, "seq", [(i, i ^ bits) for i in range(n)])


def run(body, outs, name, scalars, arrays, scratch=(), vmem=16 << 20):
    many = isinstance(outs, (list, tuple))
    return pl.pallas_call(
        body,
        out_shape=outs,
        in_specs=[SM] * len(scalars) + [VM] * len(arrays),
        out_specs=[VM] * len(outs) if many else VM,
        scratch_shapes=list(scratch),
        compiler_params=pltpu.CompilerParams(vmem_limit_bytes=vmem),
        cost_estimate=pl.CostEstimate(flops=2_000_000_000, transcendentals=0, bytes_accessed=10_000_000),
        name=name,
    )(*scalars, *arrays)


def dot(a, b):
    return jnp.dot(a, b, preferred_element_type=f32)


def copy_body(source, out):
    out[...] = source[...]


def merge(kept, landed, first, second):
    half = first.shape[0]
    first[...] = (kept[:half, :].astype(f32) + landed[:half, :].astype(f32)).astype(bf16)
    second[...] = (kept[half:, :].astype(f32) + landed[half:, :].astype(f32)).astype(bf16)


def norm_kv_body(place, x0, x1, x2, x3, gain, wkv, n_out, kv_out, kept):
    f = place[0]
    xs = (x0, x1, x2, x3)
    tokens, width = x0.shape
    step = 128
    for r in range(tokens // step):
        rows = pl.ds(r * step, step)
        total = None
        for x in xs:
            v = x[rows, :].astype(f32)
            part = jnp.sum(v * v, axis=1, keepdims=True)
            total = part if total is None else total + part
        scale = lax.rsqrt(total / (width * 4) + epsilon)
        for d, x in enumerate(xs):
            g = lax.rem(f + d, 4)
            v = x[rows, :].astype(f32) * scale * gain[pl.ds(g, 1), :]
            n_out[d, rows, :] = v.astype(bf16)
    own = kept.shape[1]
    own_rows = pl.ds(pl.multiple_of(f * own, own), own)
    for d, x in enumerate(xs):
        kept[lax.rem(f + d, 4)] = x[own_rows, :]
    acc = None
    for d in range(4):
        g = lax.rem(f + d, 4)
        start = pl.multiple_of(g * width, 128)
        part = dot(n_out[d], wkv[pl.ds(start, width), :])
        acc = part if acc is None else acc + part
    kv = acc.astype(bf16)
    half = tokens // 2
    kv_out[...] = jnp.concatenate([kv[:half], kv[half:]], axis=1)


def query_body(place, n_in, wq, cosine, sine, q_out):
    f = place[0]
    width = n_in.shape[2]
    acc = None
    for d in range(4):
        g = lax.rem(f + d, 4)
        start = pl.multiple_of(g * width, 128)
        part = dot(n_in[d], wq[pl.ds(start, width), :])
        acc = part if acc is None else acc + part
    c = cosine[...]
    s = sine[...]
    for h in range(acc.shape[1] // HD):
        v = acc[:, h * HD : (h + 1) * HD]
        q_out[:, h * HD : (h + 1) * HD] = (v * c + pltpu.roll(v, HD // 2, 1) * s).astype(bf16)


def rotate_body(place, y0, y1, y2, y3, cosine, sine, out, hold):
    f = place[0]
    half = y0.shape[0]
    for d, y in enumerate((y0, y1, y2, y3)):
        hold[lax.rem(f + d, 4)] = y[...].astype(f32)
    for part in range(2):
        rows = pl.ds(part * half, half)
        lanes = slice(part * 64, part * 64 + 64)
        k = jnp.concatenate([hold[0][:, lanes], hold[1][:, lanes]], axis=1)
        v = jnp.concatenate([hold[2][:, lanes], hold[3][:, lanes]], axis=1)
        k = k * cosine[rows, :] + pltpu.roll(k, HD // 2, 1) * sine[rows, :]
        out[rows, :HD] = k.astype(bf16)
        out[rows, HD:] = v.astype(bf16)


def attend_body(d, place, offsets, q, far, near, own, wo, *refs):
    if d == 0:
        merge(refs[0], refs[1], refs[3], refs[4])
        refs = refs[2:3] + refs[5:]
    out, win, att = refs
    f = place[0]
    first = place[1]
    tokens = own.shape[0]
    heads = q.shape[1] // HD
    win[pl.ds(0, tokens), :] = far[...]
    win[pl.ds(tokens, tokens), :] = near[...]
    win[pl.ds(2 * tokens, tokens), :] = own[...]
    step = 128
    b = lax.rem(f + d, 4)
    row0 = pl.multiple_of(b * step, step)
    pos = first + row0 + lax.broadcasted_iota(jnp.int32, (step, 1), 0)
    begin = jnp.zeros((step, 1), jnp.int32)
    for r in range(offsets.shape[0]):
        begin = jnp.where(pos >= offsets[r], offsets[r], begin)
    low = jnp.maximum(pos - (WIN - 1), begin)
    low = jnp.concatenate([low] * heads, axis=0)
    high = jnp.concatenate([pos] * heads, axis=0)
    qs = jnp.concatenate([q[pl.ds(row0, step), h * HD : (h + 1) * HD] for h in range(heads)], axis=0)
    factor = HD**-0.5 * math.log2(math.e)
    total = None
    mixed = None
    for start, size in ((0, 512), (512, 512), (1024, 128)):
        k = win[pl.ds(row0 + start, size), :HD]
        v = win[pl.ds(row0 + start, size), HD:]
        kpos = first + row0 + (start - WIN) + lax.broadcasted_iota(jnp.int32, (heads * step, size), 1)
        allowed = kpos >= low
        if start == WIN:
            allowed = allowed & (kpos <= high)
        s = lax.dot_general(qs, k, (((1,), (1,)), ((), ())), preferred_element_type=f32)
        p = jnp.where(allowed, jnp.exp2(s * factor), 0.0)
        part = jnp.sum(p, axis=1, keepdims=True)
        total = part if total is None else total + part
        part = dot(p.astype(bf16), v)
        mixed = part if mixed is None else mixed + part
    mixed = (mixed / total).astype(bf16)
    for h in range(heads):
        att[:, h * HD : (h + 1) * HD] = mixed[h * step : (h + 1) * step]
    out[...] = dot(att[...], wo[...]).astype(out.dtype)


def residual_body(kept, p0, p1, p2, p3, gain, rows, landed, res_out, n_out, first, second):
    merge(rows, landed, first, second)
    width = kept.shape[2]
    total = None
    for g in range(4):
        cols = slice(g * width, (g + 1) * width)
        v = kept[g].astype(f32) + p0[:, cols]
        v = v + p1[:, cols].astype(f32)
        v = v + p2[:, cols].astype(f32)
        v = v + p3[:, cols].astype(f32)
        res_out[g] = v
        part = jnp.sum(v * v, axis=1, keepdims=True)
        total = part if total is None else total + part
    scale = lax.rsqrt(total / (width * 4) + epsilon)
    for g in range(4):
        cols = slice(g * width, (g + 1) * width)
        n_out[:, cols] = (res_out[g] * scale * gain[:, cols]).astype(bf16)


def gelu(x):
    inner = math.sqrt(2 / math.pi) * (x + 0.044715 * (x * x * x))
    return x * (0.5 * (1.0 + jnp.tanh(inner)))


def feed_body(count, own, before, *refs):
    place = refs[0]
    blocks = refs[1 : 1 + count]
    refs = refs[1 + count :]
    res = earlier = None
    if own:
        merge(refs[0], refs[1], refs[-4], refs[-3])
        res, refs = refs[2], refs[3:-4] + refs[-2:]
    elif before:
        earlier, refs = refs[:3], refs[3:]
    else:
        refs[-3][...] = (refs[0][...].astype(f32) + refs[1][...].astype(f32)).astype(bf16)
        refs = refs[2:-3] + refs[-2:]
    wg, wu, wd, o0, o1, o2, o3, act, hold = refs
    f = place[0]
    rows, width = o0.shape
    n = jnp.concatenate([r[...] for r in blocks], axis=0) if count > 1 else blocks[0][...]
    chunk = 384
    for c in range(wg.shape[1] // chunk):
        cols = slice(c * chunk, (c + 1) * chunk)
        act[:, cols] = (gelu(dot(n, wg[:, cols])) * dot(n, wu[:, cols])).astype(bf16)
    for g in range(4):
        part = dot(act[...], wd[:, g * width : (g + 1) * width])
        hold[g] = part + res[g] if own else part
    o0[...] = hold[f]
    for d, o in ((1, o1), (2, o2), (3, o3)):
        lead = o.shape[0] - rows
        if before:
            o[:lead, :] = earlier[d - 1][...]
        o[lead:, :] = hold[lax.rem(f + d, 4)].astype(o.dtype)


def finish_body(place, *refs):
    ins, out, hold = refs[:-2], refs[-2], refs[-1]
    f = place[0]
    step = hold.shape[1]
    own, both, far = ins[:3]
    hold[f] = own[...]
    hold[lax.rem(f + 1, 4)] = both[:step]
    hold[lax.rem(f + 3, 4)] = both[step:]
    hold[lax.rem(f + 2, 4)] = far[...]
    for e in range(1, 4):
        early, far = ins[2 * e + 1 : 2 * e + 3]
        for row, shift in ((0, 0), (1, 1), (2, 3)):
            b = lax.rem(f + e + shift, 4)
            hold[b] = hold[b] + early[row * step : (row + 1) * step].astype(f32)
        b = lax.rem(f + e + 2, 4)
        hold[b] = hold[b] + far[...].astype(f32)
    for b in range(4):
        out[b * step : (b + 1) * step, :] = hold[b].astype(bf16)


def image_body(target, other, rows, sibling, sent, kept):
    step = sent.shape[0]
    for part, out in enumerate((sent, kept)):
        index = part * step + lax.broadcasted_iota(jnp.int32, (step, target.shape[1]), 0)
        hot = jnp.where(index == target[...], 1.0, 0.0).astype(bf16)
        total = dot(hot, rows[...])
        hot = jnp.where(index == other[...], 1.0, 0.0).astype(bf16)
        out[...] = (total + dot(hot, sibling[...])).astype(bf16)


def shards(
    hidden,
    lengths,
    page_table,
    first_gain,
    query_weight,
    keyvalue_weight,
    output_weight,
    second_gain,
    gate_weight,
    up_weight,
    down_weight,
):
    tokens, width = hidden.shape
    full = width * 4
    seq_index = lax.axis_index("seq")
    f = lax.axis_index("feat")
    first = seq_index * tokens
    place = jnp.stack([f, first]).astype(jnp.int32)
    sds = jax.ShapeDtypeStruct

    x0 = run(copy_body, sds(hidden.shape, bf16), "take_own", [], [hidden])
    x2 = from_peer(hidden, 2)
    x1 = from_peer(hidden, 1)
    x3 = from_peer(hidden, 3)

    offsets = jnp.cumsum(lengths) - lengths
    ticks = jnp.arange(tokens, dtype=jnp.int32)
    places = jnp.concatenate([first + ticks, (seq_index ^ 1) * tokens + ticks])
    numbers = jnp.arange(lengths.shape[0], dtype=jnp.int32)
    segment = jnp.sum((places[:, None] >= offsets[None, :]).astype(jnp.int32), axis=1) - 1
    member = (segment[:, None] == numbers[None, :]).astype(jnp.int32)
    inner = places - jnp.sum(member * offsets[None, :], axis=1)
    length = jnp.sum(member * lengths[None, :], axis=1)
    half = HD // 2
    freq = jnp.exp(jnp.arange(half, dtype=f32) * (-2.0 * math.log(10000.0) / HD))
    angle = inner[:tokens].astype(f32)[:, None] * freq[None, :]
    cosine = jnp.cos(angle)
    sine = jnp.sin(angle)
    cosine = jnp.concatenate([cosine, cosine], axis=1)
    sine = jnp.concatenate([-sine, sine], axis=1)

    pages = page_table.shape[0]
    part_rows = BLK // 4
    keep = inner >= length - WIN
    slot = inner % WIN
    entry = segment * (WIN // BLK) + slot // BLK
    page = jnp.sum(
        jnp.where(
            entry[:, None] == jnp.arange(pages, dtype=jnp.int32)[None, :], page_table[None, :], 0
        ),
        axis=1,
    )
    within = slot % BLK
    owner = page // 2

    def rank(mine, theirs):
        apart = mine ^ theirs
        return jnp.where(apart == 1, 0, jnp.where(apart == 2, 1, jnp.where(apart == 0, 2, 3)))

    column = rank(seq_index // 8, owner // 8) * 4 + rank(seq_index // 2 % 4, owner // 2 % 4)
    mine = keep & (within // part_rows == f) & (owner % 2 == seq_index % 2)
    target = jnp.where(mine, (column * 2 + page % 2) * part_rows + within % part_rows, -1)
    other = target[None, tokens:]
    target = target[None, :tokens]
    held_rows = 2 * part_rows

    gain1 = first_gain.reshape(4, width)
    gain2 = second_gain.reshape(1, full)
    x1, x2, x3, target, other, cosine, sine, offsets, place, gain1, gain2 = lax.optimization_barrier(
        (x1, x2, x3, target, other, cosine, sine, offsets, place, gain1, gain2)
    )
    step = tokens // 4

    normed, kv_part, kept = run(
        norm_kv_body,
        (
            sds((4, tokens, width), bf16),
            sds((tokens // 2, 128), bf16),
            sds((4, step, width), bf16),
        ),
        "norm_kv",
        [place],
        [x0, x1, x2, x3, gain1, keyvalue_weight],
    )
    y2 = from_peer(kv_part, 2)
    y1 = from_peer(kv_part, 1)
    y3 = from_peer(kv_part, 3)
    queries = run(
        query_body,
        sds((tokens, query_weight.shape[1]), bf16),
        "queries",
        [place],
        [normed, query_weight, cosine, sine],
    )
    rotated = run(
        rotate_body,
        sds((tokens, 2 * HD), bf16),
        "rotate",
        [place],
        [kv_part, y1, y2, y3, cosine, sine],
        [pltpu.VMEM((4, tokens // 2, 128), f32)],
    )
    far = from_earlier(rotated, 2)
    near = from_earlier(rotated, 1)
    sibling = from_partner(rotated, 1)
    image_sent, image_kept = run(
        image_body,
        [sds((8 * held_rows, 2 * HD), bf16)] * 2,
        "image",
        [],
        [target, other, rotated, sibling],
    )
    landed = from_partner(image_sent, 8)

    def halves(rows):
        return [sds((rows.shape[0] // 2, 2 * HD), bf16)] * 2

    queries = lax.optimization_barrier((queries, image_sent))[0]

    def attend(d, kind, cached=()):
        out = sds((step, full), kind)
        return run(
            functools.partial(attend_body, d),
            [out, *halves(cached[0])] if cached else out,
            f"attend{d}",
            [place, offsets],
            [queries, far, near, rotated, output_weight, *cached],
            [
                pltpu.VMEM((3 * tokens, 2 * HD), bf16),
                pltpu.VMEM((step, query_weight.shape[1]), bf16),
            ],
        )

    p2 = from_peer(attend(2, bf16), 2)
    p1 = from_peer(attend(1, bf16), 3)
    p3 = from_peer(attend(3, bf16), 1)
    p0, stay, go = attend(0, f32, [image_kept, landed])
    landed = from_partner(go, 24)
    residual, normed2, go, stay = run(
        residual_body,
        [sds((4, step, width), f32), sds((step, full), bf16), *halves(stay)],
        "residual",
        [],
        [kept, p0, p1, p2, p3, gain2, stay, landed],
    )
    landed = from_partner(go, 2)
    m1 = from_peer(normed2, 1)
    m3 = from_peer(normed2, 3)
    m2 = from_peer(normed2, 2)

    hidden_units = gate_weight.shape[1]

    def feed(blocks, res=(), before=(), cached=()):
        rows = step * len(blocks)
        sent = rows + (step if before else 0)
        outs = [sds((rows, width), f32)] + [sds((sent, width), bf16)] * 3
        if cached:
            outs = outs + (halves(cached[0]) if res else [sds(cached[0].shape, bf16)])
        return run(
            functools.partial(feed_body, len(blocks), bool(res), bool(before)),
            outs,
            f"feed{len(blocks)}" + ("own" if res else ""),
            [place],
            [*blocks, *cached, *res, *before, gate_weight, up_weight, down_weight],
            [pltpu.VMEM((rows, hidden_units), bf16), pltpu.VMEM((4, rows, width), f32)],
            vmem=24 << 20,
        )

    own0, *own_sent, stay, go = feed([normed2], res=[residual], cached=[stay, landed])
    landed = from_partner(go, 6)
    both0, *early = feed([m1, m3], before=own_sent)
    early = [from_peer(early[1], 2), from_peer(early[0], 3), from_peer(early[2], 1)]
    far0, *late, cache = feed([m2], cached=[stay, landed])
    late = [from_peer(late[1], 2), from_peer(late[0], 3), from_peer(late[2], 1)]
    got = [own0, both0, far0, early[2], late[2], early[0], late[0], early[1], late[1]]
    output = run(
        finish_body,
        sds((tokens, width), bf16),
        "finish",
        [place],
        got,
        [pltpu.VMEM((4, step, width), f32)],
    )
    return (output, cache.reshape(2, part_rows, 2 * HD))


def solution(mesh):
    placed = (
        P("seq", "feat"),
        P(),
        P(),
        P(),
        P(None, "feat"),
        P(None, "feat"),
        P("feat", None),
        P(),
        P(None, "feat"),
        P(None, "feat"),
        P("feat", None),
    )
    return jax.shard_map(
        shards,
        mesh=mesh,
        in_specs=placed,
        out_specs=(P("seq", "feat"), P("seq", "feat", None)),
        check_vma=False,
    )
```

time: 155 us -> 119 us (0.77)
  Pallas kernels: 65.1 us -> 25.6 us
  waiting for transfers between devices: 32.8 us -> 44.8 us
  local copies, waits for them, and re-layouts: 10.5 us -> 3.57 us
  other arithmetic: 9.16 us -> 4.52 us
  starting transfers between devices: 36.3 us -> 39.8 us
    pallas_call x16 -> x14, Pallas kernels: 65.1 us -> 25.6 us  [run(): pl.pallas_call(body, out_shape=outs, in_specs=[SM] * len(scalars) + [VM]...]
    ppermute x0 -> x5, waiting for transfers between devices: none -> 9.58 us  [from_partner(): return lax.ppermute(block, 'seq', [(i, i ^ bits) for i in range(n)])]
    ppermute x15 -> x18, starting transfers between devices: 23.8 us -> 31.2 us  [from_peer(): lax.ppermute(block, 'feat', [(i, (i - distance) % n) for i in range(n)])]
    all_to_all x1 -> x0, starting transfers between devices: 6.83 us -> none  [shards(): landed = lax.all_to_all(image, 'seq', 0, 0, tiled=False)]
    unnamed x39 -> x13, local copies, waits for them, and re-layouts: 8.59 us -> 2.16 us
    ppermute x0 -> x5, starting transfers between devices: none -> 2.39 us  [from_partner(): return lax.ppermute(block, 'seq', [(i, i ^ bits) for i in range(n)])]
    convert_element_type x1, other arithmetic: 2.05 us -> 0.01 us  [shards(): angle = inner[:tokens].astype(f32)[:, None] * freq[None, :]]
    ppermute x15 -> x18, waiting for transfers between devices: 27.6 us -> 29.2 us  [from_peer(): lax.ppermute(block, 'feat', [(i, (i - distance) % n) for i in range(n)])]
  transfers between devices with their start and end apart: 18 -> 25, of which waited for: 9 -> 15; matrix products, arithmetic and copies ran while one was open for 7% -> 6% of each run, Pallas kernels for 36% -> 18%
where the time goes in v2:
time: 119 us
  waiting for transfers between devices  44.8 us (38%)
  starting transfers between devices  39.8 us (33%)
  Pallas kernels  25.6 us (22%)
  other arithmetic  4.52 us (4%)
  local copies, waits for them, and re-layouts  3.57 us (3%)
    ppermute x18, starting transfers between devices, from_peer(): lax.ppermute(block, 'feat', [(i, (i - distance) % n) for i in range(n)])  31.2 us
    ppermute x18, waiting for transfers between devices, from_peer(): lax.ppermute(block, 'feat', [(i, (i - distance) % n) for i in range(n)])  29.2 us
    pallas_call x14, Pallas kernels, run(): pl.pallas_call(body, out_shape=outs, in_specs=[SM] * len(scalars) + [VM]...  25.6 us
    ppermute x5, waiting for transfers between devices, from_partner(): return lax.ppermute(block, 'seq', [(i, i ^ bits) for i in range(n)])  9.58 us
    ppermute x2, starting transfers between devices, from_earlier(): lax.ppermute(block, 'seq', [(i - distance, i) for i in range(distance, n)])  6.22 us
    ppermute x2, waiting for transfers between devices, from_earlier(): lax.ppermute(block, 'seq', [(i - distance, i) for i in range(distance, n)])  6.07 us
    ppermute x5, starting transfers between devices, from_partner(): return lax.ppermute(block, 'seq', [(i, i ^ bits) for i in range(n)])  2.39 us
  transfers between devices with their start and end apart: 25, of which 15 were waited for; matrix products, arithmetic and copies ran while one was open for 6% of the time, Pallas kernels for 18%

profile of v2, /device:TPU:6, one launch (start us, length us, event | category | flops | bytes accessed | tf_op | source)
XLA Modules:
  0.0 119.2 jit_solution(12637059364523963598)
XLA Ops:
  0.6 3.3 %collective-permute-start.1 = (bf16[512,384]{1,0:T(8,128)(2,1)}, bf16[512,384]{1,0:T(8,128)(2,1)S(1)}, u32[]{:S(2)}, u32[]{:S(2)}) collective-permute-start(bf16[512,384]{1,0:T(8,128)(2,1)} %source.1), channel_id=1, source_target_pairs={{0,2},{1,3},{2,0},{3,1},{4,6},{5,7},{6,4},{7,5},{8,10},{9,11},{10,... | collective-permute-start | bytes 1179656 | tf_op jit(solution)/shard_map/ppermute | solution.py:23
  14.5 7.6 %collective-permute-done.x1 = bf16[512,384]{1,0:T(8,128)(2,1)S(1)} collective-permute-done((bf16[512,384]{1,0:T(8,128)(2,1)}, bf16[512,384]{1,0:T(8,128)(2,1)S(1)}, u32[]{:S(2)}, u32[]{:S(2)}) %collective-permute-start) | collective-permute-done | bytes 393248 | tf_op jit(solution)/shard_map/ppermute | solution.py:23
  25.2 2.7 %collective-permute-start.4 = (bf16[256,128]{1,0:T(8,128)(2,1)S(1)}, bf16[256,128]{1,0:T(8,128)(2,1)S(1)}, u32[]{:S(2)}, u32[]{:S(2)}) collective-permute-start(bf16[256,128]{1,0:T(8,128)(2,1)S(1)} %get-tuple-element.53.y0), channel_id=1, source_target_pairs={{0,2},{1,3},{2,0},{3,1},{4,6},{5,7},{6,4},{7,5},{8,10},{9,11},{10,... | collective-permute-start | bytes 196616 | tf_op jit(solution)/shard_map/ppermute | solution.py:23
  29.4 2.0 %collective-permute-done.4.y2 = bf16[256,128]{1,0:T(8,128)(2,1)S(1)} collective-permute-done((bf16[256,128]{1,0:T(8,128)(2,1)S(1)}, bf16[256,128]{1,0:T(8,128)(2,1)S(1)}, u32[]{:S(2)}, u32[]{:S(2)}) %collective-permute-start.4) | collective-permute-done | bytes 65568 | tf_op jit(solution)/shard_map/ppermute | solution.py:23
  33.2 2.4 %collective-permute-start.8 = (bf16[512,256]{1,0:T(8,128)(2,1)S(1)}, bf16[512,256]{1,0:T(8,128)(2,1)S(1)}, u32[]{:S(2)}, u32[]{:S(2)}) collective-permute-start(bf16[512,256]{1,0:T(8,128)(2,1)S(1)} %rotate.1.rows.own), channel_id=1, source_target_pairs={{0,4},{4,8},{8,12},{12,16},{16,20},{20,24},{24,28},{28,32},{32,36}... | collective-permute-start | bytes 786440 | tf_op jit(solution)/shard_map/ppermute | solution.py:28
  35.6 3.8 %collective-permute-start.7 = (bf16[512,256]{1,0:T(8,128)(2,1)S(1)}, bf16[512,256]{1,0:T(8,128)(2,1)S(1)}, u32[]{:S(2)}, u32[]{:S(2)}) collective-permute-start(bf16[512,256]{1,0:T(8,128)(2,1)S(1)} %rotate.1.rows.own), channel_id=1, source_target_pairs={{0,8},{4,12},{8,16},{12,20},{16,24},{20,28},{24,32},{28,36},{32,40... | collective-permute-start | bytes 786440 | tf_op jit(solution)/shard_map/ppermute | solution.py:28
  43.7 5.3 %collective-permute-done.7.far = bf16[512,256]{1,0:T(8,128)(2,1)S(1)} collective-permute-done((bf16[512,256]{1,0:T(8,128)(2,1)S(1)}, bf16[512,256]{1,0:T(8,128)(2,1)S(1)}, u32[]{:S(2)}, u32[]{:S(2)}) %collective-permute-start.7) | collective-permute-done | bytes 262176 | tf_op jit(solution)/shard_map/ppermute | solution.py:28
  51.7 1.9 %attend2.1 = bf16[128,1536]{1,0:T(8,128)(2,1)S(1)} custom-call(s32[2]{0:T(128)S(1)} %pad_add_fusion.1.place.refs_0_, s32[8]{0:T(128)S(1)} %bitcast_subtract_fusion.offsets, bf16[512,384]{1,0:T(8,128)(2,1)S(1)} %queries.1.q, bf16[512,256]{1,0:T(8,128)(2,1)S(1)} %collective-permute-done.7.far, bf16[512,256]{1,0:T(8,128)(2,1)S(1)} %collective-permute-done.8.near, ...), custom_call_target="tpu_custom_call" | custom-call | flops 2000000000 | bytes 10000000 | tf_op jit(solution)/shard_map/attend2/pallas_call | solution.py:38
  53.5 3.4 %collective-permute-start.11 = (bf16[128,1536]{1,0:T(8,128)(2,1)S(1)}, bf16[128,1536]{1,0:T(8,128)(2,1)S(1)}, u32[]{:S(2)}, u32[]{:S(2)}) collective-permute-start(bf16[128,1536]{1,0:T(8,128)(2,1)S(1)} %attend2.1), channel_id=1, source_target_pairs={{0,2},{1,3},{2,0},{3,1},{4,6},{5,7},{6,4},{7,5},{8,10},{9,11},{10,... | collective-permute-start | bytes 1179656 | tf_op jit(solution)/shard_map/ppermute | solution.py:23
  56.9 1.9 %attend3.1 = bf16[128,1536]{1,0:T(8,128)(2,1)S(1)} custom-call(s32[2]{0:T(128)S(1)} %pad_add_fusion.1.place.refs_0_, s32[8]{0:T(128)S(1)} %bitcast_subtract_fusion.offsets, bf16[512,384]{1,0:T(8,128)(2,1)S(1)} %queries.1.q, bf16[512,256]{1,0:T(8,128)(2,1)S(1)} %collective-permute-done.7.far, bf16[512,256]{1,0:T(8,128)(2,1)S(1)} %collective-permute-done.8.near, ...), custom_call_target="tpu_custom_call" | custom-call | flops 2000000000 | bytes 10000000 | tf_op jit(solution)/shard_map/attend3/pallas_call | solution.py:38
  59.4 1.9 %attend0.1 = (f32[128,1536]{1,0:T(8,128)S(1)}, bf16[256,256]{1,0:T(8,128)(2,1)S(1)}, bf16[256,256]{1,0:T(8,128)(2,1)S(1)}) custom-call(s32[2]{0:T(128)S(1)} %pad_add_fusion.1.place.refs_0_, s32[8]{0:T(128)S(1)} %bitcast_subtract_fusion.offsets, bf16[512,384]{1,0:T(8,128)(2,1)S(1)} %queries.1.q, bf16[512,256]{1,0:T(8,128)(2,1)S(1)} %collective-permute-done.7.far, ...), custom_call_target="tpu_custom_call" | custom-call | flops 2000000000 | bytes 10000000 | tf_op jit(solution)/shard_map/attend0/pallas_call | solution.py:38
  61.4 6.2 %collective-permute-done.13.landed = bf16[256,256]{1,0:T(8,128)(2,1)S(1)} collective-permute-done((bf16[256,256]{1,0:T(8,128)(2,1)S(1)}, bf16[256,256]{1,0:T(8,128)(2,1)S(1)}, u32[]{:S(2)}, u32[]{:S(2)}) %collective-permute-start.13) | collective-permute-done | bytes 131104 | tf_op jit(solution)/shard_map/ppermute | solution.py:33
  67.6 5.0 %collective-permute-done.11.p2 = bf16[128,1536]{1,0:T(8,128)(2,1)S(1)} collective-permute-done((bf16[128,1536]{1,0:T(8,128)(2,1)S(1)}, bf16[128,1536]{1,0:T(8,128)(2,1)S(1)}, u32[]{:S(2)}, u32[]{:S(2)}) %collective-permute-start.11) | collective-permute-done | bytes 393248 | tf_op jit(solution)/shard_map/ppermute | solution.py:23
  75.9 2.2 %collective-permute-start.15 = (bf16[128,1536]{1,0:T(8,128)(2,1)S(1)}, bf16[128,1536]{1,0:T(8,128)(2,1)S(1)}, u32[]{:S(2)}, u32[]{:S(2)}) collective-permute-start(bf16[128,1536]{1,0:T(8,128)(2,1)S(1)} %get-tuple-element.61.refs_1_), channel_id=1, source_target_pairs={{0,3},{1,0},{2,1},{3,2},{4,7},{5,4},{6,5},{7,6},{8,11},{9,8},{10,9... | collective-permute-start | bytes 1179656 | tf_op jit(solution)/shard_map/ppermute | solution.py:23
  79.0 3.4 %collective-permute-done.14.refs_3_ = bf16[128,256]{1,0:T(8,128)(2,1)S(1)} collective-permute-done((bf16[128,256]{1,0:T(8,128)(2,1)S(1)}, bf16[128,256]{1,0:T(8,128)(2,1)S(1)}, u32[]{:S(2)}, u32[]{:S(2)}) %collective-permute-start.14) | collective-permute-done | bytes 65568 | tf_op jit(solution)/shard_map/ppermute | solution.py:33
  82.4 2.8 %feed1own.1 = (f32[128,384]{1,0:T(8,128)S(1)}, bf16[128,384]{1,0:T(8,128)(2,1)S(1)}, bf16[128,384]{1,0:T(8,128)(2,1)S(1)}, bf16[128,384]{1,0:T(8,128)(2,1)S(1)},...) custom-call(s32[2]{0:T(128)S(1)} %pad_add_fusion.1.place.refs_0_, ...), custom_call_target="tpu_custom_call" | custom-call | flops 2000000000 | bytes 10000000 | tf_op jit(solution)/shard_map/feed1own/pallas_call | solution.py:38
  86.8 6.8 %collective-permute-done.15.refs_1_ = bf16[128,1536]{1,0:T(8,128)(2,1)S(1)} collective-permute-done((bf16[128,1536]{1,0:T(8,128)(2,1)S(1)}, bf16[128,1536]{1,0:T(8,128)(2,1)S(1)}, u32[]{:S(2)}, u32[]{:S(2)}) %collective-permute-start.15) | collective-permute-done | bytes 393248 | tf_op jit(solution)/shard_map/ppermute | solution.py:23
  93.7 4.8 %feed2.1 = (f32[256,384]{1,0:T(8,128)S(1)}, bf16[384,384]{1,0:T(8,128)(2,1)S(1)}, bf16[384,384]{1,0:T(8,128)(2,1)S(1)}, bf16[384,384]{1,0:T(8,128)(2,1)S(1)}) custom-call(s32[2]{0:T(128)S(1)} %pad_add_fusion.1.place.refs_0_, bf16[128,1536]{1,0:T(8,128)(2,1)S(1)} %collective-permute-done.15.refs_1_, bf16[128,1536]{1,0:T(8,128)(2,1)S(1)} %collective-permute-done.16.refs_2_, ...), custom_call_target="tpu_custom_call" | custom-call | flops 2000000000 | bytes 10000000 | tf_op jit(solution)/shard_map/feed2/pallas_call | solution.py:38
  98.5 3.9 %collective-permute-start.19 = (bf16[384,384]{1,0:T(8,128)(2,1)S(1)}, bf16[384,384]{1,0:T(8,128)(2,1)S(1)}, u32[]{:S(2)}, u32[]{:S(2)}) collective-permute-start(bf16[384,384]{1,0:T(8,128)(2,1)S(1)} %get-tuple-element.73), channel_id=1, source_target_pairs={{0,3},{1,0},{2,1},{3,2},{4,7},{5,4},{6,5},{7,6},{8,11},{9,8},{10,9... | collective-permute-start | bytes 884744 | tf_op jit(solution)/shard_map/ppermute | solution.py:23
  103.3 3.2 %feed1.1 = (f32[128,384]{1,0:T(8,128)S(1)}, bf16[128,384]{1,0:T(8,128)(2,1)S(1)}, bf16[128,384]{1,0:T(8,128)(2,1)S(1)}, bf16[128,384]{1,0:T(8,128)(2,1)S(1)}, bf16[64,256]{1,0:T(8,128)(2,1)}) custom-call(s32[2]{0:T(128)S(1)} %pad_add_fusion.1.place.refs_0_, bf16[128,1536]{1,0:T(8,128)(2,1)S(1)} %collective-permute-done.17.refs_1_, ...), custom_call_target="tpu_custom_call" | custom-call | flops 2000000000 | bytes 10000000 | tf_op jit(solution)/shard_map/feed1/pallas_call | solution.py:38
  106.6 2.3 %collective-permute-start.20 = (bf16[128,384]{1,0:T(8,128)(2,1)S(1)}, bf16[128,384]{1,0:T(8,128)(2,1)S(1)}, u32[]{:S(2)}, u32[]{:S(2)}) collective-permute-start(bf16[128,384]{1,0:T(8,128)(2,1)S(1)} %get-tuple-element.74), channel_id=1, source_target_pairs={{0,3},{1,0},{2,1},{3,2},{4,7},{5,4},{6,5},{7,6},{8,11},{9,8},{10,9... | collective-permute-start | bytes 294920 | tf_op jit(solution)/shard_map/ppermute | solution.py:23
  108.9 2.3 %collective-permute-start.22 = (bf16[128,384]{1,0:T(8,128)(2,1)S(1)}, bf16[128,384]{1,0:T(8,128)(2,1)S(1)}, u32[]{:S(2)}, u32[]{:S(2)}) collective-permute-start(bf16[128,384]{1,0:T(8,128)(2,1)S(1)} %get-tuple-element.76), channel_id=1, source_target_pairs={{0,2},{1,3},{2,0},{3,1},{4,6},{5,7},{6,4},{7,5},{8,10},{9,11},{10,... | collective-permute-start | bytes 294920 | tf_op jit(solution)/shard_map/ppermute | solution.py:23
  111.7 2.0 %collective-permute-start.24 = (bf16[128,384]{1,0:T(8,128)(2,1)S(1)}, bf16[128,384]{1,0:T(8,128)(2,1)S(1)}, u32[]{:S(2)}, u32[]{:S(2)}) collective-permute-start(bf16[128,384]{1,0:T(8,128)(2,1)S(1)} %get-tuple-element.78), channel_id=1, source_target_pairs={{0,1},{1,2},{2,3},{3,0},{4,5},{5,6},{6,7},{7,4},{8,9},{9,10},{10,1... | collective-permute-start | bytes 294920 | tf_op jit(solution)/shard_map/ppermute | solution.py:23
  113.8 2.2 %collective-permute-done.22.refs_6_ = bf16[128,384]{1,0:T(8,128)(2,1)S(1)} collective-permute-done((bf16[128,384]{1,0:T(8,128)(2,1)S(1)}, bf16[128,384]{1,0:T(8,128)(2,1)S(1)}, u32[]{:S(2)}, u32[]{:S(2)}) %collective-permute-start.22) | collective-permute-done | bytes 98336 | tf_op jit(solution)/shard_map/ppermute | solution.py:23
  (72 shorter events, 34.8 us)
Async XLA Ops:
  0.6 13.8 %collective-permute-start.1 = (bf16[512,384]{1,0:T(8,128)(2,1)}, bf16[512,384]{1,0:T(8,128)(2,1)S(1)}, u32[]{:S(2)}, u32[]{:S(2)}) collective-permute-start(bf16[512,384]{1,0:T(8,128)(2,1)} %source.1), channel_id=1, source_target_pairs={{0,2},{1,3},{2,0},{3,1},{4,6},{5,7},{6,4},{7,5},{8,10},{9,11},{10,... | collective-permute-start | bytes 1179656 | tf_op jit(solution)/shard_map/ppermute | solution.py:23
  3.9 18.2 %collective-permute-start = (bf16[512,384]{1,0:T(8,128)(2,1)}, bf16[512,384]{1,0:T(8,128)(2,1)S(1)}, u32[]{:S(2)}, u32[]{:S(2)}) collective-permute-start(bf16[512,384]{1,0:T(8,128)(2,1)} %source.1), channel_id=1, source_target_pairs={{0,3},{1,0},{2,1},{3,2},{4,7},{5,4},{6,5},{7,6},{8,11},{9,8},{10,9... | collective-permute-start | bytes 1179656 | tf_op jit(solution)/shard_map/ppermute | solution.py:23
  5.0 17.1 %collective-permute-start.2 = (bf16[512,384]{1,0:T(8,128)(2,1)}, bf16[512,384]{1,0:T(8,128)(2,1)S(1)}, u32[]{:S(2)}, u32[]{:S(2)}) collective-permute-start(bf16[512,384]{1,0:T(8,128)(2,1)} %source.1), channel_id=1, source_target_pairs={{0,1},{1,2},{2,3},{3,0},{4,5},{5,6},{6,7},{7,4},{8,9},{9,10},{10,1... | collective-permute-start | bytes 1179656 | tf_op jit(solution)/shard_map/ppermute | solution.py:23
  23.8 5.6 %collective-permute-start.5 = (bf16[256,128]{1,0:T(8,128)(2,1)S(1)}, bf16[256,128]{1,0:T(8,128)(2,1)S(1)}, u32[]{:S(2)}, u32[]{:S(2)}) collective-permute-start(bf16[256,128]{1,0:T(8,128)(2,1)S(1)} %get-tuple-element.53.y0), channel_id=1, source_target_pairs={{0,1},{1,2},{2,3},{3,0},{4,5},{5,6},{6,7},{7,4},{8,9},{9,10},{10,1... | collective-permute-start | bytes 196616 | tf_op jit(solution)/shard_map/ppermute | solution.py:23
  25.2 6.1 %collective-permute-start.4 = (bf16[256,128]{1,0:T(8,128)(2,1)S(1)}, bf16[256,128]{1,0:T(8,128)(2,1)S(1)}, u32[]{:S(2)}, u32[]{:S(2)}) collective-permute-start(bf16[256,128]{1,0:T(8,128)(2,1)S(1)} %get-tuple-element.53.y0), channel_id=1, source_target_pairs={{0,2},{1,3},{2,0},{3,1},{4,6},{5,7},{6,4},{7,5},{8,10},{9,11},{10,... | collective-permute-start | bytes 196616 | tf_op jit(solution)/shard_map/ppermute | solution.py:23
  28.0 4.3 %collective-permute-start.3 = (bf16[256,128]{1,0:T(8,128)(2,1)S(1)}, bf16[256,128]{1,0:T(8,128)(2,1)S(1)}, u32[]{:S(2)}, u32[]{:S(2)}) collective-permute-start(bf16[256,128]{1,0:T(8,128)(2,1)S(1)} %get-tuple-element.53.y0), channel_id=1, source_target_pairs={{0,3},{1,0},{2,1},{3,2},{4,7},{5,4},{6,5},{7,6},{8,11},{9,8},{10,9... | collective-permute-start | bytes 196616 | tf_op jit(solution)/shard_map/ppermute | solution.py:23
  33.1 8.2 %collective-permute-start.6 = (bf16[512,256]{1,0:T(8,128)(2,1)S(1)}, bf16[512,256]{1,0:T(8,128)(2,1)S(1)}, u32[]{:S(2)}, u32[]{:S(2)}) collective-permute-start(bf16[512,256]{1,0:T(8,128)(2,1)S(1)} %rotate.1.rows.own), channel_id=1, source_target_pairs={{0,4},{4,0},{8,12},{12,8},{16,20},{20,16},{24,28},{28,24},{32,36},... | collective-permute-start | bytes 786440 | tf_op jit(solution)/shard_map/ppermute | solution.py:33
  33.2 10.5 %collective-permute-start.8 = (bf16[512,256]{1,0:T(8,128)(2,1)S(1)}, bf16[512,256]{1,0:T(8,128)(2,1)S(1)}, u32[]{:S(2)}, u32[]{:S(2)}) collective-permute-start(bf16[512,256]{1,0:T(8,128)(2,1)S(1)} %rotate.1.rows.own), channel_id=1, source_target_pairs={{0,4},{4,8},{8,12},{12,16},{16,20},{20,24},{24,28},{28,32},{32,36}... | collective-permute-start | bytes 786440 | tf_op jit(solution)/shard_map/ppermute | solution.py:28
  35.6 13.4 %collective-permute-start.7 = (bf16[512,256]{1,0:T(8,128)(2,1)S(1)}, bf16[512,256]{1,0:T(8,128)(2,1)S(1)}, u32[]{:S(2)}, u32[]{:S(2)}) collective-permute-start(bf16[512,256]{1,0:T(8,128)(2,1)S(1)} %rotate.1.rows.own), channel_id=1, source_target_pairs={{0,8},{4,12},{8,16},{12,20},{16,24},{20,28},{24,32},{28,36},{32,40... | collective-permute-start | bytes 786440 | tf_op jit(solution)/shard_map/ppermute | solution.py:28
  42.0 17.3 %collective-permute-start.9 = (bf16[512,256]{1,0:T(8,128)(2,1)S(1)}, bf16[512,256]{1,0:T(8,128)(2,1)S(1)}, u32[]{:S(2)}, u32[]{:S(2)}) collective-permute-start(bf16[512,256]{1,0:T(8,128)(2,1)S(1)} %get-tuple-element.54), channel_id=1, source_target_pairs={{0,32},{4,36},{8,40},{12,44},{16,48},{20,52},{24,56},{28,60},{32,0... | collective-permute-start | bytes 786440 | tf_op jit(solution)/shard_map/ppermute | solution.py:33
  50.9 16.7 %collective-permute-start.10 = (bf16[128,1536]{1,0:T(8,128)(2,1)S(1)}, bf16[128,1536]{1,0:T(8,128)(2,1)S(1)}, u32[]{:S(2)}, u32[]{:S(2)}) collective-permute-start(bf16[128,1536]{1,0:T(8,128)(2,1)S(1)} %attend1.1), channel_id=1, source_target_pairs={{0,1},{1,2},{2,3},{3,0},{4,5},{5,6},{6,7},{7,4},{8,9},{9,10},{10,1... | collective-permute-start | bytes 1179656 | tf_op jit(solution)/shard_map/ppermute | solution.py:23
  53.5 19.1 %collective-permute-start.11 = (bf16[128,1536]{1,0:T(8,128)(2,1)S(1)}, bf16[128,1536]{1,0:T(8,128)(2,1)S(1)}, u32[]{:S(2)}, u32[]{:S(2)}) collective-permute-start(bf16[128,1536]{1,0:T(8,128)(2,1)S(1)} %attend2.1), channel_id=1, source_target_pairs={{0,2},{1,3},{2,0},{3,1},{4,6},{5,7},{6,4},{7,5},{8,10},{9,11},{10,... | collective-permute-start | bytes 1179656 | tf_op jit(solution)/shard_map/ppermute | solution.py:23
  58.8 15.6 %collective-permute-start.12 = (bf16[128,1536]{1,0:T(8,128)(2,1)S(1)}, bf16[128,1536]{1,0:T(8,128)(2,1)S(1)}, u32[]{:S(2)}, u32[]{:S(2)}) collective-permute-start(bf16[128,1536]{1,0:T(8,128)(2,1)S(1)} %attend3.1), channel_id=1, source_target_pairs={{0,3},{1,0},{2,1},{3,2},{4,7},{5,4},{6,5},{7,6},{8,11},{9,8},{10,9... | collective-permute-start | bytes 1179656 | tf_op jit(solution)/shard_map/ppermute | solution.py:23
  61.3 6.3 %collective-permute-start.13 = (bf16[256,256]{1,0:T(8,128)(2,1)S(1)}, bf16[256,256]{1,0:T(8,128)(2,1)S(1)}, u32[]{:S(2)}, u32[]{:S(2)}) collective-permute-start(bf16[256,256]{1,0:T(8,128)(2,1)S(1)} %get-tuple-element.60), channel_id=1, source_target_pairs={{0,96},{4,100},{8,104},{12,108},{16,112},{20,116},{24,120},{28,124... | collective-permute-start | bytes 393224 | tf_op jit(solution)/shard_map/ppermute | solution.py:33
  74.8 12.0 %collective-permute-start.16 = (bf16[128,1536]{1,0:T(8,128)(2,1)S(1)}, bf16[128,1536]{1,0:T(8,128)(2,1)S(1)}, u32[]{:S(2)}, u32[]{:S(2)}) collective-permute-start(bf16[128,1536]{1,0:T(8,128)(2,1)S(1)} %get-tuple-element.61.refs_1_), channel_id=1, source_target_pairs={{0,1},{1,2},{2,3},{3,0},{4,5},{5,6},{6,7},{7,4},{8,9},{9,10},{10,1... | collective-permute-start | bytes 1179656 | tf_op jit(solution)/shard_map/ppermute | solution.py:23
  75.9 17.7 %collective-permute-start.15 = (bf16[128,1536]{1,0:T(8,128)(2,1)S(1)}, bf16[128,1536]{1,0:T(8,128)(2,1)S(1)}, u32[]{:S(2)}, u32[]{:S(2)}) collective-permute-start(bf16[128,1536]{1,0:T(8,128)(2,1)S(1)} %get-tuple-element.61.refs_1_), channel_id=1, source_target_pairs={{0,3},{1,0},{2,1},{3,2},{4,7},{5,4},{6,5},{7,6},{8,11},{9,8},{10,9... | collective-permute-start | bytes 1179656 | tf_op jit(solution)/shard_map/ppermute | solution.py:23
  78.1 25.2 %collective-permute-start.17 = (bf16[128,1536]{1,0:T(8,128)(2,1)S(1)}, bf16[128,1536]{1,0:T(8,128)(2,1)S(1)}, u32[]{:S(2)}, u32[]{:S(2)}) collective-permute-start(bf16[128,1536]{1,0:T(8,128)(2,1)S(1)} %get-tuple-element.61.refs_1_), channel_id=1, source_target_pairs={{0,2},{1,3},{2,0},{3,1},{4,6},{5,7},{6,4},{7,5},{8,10},{9,11},{10,... | collective-permute-start | bytes 1179656 | tf_op jit(solution)/shard_map/ppermute | solution.py:23
  85.2 18.1 %collective-permute-start.18 = (bf16[64,256]{1,0:T(8,128)(2,1)S(1)}, bf16[64,256]{1,0:T(8,128)(2,1)S(1)}, u32[]{:S(2)}, u32[]{:S(2)}) collective-permute-start(bf16[64,256]{1,0:T(8,128)(2,1)S(1)} %get-tuple-element.71), channel_id=1, source_target_pairs={{0,24},{4,28},{8,16},{12,20},{16,8},{20,12},{24,0},{28,4},{32,56},... | collective-permute-start | bytes 98312 | tf_op jit(solution)/shard_map/ppermute | solution.py:33
  98.5 19.1 %collective-permute-start.19 = (bf16[384,384]{1,0:T(8,128)(2,1)S(1)}, bf16[384,384]{1,0:T(8,128)(2,1)S(1)}, u32[]{:S(2)}, u32[]{:S(2)}) collective-permute-start(bf16[384,384]{1,0:T(8,128)(2,1)S(1)} %get-tuple-element.73), channel_id=1, source_target_pairs={{0,3},{1,0},{2,1},{3,2},{4,7},{5,4},{6,5},{7,6},{8,11},{9,8},{10,9... | collective-permute-start | bytes 884744 | tf_op jit(solution)/shard_map/ppermute | solution.py:23
  102.4 15.2 %collective-permute-start.21 = (bf16[384,384]{1,0:T(8,128)(2,1)S(1)}, bf16[384,384]{1,0:T(8,128)(2,1)S(1)}, u32[]{:S(2)}, u32[]{:S(2)}) collective-permute-start(bf16[384,384]{1,0:T(8,128)(2,1)S(1)} %get-tuple-element.75), channel_id=1, source_target_pairs={{0,2},{1,3},{2,0},{3,1},{4,6},{5,7},{6,4},{7,5},{8,10},{9,11},{10,... | collective-permute-start | bytes 884744 | tf_op jit(solution)/shard_map/ppermute | solution.py:23
  102.4 15.2 %collective-permute-start.23 = (bf16[384,384]{1,0:T(8,128)(2,1)S(1)}, bf16[384,384]{1,0:T(8,128)(2,1)S(1)}, u32[]{:S(2)}, u32[]{:S(2)}) collective-permute-start(bf16[384,384]{1,0:T(8,128)(2,1)S(1)} %get-tuple-element.77), channel_id=1, source_target_pairs={{0,1},{1,2},{2,3},{3,0},{4,5},{5,6},{6,7},{7,4},{8,9},{9,10},{10,1... | collective-permute-start | bytes 884744 | tf_op jit(solution)/shard_map/ppermute | solution.py:23
  106.6 5.1 %collective-permute-start.20 = (bf16[128,384]{1,0:T(8,128)(2,1)S(1)}, bf16[128,384]{1,0:T(8,128)(2,1)S(1)}, u32[]{:S(2)}, u32[]{:S(2)}) collective-permute-start(bf16[128,384]{1,0:T(8,128)(2,1)S(1)} %get-tuple-element.74), channel_id=1, source_target_pairs={{0,3},{1,0},{2,1},{3,2},{4,7},{5,4},{6,5},{7,6},{8,11},{9,8},{10,9... | collective-permute-start | bytes 294920 | tf_op jit(solution)/shard_map/ppermute | solution.py:23
  108.9 7.0 %collective-permute-start.22 = (bf16[128,384]{1,0:T(8,128)(2,1)S(1)}, bf16[128,384]{1,0:T(8,128)(2,1)S(1)}, u32[]{:S(2)}, u32[]{:S(2)}) collective-permute-start(bf16[128,384]{1,0:T(8,128)(2,1)S(1)} %get-tuple-element.76), channel_id=1, source_target_pairs={{0,2},{1,3},{2,0},{3,1},{4,6},{5,7},{6,4},{7,5},{8,10},{9,11},{10,... | collective-permute-start | bytes 294920 | tf_op jit(solution)/shard_map/ppermute | solution.py:23
  111.7 5.8 %collective-permute-start.24 = (bf16[128,384]{1,0:T(8,128)(2,1)S(1)}, bf16[128,384]{1,0:T(8,128)(2,1)S(1)}, u32[]{:S(2)}, u32[]{:S(2)}) collective-permute-start(bf16[128,384]{1,0:T(8,128)(2,1)S(1)} %get-tuple-element.78), channel_id=1, source_target_pairs={{0,1},{1,2},{2,3},{3,0},{4,5},{5,6},{6,7},{7,4},{8,9},{9,10},{10,1... | collective-permute-start | bytes 294920 | tf_op jit(solution)/shard_map/ppermute | solution.py:23
  (7 other events, 67.7 us)

commit v3 on v2

--- a/solution.py
+++ b/solution.py
@@ -33,7 +33,7 @@
     return lax.ppermute(block, "seq", [(i, i ^ bits) for i in range(n)])
 
 
-def run(body, outs, name, scalars, arrays, scratch=(), vmem=16 << 20):
+def run(body, outs, name, scalars, arrays, scratch=(), vmem=16 << 20, flops=2_000_000_000):
     many = isinstance(outs, (list, tuple))
     return pl.pallas_call(
         body,
@@ -42,7 +42,7 @@
         out_specs=[VM] * len(outs) if many else VM,
         scratch_shapes=list(scratch),
         compiler_params=pltpu.CompilerParams(vmem_limit_bytes=vmem),
-        cost_estimate=pl.CostEstimate(flops=2_000_000_000, transcendentals=0, bytes_accessed=10_000_000),
+        cost_estimate=pl.CostEstimate(flops=flops, transcendentals=0, bytes_accessed=flops // 200),
         name=name,
     )(*scalars, *arrays)
 
@@ -124,7 +124,7 @@
         out[rows, HD:] = v.astype(bf16)
 
 
-def attend_body(d, place, offsets, q, far, near, own, wo, *refs):
+def attend_body(d, place, offsets, q, far, far_other, own, other, wo, *refs):
     if d == 0:
         merge(refs[0], refs[1], refs[3], refs[4])
         refs = refs[2:3] + refs[5:]
@@ -133,12 +133,13 @@
     first = place[1]
     tokens = own.shape[0]
     heads = q.shape[1] // HD
-    win[pl.ds(0, tokens), :] = far[...]
-    win[pl.ds(tokens, tokens), :] = near[...]
-    win[pl.ds(2 * tokens, tokens), :] = own[...]
+    core = place[2]
+    for slot, part in ((core, far), (1 - core, far_other), (2 + core, own), (3 - core, other)):
+        win[pl.ds(pl.multiple_of(slot * tokens, tokens), tokens), :] = part[...]
     step = 128
     b = lax.rem(f + d, 4)
     row0 = pl.multiple_of(b * step, step)
+    key0 = pl.multiple_of(core * tokens + b * step, step)
     pos = first + row0 + lax.broadcasted_iota(jnp.int32, (step, 1), 0)
     begin = jnp.zeros((step, 1), jnp.int32)
     for r in range(offsets.shape[0]):
@@ -151,8 +152,8 @@
     total = None
     mixed = None
     for start, size in ((0, 512), (512, 512), (1024, 128)):
-        k = win[pl.ds(row0 + start, size), :HD]
-        v = win[pl.ds(row0 + start, size), HD:]
+        k = win[pl.ds(key0 + start, size), :HD]
+        v = win[pl.ds(key0 + start, size), HD:]
         kpos = first + row0 + (start - WIN) + lax.broadcasted_iota(jnp.int32, (heads * step, size), 1)
         allowed = kpos >= low
         if start == WIN:
@@ -188,6 +189,12 @@
         n_out[:, cols] = (res_out[g] * scale * gain[:, cols]).astype(bf16)
 
 
+def split_body(a, b, upper, lower):
+    half = upper.shape[0]
+    upper[...] = a[:half, :]
+    lower[...] = b[half:, :]
+
+
 def gelu(x):
     inner = math.sqrt(2 / math.pi) * (x + 0.044715 * (x * x * x))
     return x * (0.5 * (1.0 + jnp.tanh(inner)))
@@ -202,10 +209,8 @@
         merge(refs[0], refs[1], refs[-4], refs[-3])
         res, refs = refs[2], refs[3:-4] + refs[-2:]
     elif before:
-        earlier, refs = refs[:3], refs[3:]
-    else:
         refs[-3][...] = (refs[0][...].astype(f32) + refs[1][...].astype(f32)).astype(bf16)
-        refs = refs[2:-3] + refs[-2:]
+        earlier, refs = refs[2:5], refs[5:-3] + refs[-2:]
     wg, wu, wd, o0, o1, o2, o3, act, hold = refs
     f = place[0]
     rows, width = o0.shape
@@ -273,7 +278,7 @@
     seq_index = lax.axis_index("seq")
     f = lax.axis_index("feat")
     first = seq_index * tokens
-    place = jnp.stack([f, first]).astype(jnp.int32)
+    place = jnp.stack([f, first, seq_index % 2]).astype(jnp.int32)
     sds = jax.ShapeDtypeStruct
 
     x0 = run(copy_body, sds(hidden.shape, bf16), "take_own", [], [hidden])
@@ -359,7 +364,6 @@
         [pltpu.VMEM((4, tokens // 2, 128), f32)],
     )
     far = from_earlier(rotated, 2)
-    near = from_earlier(rotated, 1)
     sibling = from_partner(rotated, 1)
     image_sent, image_kept = run(
         image_body,
@@ -373,7 +377,8 @@
     def halves(rows):
         return [sds((rows.shape[0] // 2, 2 * HD), bf16)] * 2
 
-    queries = lax.optimization_barrier((queries, image_sent))[0]
+    far, queries, _ = lax.optimization_barrier((far, queries, image_sent))
+    far_other = from_partner(far, 1)
 
     def attend(d, kind, cached=()):
         out = sds((step, full), kind)
@@ -382,9 +387,9 @@
             [out, *halves(cached[0])] if cached else out,
             f"attend{d}",
             [place, offsets],
-            [queries, far, near, rotated, output_weight, *cached],
+            [queries, far, far_other, rotated, sibling, output_weight, *cached],
             [
-                pltpu.VMEM((3 * tokens, 2 * HD), bf16),
+                pltpu.VMEM((4 * tokens, 2 * HD), bf16),
                 pltpu.VMEM((step, query_weight.shape[1]), bf16),
             ],
         )
@@ -404,12 +409,10 @@
     landed = from_partner(go, 2)
     m1 = from_peer(normed2, 1)
     m3 = from_peer(normed2, 3)
-    m2 = from_peer(normed2, 2)
-
     hidden_units = gate_weight.shape[1]
 
     def feed(blocks, res=(), before=(), cached=()):
-        rows = step * len(blocks)
+        rows = sum(block.shape[0] for block in blocks)
         sent = rows + (step if before else 0)
         outs = [sds((rows, width), f32)] + [sds((sent, width), bf16)] * 3
         if cached:
@@ -417,7 +420,7 @@
         return run(
             functools.partial(feed_body, len(blocks), bool(res), bool(before)),
             outs,
-            f"feed{len(blocks)}" + ("own" if res else ""),
+            "feed_own" if res else "feed_near" if before else "feed_far",
             [place],
             [*blocks, *cached, *res, *before, gate_weight, up_weight, down_weight],
             [pltpu.VMEM((rows, hidden_units), bf16), pltpu.VMEM((4, rows, width), f32)],
@@ -426,9 +429,17 @@
 
     own0, *own_sent, stay, go = feed([normed2], res=[residual], cached=[stay, landed])
     landed = from_partner(go, 6)
-    both0, *early = feed([m1, m3], before=own_sent)
+    half_rows = step // 2
+    m1, m3, _ = lax.optimization_barrier((m1, m3, own0))
+    upper, lower = run(
+        split_body, [sds((half_rows, full), bf16)] * 2, "split", [], [m1, m3]
+    )
+    m1, m3, upper, lower = lax.optimization_barrier((m1, m3, upper, lower))
+    m2 = [from_peer(upper, 1), from_peer(lower, 3)]
+
+    both0, *early, cache = feed([m1, m3], before=own_sent, cached=[stay, landed])
     early = [from_peer(early[1], 2), from_peer(early[0], 3), from_peer(early[2], 1)]
-    far0, *late, cache = feed([m2], cached=[stay, landed])
+    far0, *late = feed(m2)
     late = [from_peer(late[1], 2), from_peer(late[0], 3), from_peer(late[2], 1)]
     got = [own0, both0, far0, early[2], late[2], early[0], late[0], early[1], late[1]]
     output = run(

time: 119 us -> 120 us (level)
  waiting for transfers between devices: 44.8 us -> 55.8 us
  starting transfers between devices: 39.8 us -> 29.3 us
    ppermute x18 -> x19, waiting for transfers between devices: 29.2 us -> 37.7 us  [from_peer(): lax.ppermute(block, 'feat', [(i, (i - distance) % n) for i in range(n)])]
    ppermute x18 -> x19, starting transfers between devices: 31.2 us -> 23 us  [from_peer(): lax.ppermute(block, 'feat', [(i, (i - distance) % n) for i in range(n)])]
    ppermute x2 -> x1, starting transfers between devices: 6.22 us -> 3.83 us  [from_earlier(): lax.ppermute(block, 'seq', [(i - distance, i) for i in range(distance, n)])]
    ppermute x5 -> x6, waiting for transfers between devices: 9.58 us -> 11.3 us  [from_partner(): return lax.ppermute(block, 'seq', [(i, i ^ bits) for i in range(n)])]
    ppermute x2 -> x1, waiting for transfers between devices: 6.07 us -> 6.77 us  [from_earlier(): lax.ppermute(block, 'seq', [(i - distance, i) for i in range(distance, n)])]
    pallas_call x14 -> x15, Pallas kernels: 25.6 us -> 25.8 us  [run(): pl.pallas_call(body, out_shape=outs, in_specs=[SM] * len(scalars) + [VM]...]
    ppermute x5 -> x6, starting transfers between devices: 2.39 us -> 2.4 us  [from_partner(): return lax.ppermute(block, 'seq', [(i, i ^ bits) for i in range(n)])]
  transfers between devices with their start and end apart: 25 -> 26, of which waited for: 15 -> 16; matrix products, arithmetic and copies ran while one was open for 6% -> 6% of each run, Pallas kernels for 18% -> 18%
where the time goes in v3:
time: 120 us
  waiting for transfers between devices  55.8 us (46%)
  starting transfers between devices  29.3 us (24%)
  Pallas kernels  25.8 us (22%)
  other arithmetic  4.52 us (4%)
  local copies, waits for them, and re-layouts  3.57 us (3%)
    ppermute x19, waiting for transfers between devices, from_peer(): lax.ppermute(block, 'feat', [(i, (i - distance) % n) for i in range(n)])  37.7 us
    pallas_call x15, Pallas kernels, run(): pl.pallas_call(body, out_shape=outs, in_specs=[SM] * len(scalars) + [VM]...  25.8 us
    ppermute x19, starting transfers between devices, from_peer(): lax.ppermute(block, 'feat', [(i, (i - distance) % n) for i in range(n)])  23 us
    ppermute x6, waiting for transfers between devices, from_partner(): return lax.ppermute(block, 'seq', [(i, i ^ bits) for i in range(n)])  11.3 us
    ppermute x1, waiting for transfers between devices, from_earlier(): lax.ppermute(block, 'seq', [(i - distance, i) for i in range(distance, n)])  6.77 us
    ppermute x1, starting transfers between devices, from_earlier(): lax.ppermute(block, 'seq', [(i - distance, i) for i in range(distance, n)])  3.83 us
    ppermute x6, starting transfers between devices, from_partner(): return lax.ppermute(block, 'seq', [(i, i ^ bits) for i in range(n)])  2.4 us
  transfers between devices with their start and end apart: 26, of which 16 were waited for; matrix products, arithmetic and copies ran while one was open for 6% of the time, Pallas kernels for 18%

profile of v3, /device:TPU:6, one launch (start us, length us, event | category | flops | bytes accessed | tf_op | source)
XLA Modules:
  0.0 119.9 jit_solution(4258861322293684343)
XLA Ops:
  0.6 3.1 %collective-permute-start = (bf16[512,384]{1,0:T(8,128)(2,1)}, bf16[512,384]{1,0:T(8,128)(2,1)S(1)}, u32[]{:S(2)}, u32[]{:S(2)}) collective-permute-start(bf16[512,384]{1,0:T(8,128)(2,1)} %source.1), channel_id=1, source_target_pairs={{0,3},{1,0},{2,1},{3,2},{4,7},{5,4},{6,5},{7,6},{8,11},{9,8},{10,9... | collective-permute-start | bytes 1179656 | tf_op jit(solution)/shard_map/ppermute | solution.py:23
  13.5 7.3 %collective-permute-done.x1 = bf16[512,384]{1,0:T(8,128)(2,1)S(1)} collective-permute-done((bf16[512,384]{1,0:T(8,128)(2,1)}, bf16[512,384]{1,0:T(8,128)(2,1)S(1)}, u32[]{:S(2)}, u32[]{:S(2)}) %collective-permute-start) | collective-permute-done | bytes 393248 | tf_op jit(solution)/shard_map/ppermute | solution.py:23
  20.8 3.6 %collective-permute-done.2.x3 = bf16[512,384]{1,0:T(8,128)(2,1)S(1)} collective-permute-done((bf16[512,384]{1,0:T(8,128)(2,1)}, bf16[512,384]{1,0:T(8,128)(2,1)S(1)}, u32[]{:S(2)}, u32[]{:S(2)}) %collective-permute-start.2) | collective-permute-done | bytes 393248 | tf_op jit(solution)/shard_map/ppermute | solution.py:23
  28.3 2.7 %collective-permute-done.3.y1 = bf16[256,128]{1,0:T(8,128)(2,1)S(1)} collective-permute-done((bf16[256,128]{1,0:T(8,128)(2,1)S(1)}, bf16[256,128]{1,0:T(8,128)(2,1)S(1)}, u32[]{:S(2)}, u32[]{:S(2)}) %collective-permute-start.3) | collective-permute-done | bytes 65568 | tf_op jit(solution)/shard_map/ppermute | solution.py:23
  30.9 1.9 %collective-permute-done.4.y2 = bf16[256,128]{1,0:T(8,128)(2,1)S(1)} collective-permute-done((bf16[256,128]{1,0:T(8,128)(2,1)S(1)}, bf16[256,128]{1,0:T(8,128)(2,1)S(1)}, u32[]{:S(2)}, u32[]{:S(2)}) %collective-permute-start.4) | collective-permute-done | bytes 65568 | tf_op jit(solution)/shard_map/ppermute | solution.py:23
  34.3 3.8 %collective-permute-start.6 = (bf16[512,256]{1,0:T(8,128)(2,1)S(1)}, bf16[512,256]{1,0:T(8,128)(2,1)S(1)}, u32[]{:S(2)}, u32[]{:S(2)}) collective-permute-start(bf16[512,256]{1,0:T(8,128)(2,1)S(1)} %rotate.1.rows.own), channel_id=1, source_target_pairs={{0,8},{4,12},{8,16},{12,20},{16,24},{20,28},{24,32},{28,36},{32,40... | collective-permute-start | bytes 786440 | tf_op jit(solution)/shard_map/ppermute | solution.py:28
  40.7 6.8 %collective-permute-done.6.far = bf16[512,256]{1,0:T(8,128)(2,1)S(1)} collective-permute-done((bf16[512,256]{1,0:T(8,128)(2,1)S(1)}, bf16[512,256]{1,0:T(8,128)(2,1)S(1)}, u32[]{:S(2)}, u32[]{:S(2)}) %collective-permute-start.6) | collective-permute-done | bytes 262176 | tf_op jit(solution)/shard_map/ppermute | solution.py:28
  49.0 1.9 %attend1.1 = bf16[128,1536]{1,0:T(8,128)(2,1)S(1)} custom-call(s32[3]{0:T(128)S(1)} %pad_add_fusion.1.place.refs_0_, s32[8]{0:T(128)S(1)} %bitcast_subtract_fusion.offsets, bf16[512,384]{1,0:T(8,128)(2,1)S(1)} %queries.1.q, bf16[512,256]{1,0:T(8,128)(2,1)S(1)} %collective-permute-done.6.far, bf16[512,256]{1,0:T(8,128)(2,1)S(1)} %collective-permute-done.8.far_other, ...), custom_call_target="tpu_custom_call" | custom-call | flops 2000000000 | bytes 10000000 | tf_op jit(solution)/shard_map/attend1/pallas_call | solution.py:38
  51.7 1.9 %attend2.1 = bf16[128,1536]{1,0:T(8,128)(2,1)S(1)} custom-call(s32[3]{0:T(128)S(1)} %pad_add_fusion.1.place.refs_0_, s32[8]{0:T(128)S(1)} %bitcast_subtract_fusion.offsets, bf16[512,384]{1,0:T(8,128)(2,1)S(1)} %queries.1.q, bf16[512,256]{1,0:T(8,128)(2,1)S(1)} %collective-permute-done.6.far, bf16[512,256]{1,0:T(8,128)(2,1)S(1)} %collective-permute-done.8.far_other, ...), custom_call_target="tpu_custom_call" | custom-call | flops 2000000000 | bytes 10000000 | tf_op jit(solution)/shard_map/attend2/pallas_call | solution.py:38
  53.6 2.7 %collective-permute-start.11 = (bf16[128,1536]{1,0:T(8,128)(2,1)S(1)}, bf16[128,1536]{1,0:T(8,128)(2,1)S(1)}, u32[]{:S(2)}, u32[]{:S(2)}) collective-permute-start(bf16[128,1536]{1,0:T(8,128)(2,1)S(1)} %attend2.1), channel_id=1, source_target_pairs={{0,2},{1,3},{2,0},{3,1},{4,6},{5,7},{6,4},{7,5},{8,10},{9,11},{10,... | collective-permute-start | bytes 1179656 | tf_op jit(solution)/shard_map/ppermute | solution.py:23
  59.1 2.0 %attend0.1 = (f32[128,1536]{1,0:T(8,128)S(1)}, bf16[256,256]{1,0:T(8,128)(2,1)S(1)}, bf16[256,256]{1,0:T(8,128)(2,1)S(1)}) custom-call(s32[3]{0:T(128)S(1)} %pad_add_fusion.1.place.refs_0_, s32[8]{0:T(128)S(1)} %bitcast_subtract_fusion.offsets, bf16[512,384]{1,0:T(8,128)(2,1)S(1)} %queries.1.q, bf16[512,256]{1,0:T(8,128)(2,1)S(1)} %collective-permute-done.6.far, ...), custom_call_target="tpu_custom_call" | custom-call | flops 2000000000 | bytes 10000000 | tf_op jit(solution)/shard_map/attend0/pallas_call | solution.py:38
  61.3 6.0 %collective-permute-done.13.landed = bf16[256,256]{1,0:T(8,128)(2,1)S(1)} collective-permute-done((bf16[256,256]{1,0:T(8,128)(2,1)S(1)}, bf16[256,256]{1,0:T(8,128)(2,1)S(1)}, u32[]{:S(2)}, u32[]{:S(2)}) %collective-permute-start.13) | collective-permute-done | bytes 131104 | tf_op jit(solution)/shard_map/ppermute | solution.py:33
  67.3 4.6 %collective-permute-done.11.p2 = bf16[128,1536]{1,0:T(8,128)(2,1)S(1)} collective-permute-done((bf16[128,1536]{1,0:T(8,128)(2,1)S(1)}, bf16[128,1536]{1,0:T(8,128)(2,1)S(1)}, u32[]{:S(2)}, u32[]{:S(2)}) %collective-permute-start.11) | collective-permute-done | bytes 393248 | tf_op jit(solution)/shard_map/ppermute | solution.py:23
  71.9 2.5 %collective-permute-done.12.p3 = bf16[128,1536]{1,0:T(8,128)(2,1)S(1)} collective-permute-done((bf16[128,1536]{1,0:T(8,128)(2,1)S(1)}, bf16[128,1536]{1,0:T(8,128)(2,1)S(1)}, u32[]{:S(2)}, u32[]{:S(2)}) %collective-permute-start.12) | collective-permute-done | bytes 393248 | tf_op jit(solution)/shard_map/ppermute | solution.py:23
  74.8 2.7 %collective-permute-start.15 = (bf16[128,1536]{1,0:T(8,128)(2,1)S(1)}, bf16[128,1536]{1,0:T(8,128)(2,1)S(1)}, u32[]{:S(2)}, u32[]{:S(2)}) collective-permute-start(bf16[128,1536]{1,0:T(8,128)(2,1)S(1)} %get-tuple-element.71.refs_1_), channel_id=1, source_target_pairs={{0,3},{1,0},{2,1},{3,2},{4,7},{5,4},{6,5},{7,6},{8,11},{9,8},{10,9... | collective-permute-start | bytes 1179656 | tf_op jit(solution)/shard_map/ppermute | solution.py:23
  77.5 4.3 %collective-permute-done.14.refs_3_ = bf16[128,256]{1,0:T(8,128)(2,1)S(1)} collective-permute-done((bf16[128,256]{1,0:T(8,128)(2,1)S(1)}, bf16[128,256]{1,0:T(8,128)(2,1)S(1)}, u32[]{:S(2)}, u32[]{:S(2)}) %collective-permute-start.14) | collective-permute-done | bytes 65568 | tf_op jit(solution)/shard_map/ppermute | solution.py:33
  81.8 2.8 %feed_own.1 = (f32[128,384]{1,0:T(8,128)S(1)}, bf16[128,384]{1,0:T(8,128)(2,1)S(1)}, bf16[128,384]{1,0:T(8,128)(2,1)S(1)}, bf16[128,384]{1,0:T(8,128)(2,1)S(1)},...) custom-call(s32[3]{0:T(128)S(1)} %pad_add_fusion.1.place.refs_0_, ...), custom_call_target="tpu_custom_call" | custom-call | flops 2000000000 | bytes 10000000 | tf_op jit(solution)/shard_map/feed_own/pallas_call | solution.py:38
  86.2 3.3 %collective-permute-done.16.b.refs_2_ = bf16[128,1536]{1,0:T(8,128)(2,1)S(1)} collective-permute-done((bf16[128,1536]{1,0:T(8,128)(2,1)S(1)}, bf16[128,1536]{1,0:T(8,128)(2,1)S(1)}, u32[]{:S(2)}, u32[]{:S(2)}) %collective-permute-start.16) | collective-permute-done | bytes 393248 | tf_op jit(solution)/shard_map/ppermute | solution.py:23
  91.6 5.4 %feed_near.1 = (f32[256,384]{1,0:T(8,128)S(1)}, bf16[384,384]{1,0:T(8,128)(2,1)S(1)}, bf16[384,384]{1,0:T(8,128)(2,1)S(1)}, bf16[384,384]{1,0:T(8,128)(2,1)S(1)}, bf16[64,256]{1,0:T(8,128)(2,1)}) custom-call(s32[3]{0:T(128)S(1)} %pad_add_fusion.1.place.refs_0_, bf16[128,1536]{1,0:T(8,128)(2,1)S(1)} %collective-permute-done.15.a.refs_1_, ...), custom_call_target="tpu_custom_call" | custom-call | flops 2000000000 | bytes 10000000 | tf_op jit(solution)/shard_map/feed_near/pallas_call | solution.py:38
  99.4 2.8 %feed_far.1 = (f32[128,384]{1,0:T(8,128)S(1)}, bf16[128,384]{1,0:T(8,128)(2,1)S(1)}, bf16[128,384]{1,0:T(8,128)(2,1)S(1)}, bf16[128,384]{1,0:T(8,128)(2,1)S(1)}) custom-call(s32[3]{0:T(128)S(1)} %pad_add_fusion.1.place.refs_0_, bf16[64,1536]{1,0:T(8,128)(2,1)S(1)} %collective-permute-done.18.refs_1_, bf16[64,1536]{1,0:T(8,128)(2,1)S(1)} %collective-permute-done.19.refs_2_, ...), custom_call_target="tpu_custom_call" | custom-call | flops 2000000000 | bytes 10000000 | tf_op jit(solution)/shard_map/feed_far/pallas_call | solution.py:38
  102.2 3.0 %collective-permute-start.21 = (bf16[128,384]{1,0:T(8,128)(2,1)S(1)}, bf16[128,384]{1,0:T(8,128)(2,1)S(1)}, u32[]{:S(2)}, u32[]{:S(2)}) collective-permute-start(bf16[128,384]{1,0:T(8,128)(2,1)S(1)} %get-tuple-element.92), channel_id=1, source_target_pairs={{0,3},{1,0},{2,1},{3,2},{4,7},{5,4},{6,5},{7,6},{8,11},{9,8},{10,9... | collective-permute-start | bytes 294920 | tf_op jit(solution)/shard_map/ppermute | solution.py:23
  107.0 5.1 %collective-permute-done.20.refs_3_ = bf16[384,384]{1,0:T(8,128)(2,1)S(1)} collective-permute-done((bf16[384,384]{1,0:T(8,128)(2,1)S(1)}, bf16[384,384]{1,0:T(8,128)(2,1)S(1)}, u32[]{:S(2)}, u32[]{:S(2)}) %collective-permute-start.20) | collective-permute-done | bytes 294944 | tf_op jit(solution)/shard_map/ppermute | solution.py:23
  112.0 2.7 %collective-permute-done.24.refs_7_ = bf16[384,384]{1,0:T(8,128)(2,1)S(1)} collective-permute-done((bf16[384,384]{1,0:T(8,128)(2,1)S(1)}, bf16[384,384]{1,0:T(8,128)(2,1)S(1)}, u32[]{:S(2)}, u32[]{:S(2)}) %collective-permute-start.24) | collective-permute-done | bytes 294944 | tf_op jit(solution)/shard_map/ppermute | solution.py:23
  114.8 2.1 %collective-permute-done.23.refs_6_ = bf16[128,384]{1,0:T(8,128)(2,1)S(1)} collective-permute-done((bf16[128,384]{1,0:T(8,128)(2,1)S(1)}, bf16[128,384]{1,0:T(8,128)(2,1)S(1)}, u32[]{:S(2)}, u32[]{:S(2)}) %collective-permute-start.23) | collective-permute-done | bytes 98336 | tf_op jit(solution)/shard_map/ppermute | solution.py:23
  (75 shorter events, 34.1 us)
Async XLA Ops:
  0.6 20.2 %collective-permute-start = (bf16[512,384]{1,0:T(8,128)(2,1)}, bf16[512,384]{1,0:T(8,128)(2,1)S(1)}, u32[]{:S(2)}, u32[]{:S(2)}) collective-permute-start(bf16[512,384]{1,0:T(8,128)(2,1)} %source.1), channel_id=1, source_target_pairs={{0,3},{1,0},{2,1},{3,2},{4,7},{5,4},{6,5},{7,6},{8,11},{9,8},{10,9... | collective-permute-start | bytes 1179656 | tf_op jit(solution)/shard_map/ppermute | solution.py:23
  3.7 17.1 %collective-permute-start.1 = (bf16[512,384]{1,0:T(8,128)(2,1)}, bf16[512,384]{1,0:T(8,128)(2,1)S(1)}, u32[]{:S(2)}, u32[]{:S(2)}) collective-permute-start(bf16[512,384]{1,0:T(8,128)(2,1)} %source.1), channel_id=1, source_target_pairs={{0,2},{1,3},{2,0},{3,1},{4,6},{5,7},{6,4},{7,5},{8,10},{9,11},{10,... | collective-permute-start | bytes 1179656 | tf_op jit(solution)/shard_map/ppermute | solution.py:23
  4.3 20.1 %collective-permute-start.2 = (bf16[512,384]{1,0:T(8,128)(2,1)}, bf16[512,384]{1,0:T(8,128)(2,1)S(1)}, u32[]{:S(2)}, u32[]{:S(2)}) collective-permute-start(bf16[512,384]{1,0:T(8,128)(2,1)} %source.1), channel_id=1, source_target_pairs={{0,1},{1,2},{2,3},{3,0},{4,5},{5,6},{6,7},{7,4},{8,9},{9,10},{10,1... | collective-permute-start | bytes 1179656 | tf_op jit(solution)/shard_map/ppermute | solution.py:23
  26.2 4.8 %collective-permute-start.3 = (bf16[256,128]{1,0:T(8,128)(2,1)S(1)}, bf16[256,128]{1,0:T(8,128)(2,1)S(1)}, u32[]{:S(2)}, u32[]{:S(2)}) collective-permute-start(bf16[256,128]{1,0:T(8,128)(2,1)S(1)} %get-tuple-element.57.y0), channel_id=1, source_target_pairs={{0,3},{1,0},{2,1},{3,2},{4,7},{5,4},{6,5},{7,6},{8,11},{9,8},{10,9... | collective-permute-start | bytes 196616 | tf_op jit(solution)/shard_map/ppermute | solution.py:23
  26.8 6.0 %collective-permute-start.4 = (bf16[256,128]{1,0:T(8,128)(2,1)S(1)}, bf16[256,128]{1,0:T(8,128)(2,1)S(1)}, u32[]{:S(2)}, u32[]{:S(2)}) collective-permute-start(bf16[256,128]{1,0:T(8,128)(2,1)S(1)} %get-tuple-element.57.y0), channel_id=1, source_target_pairs={{0,2},{1,3},{2,0},{3,1},{4,6},{5,7},{6,4},{7,5},{8,10},{9,11},{10,... | collective-permute-start | bytes 196616 | tf_op jit(solution)/shard_map/ppermute | solution.py:23
  27.5 5.9 %collective-permute-start.5 = (bf16[256,128]{1,0:T(8,128)(2,1)S(1)}, bf16[256,128]{1,0:T(8,128)(2,1)S(1)}, u32[]{:S(2)}, u32[]{:S(2)}) collective-permute-start(bf16[256,128]{1,0:T(8,128)(2,1)S(1)} %get-tuple-element.57.y0), channel_id=1, source_target_pairs={{0,1},{1,2},{2,3},{3,0},{4,5},{5,6},{6,7},{7,4},{8,9},{9,10},{10,1... | collective-permute-start | bytes 196616 | tf_op jit(solution)/shard_map/ppermute | solution.py:23
  34.2 5.8 %collective-permute-start.7 = (bf16[512,256]{1,0:T(8,128)(2,1)S(1)}, bf16[512,256]{1,0:T(8,128)(2,1)S(1)}, u32[]{:S(2)}, u32[]{:S(2)}) collective-permute-start(bf16[512,256]{1,0:T(8,128)(2,1)S(1)} %rotate.1.rows.own), channel_id=1, source_target_pairs={{0,4},{4,0},{8,12},{12,8},{16,20},{20,16},{24,28},{28,24},{32,36},... | collective-permute-start | bytes 786440 | tf_op jit(solution)/shard_map/ppermute | solution.py:33
  34.3 13.2 %collective-permute-start.6 = (bf16[512,256]{1,0:T(8,128)(2,1)S(1)}, bf16[512,256]{1,0:T(8,128)(2,1)S(1)}, u32[]{:S(2)}, u32[]{:S(2)}) collective-permute-start(bf16[512,256]{1,0:T(8,128)(2,1)S(1)} %rotate.1.rows.own), channel_id=1, source_target_pairs={{0,8},{4,12},{8,16},{12,20},{16,24},{20,28},{24,32},{28,36},{32,40... | collective-permute-start | bytes 786440 | tf_op jit(solution)/shard_map/ppermute | solution.py:28
  47.5 11.6 %collective-permute-start.9 = (bf16[512,256]{1,0:T(8,128)(2,1)S(1)}, bf16[512,256]{1,0:T(8,128)(2,1)S(1)}, u32[]{:S(2)}, u32[]{:S(2)}) collective-permute-start(bf16[512,256]{1,0:T(8,128)(2,1)S(1)} %get-tuple-element.63), channel_id=1, source_target_pairs={{0,32},{4,36},{8,40},{12,44},{16,48},{20,52},{24,56},{28,60},{32,0... | collective-permute-start | bytes 786440 | tf_op jit(solution)/shard_map/ppermute | solution.py:33
  50.9 16.4 %collective-permute-start.10 = (bf16[128,1536]{1,0:T(8,128)(2,1)S(1)}, bf16[128,1536]{1,0:T(8,128)(2,1)S(1)}, u32[]{:S(2)}, u32[]{:S(2)}) collective-permute-start(bf16[128,1536]{1,0:T(8,128)(2,1)S(1)} %attend1.1), channel_id=1, source_target_pairs={{0,1},{1,2},{2,3},{3,0},{4,5},{5,6},{6,7},{7,4},{8,9},{9,10},{10,1... | collective-permute-start | bytes 1179656 | tf_op jit(solution)/shard_map/ppermute | solution.py:23
  53.6 18.3 %collective-permute-start.11 = (bf16[128,1536]{1,0:T(8,128)(2,1)S(1)}, bf16[128,1536]{1,0:T(8,128)(2,1)S(1)}, u32[]{:S(2)}, u32[]{:S(2)}) collective-permute-start(bf16[128,1536]{1,0:T(8,128)(2,1)S(1)} %attend2.1), channel_id=1, source_target_pairs={{0,2},{1,3},{2,0},{3,1},{4,6},{5,7},{6,4},{7,5},{8,10},{9,11},{10,... | collective-permute-start | bytes 1179656 | tf_op jit(solution)/shard_map/ppermute | solution.py:23
  58.2 16.2 %collective-permute-start.12 = (bf16[128,1536]{1,0:T(8,128)(2,1)S(1)}, bf16[128,1536]{1,0:T(8,128)(2,1)S(1)}, u32[]{:S(2)}, u32[]{:S(2)}) collective-permute-start(bf16[128,1536]{1,0:T(8,128)(2,1)S(1)} %attend3.1), channel_id=1, source_target_pairs={{0,3},{1,0},{2,1},{3,2},{4,7},{5,4},{6,5},{7,6},{8,11},{9,8},{10,9... | collective-permute-start | bytes 1179656 | tf_op jit(solution)/shard_map/ppermute | solution.py:23
  61.0 6.3 %collective-permute-start.13 = (bf16[256,256]{1,0:T(8,128)(2,1)S(1)}, bf16[256,256]{1,0:T(8,128)(2,1)S(1)}, u32[]{:S(2)}, u32[]{:S(2)}) collective-permute-start(bf16[256,256]{1,0:T(8,128)(2,1)S(1)} %get-tuple-element.70), channel_id=1, source_target_pairs={{0,96},{4,100},{8,104},{12,108},{16,112},{20,116},{24,120},{28,124... | collective-permute-start | bytes 393224 | tf_op jit(solution)/shard_map/ppermute | solution.py:33
  74.8 11.3 %collective-permute-start.15 = (bf16[128,1536]{1,0:T(8,128)(2,1)S(1)}, bf16[128,1536]{1,0:T(8,128)(2,1)S(1)}, u32[]{:S(2)}, u32[]{:S(2)}) collective-permute-start(bf16[128,1536]{1,0:T(8,128)(2,1)S(1)} %get-tuple-element.71.refs_1_), channel_id=1, source_target_pairs={{0,3},{1,0},{2,1},{3,2},{4,7},{5,4},{6,5},{7,6},{8,11},{9,8},{10,9... | collective-permute-start | bytes 1179656 | tf_op jit(solution)/shard_map/ppermute | solution.py:23
  77.5 12.0 %collective-permute-start.16 = (bf16[128,1536]{1,0:T(8,128)(2,1)S(1)}, bf16[128,1536]{1,0:T(8,128)(2,1)S(1)}, u32[]{:S(2)}, u32[]{:S(2)}) collective-permute-start(bf16[128,1536]{1,0:T(8,128)(2,1)S(1)} %get-tuple-element.71.refs_1_), channel_id=1, source_target_pairs={{0,1},{1,2},{2,3},{3,0},{4,5},{5,6},{6,7},{7,4},{8,9},{9,10},{10,1... | collective-permute-start | bytes 1179656 | tf_op jit(solution)/shard_map/ppermute | solution.py:23
  84.6 7.0 %collective-permute-start.17 = (bf16[64,256]{1,0:T(8,128)(2,1)S(1)}, bf16[64,256]{1,0:T(8,128)(2,1)S(1)}, u32[]{:S(2)}, u32[]{:S(2)}) collective-permute-start(bf16[64,256]{1,0:T(8,128)(2,1)S(1)} %get-tuple-element.83), channel_id=1, source_target_pairs={{0,24},{4,28},{8,16},{12,20},{16,8},{20,12},{24,0},{28,4},{32,56},... | collective-permute-start | bytes 98312 | tf_op jit(solution)/shard_map/ppermute | solution.py:33
  89.5 9.9 %collective-permute-start.18 = (bf16[64,1536]{1,0:T(8,128)(2,1)S(1)}, bf16[64,1536]{1,0:T(8,128)(2,1)S(1)}, u32[]{:S(2)}, u32[]{:S(2)}) collective-permute-start(bf16[64,1536]{1,0:T(8,128)(2,1)S(1)} %get-tuple-element.88), channel_id=1, source_target_pairs={{0,3},{1,0},{2,1},{3,2},{4,7},{5,4},{6,5},{7,6},{8,11},{9,8},{10,9... | collective-permute-start | bytes 589832 | tf_op jit(solution)/shard_map/ppermute | solution.py:23
  89.9 9.5 %collective-permute-start.19 = (bf16[64,1536]{1,0:T(8,128)(2,1)S(1)}, bf16[64,1536]{1,0:T(8,128)(2,1)S(1)}, u32[]{:S(2)}, u32[]{:S(2)}) collective-permute-start(bf16[64,1536]{1,0:T(8,128)(2,1)S(1)} %get-tuple-element.89), channel_id=1, source_target_pairs={{0,1},{1,2},{2,3},{3,0},{4,5},{5,6},{6,7},{7,4},{8,9},{9,10},{10,1... | collective-permute-start | bytes 589832 | tf_op jit(solution)/shard_map/ppermute | solution.py:23
  97.0 15.0 %collective-permute-start.20 = (bf16[384,384]{1,0:T(8,128)(2,1)S(1)}, bf16[384,384]{1,0:T(8,128)(2,1)S(1)}, u32[]{:S(2)}, u32[]{:S(2)}) collective-permute-start(bf16[384,384]{1,0:T(8,128)(2,1)S(1)} %get-tuple-element.91), channel_id=1, source_target_pairs={{0,3},{1,0},{2,1},{3,2},{4,7},{5,4},{6,5},{7,6},{8,11},{9,8},{10,9... | collective-permute-start | bytes 884744 | tf_op jit(solution)/shard_map/ppermute | solution.py:23
  98.5 13.5 %collective-permute-start.22 = (bf16[384,384]{1,0:T(8,128)(2,1)S(1)}, bf16[384,384]{1,0:T(8,128)(2,1)S(1)}, u32[]{:S(2)}, u32[]{:S(2)}) collective-permute-start(bf16[384,384]{1,0:T(8,128)(2,1)S(1)} %get-tuple-element.93), channel_id=1, source_target_pairs={{0,2},{1,3},{2,0},{3,1},{4,6},{5,7},{6,4},{7,5},{8,10},{9,11},{10,... | collective-permute-start | bytes 884744 | tf_op jit(solution)/shard_map/ppermute | solution.py:23
  99.1 15.6 %collective-permute-start.24 = (bf16[384,384]{1,0:T(8,128)(2,1)S(1)}, bf16[384,384]{1,0:T(8,128)(2,1)S(1)}, u32[]{:S(2)}, u32[]{:S(2)}) collective-permute-start(bf16[384,384]{1,0:T(8,128)(2,1)S(1)} %get-tuple-element.95), channel_id=1, source_target_pairs={{0,1},{1,2},{2,3},{3,0},{4,5},{5,6},{6,7},{7,4},{8,9},{9,10},{10,1... | collective-permute-start | bytes 884744 | tf_op jit(solution)/shard_map/ppermute | solution.py:23
  102.2 12.6 %collective-permute-start.21 = (bf16[128,384]{1,0:T(8,128)(2,1)S(1)}, bf16[128,384]{1,0:T(8,128)(2,1)S(1)}, u32[]{:S(2)}, u32[]{:S(2)}) collective-permute-start(bf16[128,384]{1,0:T(8,128)(2,1)S(1)} %get-tuple-element.92), channel_id=1, source_target_pairs={{0,3},{1,0},{2,1},{3,2},{4,7},{5,4},{6,5},{7,6},{8,11},{9,8},{10,9... | collective-permute-start | bytes 294920 | tf_op jit(solution)/shard_map/ppermute | solution.py:23
  105.2 11.6 %collective-permute-start.23 = (bf16[128,384]{1,0:T(8,128)(2,1)S(1)}, bf16[128,384]{1,0:T(8,128)(2,1)S(1)}, u32[]{:S(2)}, u32[]{:S(2)}) collective-permute-start(bf16[128,384]{1,0:T(8,128)(2,1)S(1)} %get-tuple-element.94), channel_id=1, source_target_pairs={{0,2},{1,3},{2,0},{3,1},{4,6},{5,7},{6,4},{7,5},{8,10},{9,11},{10,... | collective-permute-start | bytes 294920 | tf_op jit(solution)/shard_map/ppermute | solution.py:23
  112.0 6.3 %collective-permute-start.25 = (bf16[128,384]{1,0:T(8,128)(2,1)S(1)}, bf16[128,384]{1,0:T(8,128)(2,1)S(1)}, u32[]{:S(2)}, u32[]{:S(2)}) collective-permute-start(bf16[128,384]{1,0:T(8,128)(2,1)S(1)} %get-tuple-element.96), channel_id=1, source_target_pairs={{0,1},{1,2},{2,3},{3,0},{4,5},{5,6},{6,7},{7,4},{8,9},{9,10},{10,1... | collective-permute-start | bytes 294920 | tf_op jit(solution)/shard_map/ppermute | solution.py:23
  (8 other events, 65.4 us)

commit v4 on v3

--- a/solution.py
+++ b/solution.py
@@ -102,40 +102,49 @@
         start = pl.multiple_of(g * width, 128)
         part = dot(n_in[d], wq[pl.ds(start, width), :])
         acc = part if acc is None else acc + part
-    c = cosine[...]
-    s = sine[...]
+    factor = HD**-0.5 * math.log2(math.e)
+    c = cosine[: acc.shape[0], :] * factor
+    s = sine[: acc.shape[0], :] * factor
     for h in range(acc.shape[1] // HD):
         v = acc[:, h * HD : (h + 1) * HD]
         q_out[:, h * HD : (h + 1) * HD] = (v * c + pltpu.roll(v, HD // 2, 1) * s).astype(bf16)
 
 
+def join_body(a, b, out):
+    half = a.shape[0]
+    out[:half, :] = a[...]
+    out[half:, :] = b[...]
+
+
 def rotate_body(place, y0, y1, y2, y3, cosine, sine, out, hold):
     f = place[0]
-    half = y0.shape[0]
     for d, y in enumerate((y0, y1, y2, y3)):
         hold[lax.rem(f + d, 4)] = y[...].astype(f32)
-    for part in range(2):
-        rows = pl.ds(part * half, half)
-        lanes = slice(part * 64, part * 64 + 64)
-        k = jnp.concatenate([hold[0][:, lanes], hold[1][:, lanes]], axis=1)
-        v = jnp.concatenate([hold[2][:, lanes], hold[3][:, lanes]], axis=1)
+    quarter = y0.shape[0] // 2
+    for block in range(4):
+        source = slice(block // 2 * quarter, block // 2 * quarter + quarter)
+        lanes = slice(block % 2 * 64, block % 2 * 64 + 64)
+        rows = pl.ds(block * quarter, quarter)
+        k = jnp.concatenate([hold[0, source, lanes], hold[1, source, lanes]], axis=1)
+        v = jnp.concatenate([hold[2, source, lanes], hold[3, source, lanes]], axis=1)
         k = k * cosine[rows, :] + pltpu.roll(k, HD // 2, 1) * sine[rows, :]
         out[rows, :HD] = k.astype(bf16)
         out[rows, HD:] = v.astype(bf16)
 
 
-def attend_body(d, place, offsets, q, far, far_other, own, other, wo, *refs):
+def attend_body(d, place, offsets, q, mine, theirs, wo, *refs):
     if d == 0:
         merge(refs[0], refs[1], refs[3], refs[4])
         refs = refs[2:3] + refs[5:]
     out, win, att = refs
     f = place[0]
     first = place[1]
-    tokens = own.shape[0]
+    tokens = q.shape[0]
     heads = q.shape[1] // HD
     core = place[2]
-    for slot, part in ((core, far), (1 - core, far_other), (2 + core, own), (3 - core, other)):
-        win[pl.ds(pl.multiple_of(slot * tokens, tokens), tokens), :] = part[...]
+    for slot, part, row in ((core, mine, 1), (1 - core, theirs, 1), (2 + core, mine, 0), (3 - core, theirs, 0)):
+        rows = pl.ds(pl.multiple_of(slot * tokens, tokens), tokens)
+        win[rows, :] = part[row * tokens : (row + 1) * tokens, :]
     step = 128
     b = lax.rem(f + d, 4)
     row0 = pl.multiple_of(b * step, step)
@@ -148,7 +157,6 @@
     low = jnp.concatenate([low] * heads, axis=0)
     high = jnp.concatenate([pos] * heads, axis=0)
     qs = jnp.concatenate([q[pl.ds(row0, step), h * HD : (h + 1) * HD] for h in range(heads)], axis=0)
-    factor = HD**-0.5 * math.log2(math.e)
     total = None
     mixed = None
     for start, size in ((0, 512), (512, 512), (1024, 128)):
@@ -159,7 +167,7 @@
         if start == WIN:
             allowed = allowed & (kpos <= high)
         s = lax.dot_general(qs, k, (((1,), (1,)), ((), ())), preferred_element_type=f32)
-        p = jnp.where(allowed, jnp.exp2(s * factor), 0.0)
+        p = jnp.where(allowed, jnp.exp2(s), 0.0)
         part = jnp.sum(p, axis=1, keepdims=True)
         total = part if total is None else total + part
         part = dot(p.astype(bf16), v)
@@ -215,13 +223,15 @@
     f = place[0]
     rows, width = o0.shape
     n = jnp.concatenate([r[...] for r in blocks], axis=0) if count > 1 else blocks[0][...]
-    chunk = 384
-    for c in range(wg.shape[1] // chunk):
-        cols = slice(c * chunk, (c + 1) * chunk)
+    chunk = 512
+    for c in range(0, wg.shape[1], chunk):
+        cols = slice(c, min(c + chunk, wg.shape[1]))
         act[:, cols] = (gelu(dot(n, wg[:, cols])) * dot(n, wu[:, cols])).astype(bf16)
-    for g in range(4):
-        part = dot(act[...], wd[:, g * width : (g + 1) * width])
-        hold[g] = part + res[g] if own else part
+    for g in (0, 2):
+        pair = dot(act[...], wd[:, g * width : (g + 2) * width])
+        for h in (0, 1):
+            part = pair[:, h * width : (h + 1) * width]
+            hold[g + h] = part + res[g + h] if own else part
     o0[...] = hold[f]
     for d, o in ((1, o1), (2, o2), (3, o3)):
         lead = o.shape[0] - rows
@@ -231,23 +241,23 @@
 
 
 def finish_body(place, *refs):
-    ins, out, hold = refs[:-2], refs[-2], refs[-1]
-    f = place[0]
-    step = hold.shape[1]
+    ins, out = refs[:-1], refs[-1]
+    f = place[0]
+    step = out.shape[0] // 4
     own, both, far = ins[:3]
-    hold[f] = own[...]
-    hold[lax.rem(f + 1, 4)] = both[:step]
-    hold[lax.rem(f + 3, 4)] = both[step:]
-    hold[lax.rem(f + 2, 4)] = far[...]
-    for e in range(1, 4):
-        early, far = ins[2 * e + 1 : 2 * e + 3]
-        for row, shift in ((0, 0), (1, 1), (2, 3)):
-            b = lax.rem(f + e + shift, 4)
-            hold[b] = hold[b] + early[row * step : (row + 1) * step].astype(f32)
-        b = lax.rem(f + e + 2, 4)
-        hold[b] = hold[b] + far[...].astype(f32)
-    for b in range(4):
-        out[b * step : (b + 1) * step, :] = hold[b].astype(bf16)
+    for r in range(4):
+        total = (own[...], both[:step], far[...], both[step:])[r]
+        for e in range(1, 4):
+            early, late = ins[2 * e + 1 : 2 * e + 3]
+            shift = (r - e) % 4
+            if shift == 2:
+                piece = late[...]
+            else:
+                row = (0, 1, None, 2)[shift] * step
+                piece = early[row : row + step]
+            total = total + piece.astype(f32)
+        rows = pl.ds(pl.multiple_of(lax.rem(f + r, 4) * step, step), step)
+        out[rows, :] = total.astype(bf16)
 
 
 def image_body(target, other, rows, sibling, sent, kept):
@@ -255,9 +265,10 @@
     for part, out in enumerate((sent, kept)):
         index = part * step + lax.broadcasted_iota(jnp.int32, (step, target.shape[1]), 0)
         hot = jnp.where(index == target[...], 1.0, 0.0).astype(bf16)
-        total = dot(hot, rows[...])
+        count = target.shape[1]
+        total = dot(hot, rows[:count, :])
         hot = jnp.where(index == other[...], 1.0, 0.0).astype(bf16)
-        out[...] = (total + dot(hot, sibling[...])).astype(bf16)
+        out[...] = (total + dot(hot, sibling[:count, :])).astype(bf16)
 
 
 def shards(
@@ -288,7 +299,7 @@
 
     offsets = jnp.cumsum(lengths) - lengths
     ticks = jnp.arange(tokens, dtype=jnp.int32)
-    places = jnp.concatenate([first + ticks, (seq_index ^ 1) * tokens + ticks])
+    places = jnp.concatenate([first + ticks, first - WIN + ticks, (seq_index ^ 1) * tokens + ticks])
     numbers = jnp.arange(lengths.shape[0], dtype=jnp.int32)
     segment = jnp.sum((places[:, None] >= offsets[None, :]).astype(jnp.int32), axis=1) - 1
     member = (segment[:, None] == numbers[None, :]).astype(jnp.int32)
@@ -296,7 +307,7 @@
     length = jnp.sum(member * lengths[None, :], axis=1)
     half = HD // 2
     freq = jnp.exp(jnp.arange(half, dtype=f32) * (-2.0 * math.log(10000.0) / HD))
-    angle = inner[:tokens].astype(f32)[:, None] * freq[None, :]
+    angle = inner[: 2 * tokens].astype(f32)[:, None] * freq[None, :]
     cosine = jnp.cos(angle)
     sine = jnp.sin(angle)
     cosine = jnp.concatenate([cosine, cosine], axis=1)
@@ -323,7 +334,7 @@
     column = rank(seq_index // 8, owner // 8) * 4 + rank(seq_index // 2 % 4, owner // 2 % 4)
     mine = keep & (within // part_rows == f) & (owner % 2 == seq_index % 2)
     target = jnp.where(mine, (column * 2 + page % 2) * part_rows + within % part_rows, -1)
-    other = target[None, tokens:]
+    other = target[None, 2 * tokens :]
     target = target[None, :tokens]
     held_rows = 2 * part_rows
 
@@ -345,9 +356,7 @@
         [place],
         [x0, x1, x2, x3, gain1, keyvalue_weight],
     )
-    y2 = from_peer(kv_part, 2)
-    y1 = from_peer(kv_part, 1)
-    y3 = from_peer(kv_part, 3)
+    far_part = from_earlier(kv_part, 2)
     queries = run(
         query_body,
         sds((tokens, query_weight.shape[1]), bf16),
@@ -355,30 +364,20 @@
         [place],
         [normed, query_weight, cosine, sine],
     )
-    rotated = run(
+    far_part, queries = lax.optimization_barrier((far_part, queries))
+    y0 = run(join_body, sds((tokens, 128), bf16), "join", [], [kv_part, far_part])
+    y2, y1, y3 = from_peer(y0, 2), from_peer(y0, 1), from_peer(y0, 3)
+    mine = run(
         rotate_body,
-        sds((tokens, 2 * HD), bf16),
+        sds((2 * tokens, 2 * HD), bf16),
         "rotate",
         [place],
-        [kv_part, y1, y2, y3, cosine, sine],
-        [pltpu.VMEM((4, tokens // 2, 128), f32)],
-    )
-    far = from_earlier(rotated, 2)
-    sibling = from_partner(rotated, 1)
-    image_sent, image_kept = run(
-        image_body,
-        [sds((8 * held_rows, 2 * HD), bf16)] * 2,
-        "image",
-        [],
-        [target, other, rotated, sibling],
-    )
-    landed = from_partner(image_sent, 8)
-
+        [y0, y1, y2, y3, cosine, sine],
+        [pltpu.VMEM((4, tokens, 128), f32)],
+    )
+    theirs = from_partner(mine, 1)
     def halves(rows):
         return [sds((rows.shape[0] // 2, 2 * HD), bf16)] * 2
-
-    far, queries, _ = lax.optimization_barrier((far, queries, image_sent))
-    far_other = from_partner(far, 1)
 
     def attend(d, kind, cached=()):
         out = sds((step, full), kind)
@@ -387,14 +386,24 @@
             [out, *halves(cached[0])] if cached else out,
             f"attend{d}",
             [place, offsets],
-            [queries, far, far_other, rotated, sibling, output_weight, *cached],
+            [queries, mine, theirs, output_weight, *cached],
             [
                 pltpu.VMEM((4 * tokens, 2 * HD), bf16),
                 pltpu.VMEM((step, query_weight.shape[1]), bf16),
             ],
         )
 
-    p2 = from_peer(attend(2, bf16), 2)
+    s2 = attend(2, bf16)
+    p2 = from_peer(s2, 2)
+    image_sent, image_kept = run(
+        image_body,
+        [sds((8 * held_rows, 2 * HD), bf16)] * 2,
+        "image",
+        [],
+        [target, other, mine, theirs],
+    )
+    landed = from_partner(image_sent, 8)
+
     p1 = from_peer(attend(1, bf16), 3)
     p3 = from_peer(attend(3, bf16), 1)
     p0, stay, go = attend(0, f32, [image_kept, landed])
@@ -404,7 +413,7 @@
         [sds((4, step, width), f32), sds((step, full), bf16), *halves(stay)],
         "residual",
         [],
-        [kept, p0, p1, p2, p3, gain2, stay, landed],
+        [kept, p0, p2, p1, p3, gain2, stay, landed],
     )
     landed = from_partner(go, 2)
     m1 = from_peer(normed2, 1)
@@ -448,7 +457,6 @@
         "finish",
         [place],
         got,
-        [pltpu.VMEM((4, step, width), f32)],
     )
     return (output, cache.reshape(2, part_rows, 2 * HD))
 

time: 120 us -> 114 us (0.950)
  waiting for transfers between devices: 55.8 us -> 40.2 us
  starting transfers between devices: 29.3 us -> 38.2 us
  other arithmetic: 4.52 us -> 7.73 us
  Pallas kernels: 25.8 us -> 24.4 us
    ppermute x19, starting transfers between devices: 23 us -> 32.2 us  [from_peer(): lax.ppermute(block, 'feat', [(i, (i - distance) % n) for i in range(n)])]
    ppermute x19, waiting for transfers between devices: 37.7 us -> 30.7 us  [from_peer(): lax.ppermute(block, 'feat', [(i, (i - distance) % n) for i in range(n)])]
    ppermute x6 -> x5, waiting for transfers between devices: 11.3 us -> 6.75 us  [from_partner(): return lax.ppermute(block, 'seq', [(i, i ^ bits) for i in range(n)])]
    ppermute x1, waiting for transfers between devices: 6.77 us -> 2.78 us  [from_earlier(): lax.ppermute(block, 'seq', [(i - distance, i) for i in range(distance, n)])]
    neg x1, other arithmetic: 0.99 us -> 2.96 us  [shards(): sine = jnp.concatenate([-sine, sine], axis=1)]
    pallas_call x15 -> x16, Pallas kernels: 25.8 us -> 24.4 us  [run(): pl.pallas_call(body, out_shape=outs, in_specs=[SM] * len(scalars) + [VM]...]
    ppermute x6 -> x5, starting transfers between devices: 2.4 us -> 2.15 us  [from_partner(): return lax.ppermute(block, 'seq', [(i, i ^ bits) for i in range(n)])]
  transfers between devices with their start and end apart: 26 -> 25, of which waited for: 16 -> 13; matrix products, arithmetic and copies ran while one was open for 6% -> 9% of each run, Pallas kernels for 18% -> 16%
where the time goes in v4:
time: 114 us
  waiting for transfers between devices  40.2 us (35%)
  starting transfers between devices  38.2 us (34%)
  Pallas kernels  24.4 us (21%)
  other arithmetic  7.73 us (7%)
  local copies, waits for them, and re-layouts  2.62 us (2%)
    ppermute x19, starting transfers between devices, from_peer(): lax.ppermute(block, 'feat', [(i, (i - distance) % n) for i in range(n)])  32.2 us
    ppermute x19, waiting for transfers between devices, from_peer(): lax.ppermute(block, 'feat', [(i, (i - distance) % n) for i in range(n)])  30.7 us
    pallas_call x16, Pallas kernels, run(): pl.pallas_call(body, out_shape=outs, in_specs=[SM] * len(scalars) + [VM]...  24.4 us
    ppermute x5, waiting for transfers between devices, from_partner(): return lax.ppermute(block, 'seq', [(i, i ^ bits) for i in range(n)])  6.75 us
    ppermute x1, starting transfers between devices, from_earlier(): lax.ppermute(block, 'seq', [(i - distance, i) for i in range(distance, n)])  3.83 us
    neg x1, other arithmetic, shards(): sine = jnp.concatenate([-sine, sine], axis=1)  2.96 us
    ppermute x1, waiting for transfers between devices, from_earlier(): lax.ppermute(block, 'seq', [(i - distance, i) for i in range(distance, n)])  2.78 us
  transfers between devices with their start and end apart: 25, of which 13 were waited for; matrix products, arithmetic and copies ran while one was open for 9% of the time, Pallas kernels for 16%

profile of v4, /device:TPU:6, one launch (start us, length us, event | category | flops | bytes accessed | tf_op | source)
XLA Modules:
  0.0 114.0 jit_solution(17147504959346458216)
XLA Ops:
  0.6 3.3 %collective-permute-start.1 = (bf16[512,384]{1,0:T(8,128)(2,1)}, bf16[512,384]{1,0:T(8,128)(2,1)S(1)}, u32[]{:S(2)}, u32[]{:S(2)}) collective-permute-start(bf16[512,384]{1,0:T(8,128)(2,1)} %source.1), channel_id=1, source_target_pairs={{0,2},{1,3},{2,0},{3,1},{4,6},{5,7},{6,4},{7,5},{8,10},{9,11},{10,... | collective-permute-start | bytes 1179656 | tf_op jit(solution)/shard_map/ppermute | solution.py:23
  11.0 3.0 %fusion = (f32[1024,64]{1,0:T(8,128)S(1)}, f32[1024,64]{1,0:T(8,128)}, f32[1024,64]{1,0:T(8,128)S(1)}) fusion(f32[64]{0:T(128)S(1)} %multiply_exponential_fusion, f32[1024]{0:T(1024)S(1)} %slice_convert_fusion), kind=kLoop, calls=%fused_computation.6 | loop fusion | flops 131072 | bytes 790784 | tf_op jit(solution)/shard_map/neg | solution.py:314
  16.4 5.7 %collective-permute-done.x1 = bf16[512,384]{1,0:T(8,128)(2,1)S(1)} collective-permute-done((bf16[512,384]{1,0:T(8,128)(2,1)}, bf16[512,384]{1,0:T(8,128)(2,1)S(1)}, u32[]{:S(2)}, u32[]{:S(2)}) %collective-permute-start) | collective-permute-done | bytes 393248 | tf_op jit(solution)/shard_map/ppermute | solution.py:23
  23.8 3.8 %collective-permute-start.3 = (bf16[256,128]{1,0:T(8,128)(2,1)S(1)}, bf16[256,128]{1,0:T(8,128)(2,1)S(1)}, u32[]{:S(2)}, u32[]{:S(2)}) collective-permute-start(bf16[256,128]{1,0:T(8,128)(2,1)S(1)} %get-tuple-element.57.a), channel_id=1, source_target_pairs={{0,8},{4,12},{8,16},{12,20},{16,24},{20,28},{24,32},{28,36},{32,40... | collective-permute-start | bytes 196616 | tf_op jit(solution)/shard_map/ppermute | solution.py:28
  29.5 2.8 %collective-permute-done.3.b = bf16[256,128]{1,0:T(8,128)(2,1)S(1)} collective-permute-done((bf16[256,128]{1,0:T(8,128)(2,1)S(1)}, bf16[256,128]{1,0:T(8,128)(2,1)S(1)}, u32[]{:S(2)}, u32[]{:S(2)}) %collective-permute-start.3) | collective-permute-done | bytes 65568 | tf_op jit(solution)/shard_map/ppermute | solution.py:28
  33.7 2.8 %collective-permute-start.5 = (bf16[512,128]{1,0:T(8,128)(2,1)S(1)}, bf16[512,128]{1,0:T(8,128)(2,1)S(1)}, u32[]{:S(2)}, u32[]{:S(2)}) collective-permute-start(bf16[512,128]{1,0:T(8,128)(2,1)S(1)} %join.1.y0), channel_id=1, source_target_pairs={{0,2},{1,3},{2,0},{3,1},{4,6},{5,7},{6,4},{7,5},{8,10},{9,11},{10,... | collective-permute-start | bytes 393224 | tf_op jit(solution)/shard_map/ppermute | solution.py:23
  39.3 2.9 %collective-permute-done.5.y2 = bf16[512,128]{1,0:T(8,128)(2,1)S(1)} collective-permute-done((bf16[512,128]{1,0:T(8,128)(2,1)S(1)}, bf16[512,128]{1,0:T(8,128)(2,1)S(1)}, u32[]{:S(2)}, u32[]{:S(2)}) %collective-permute-start.5) | collective-permute-done | bytes 131104 | tf_op jit(solution)/shard_map/ppermute | solution.py:23
  43.4 1.9 %collective-permute-done.7.sibling.theirs = bf16[1024,256]{1,0:T(8,128)(2,1)S(1)} collective-permute-done((bf16[1024,256]{1,0:T(8,128)(2,1)S(1)}, bf16[1024,256]{1,0:T(8,128)(2,1)S(1)}, u32[]{:S(2)}, u32[]{:S(2)}) %collective-permute-start.7) | collective-permute-done | bytes 524320 | tf_op jit(solution)/shard_map/ppermute | solution.py:33
  47.2 2.6 %collective-permute-start.9 = (bf16[128,1536]{1,0:T(8,128)(2,1)S(1)}, bf16[128,1536]{1,0:T(8,128)(2,1)S(1)}, u32[]{:S(2)}, u32[]{:S(2)}) collective-permute-start(bf16[128,1536]{1,0:T(8,128)(2,1)S(1)} %attend2.1), channel_id=1, source_target_pairs={{0,2},{1,3},{2,0},{3,1},{4,6},{5,7},{6,4},{7,5},{8,10},{9,11},{10,... | collective-permute-start | bytes 1179656 | tf_op jit(solution)/shard_map/ppermute | solution.py:23
  55.6 2.5 %collective-permute-start.11 = (bf16[128,1536]{1,0:T(8,128)(2,1)S(1)}, bf16[128,1536]{1,0:T(8,128)(2,1)S(1)}, u32[]{:S(2)}, u32[]{:S(2)}) collective-permute-start(bf16[128,1536]{1,0:T(8,128)(2,1)S(1)} %attend3.1), channel_id=1, source_target_pairs={{0,3},{1,0},{2,1},{3,2},{4,7},{5,4},{6,5},{7,6},{8,11},{9,8},{10,9... | collective-permute-start | bytes 1179656 | tf_op jit(solution)/shard_map/ppermute | solution.py:23
  58.6 1.9 %attend0.1 = (f32[128,1536]{1,0:T(8,128)S(1)}, bf16[256,256]{1,0:T(8,128)(2,1)S(1)}, bf16[256,256]{1,0:T(8,128)(2,1)S(1)}) custom-call(s32[3]{0:T(128)S(1)} %pad_add_fusion.1.place.refs_0_, s32[8]{0:T(128)S(1)} %bitcast_subtract_fusion.offsets, bf16[512,384]{1,0:T(8,128)(2,1)S(1)} %queries.1.q, bf16[1024,256]{1,0:T(8,128)(2,1)S(1)} %rotate.1.rows.mine, ...), custom_call_target="tpu_custom_call" | custom-call | flops 2000000000 | bytes 10000000 | tf_op jit(solution)/shard_map/attend0/pallas_call | solution.py:38
  61.2 7.1 %collective-permute-done.10.p2 = bf16[128,1536]{1,0:T(8,128)(2,1)S(1)} collective-permute-done((bf16[128,1536]{1,0:T(8,128)(2,1)S(1)}, bf16[128,1536]{1,0:T(8,128)(2,1)S(1)}, u32[]{:S(2)}, u32[]{:S(2)}) %collective-permute-start.10) | collective-permute-done | bytes 393248 | tf_op jit(solution)/shard_map/ppermute | solution.py:23
  70.0 2.1 %collective-permute-start.14 = (bf16[128,1536]{1,0:T(8,128)(2,1)S(1)}, bf16[128,1536]{1,0:T(8,128)(2,1)S(1)}, u32[]{:S(2)}, u32[]{:S(2)}) collective-permute-start(bf16[128,1536]{1,0:T(8,128)(2,1)S(1)} %get-tuple-element.71.refs_1_), channel_id=1, source_target_pairs={{0,3},{1,0},{2,1},{3,2},{4,7},{5,4},{6,5},{7,6},{8,11},{9,8},{10,9... | collective-permute-start | bytes 1179656 | tf_op jit(solution)/shard_map/ppermute | solution.py:23
  72.1 4.3 %collective-permute-done.13.refs_3_ = bf16[128,256]{1,0:T(8,128)(2,1)S(1)} collective-permute-done((bf16[128,256]{1,0:T(8,128)(2,1)S(1)}, bf16[128,256]{1,0:T(8,128)(2,1)S(1)}, u32[]{:S(2)}, u32[]{:S(2)}) %collective-permute-start.13) | collective-permute-done | bytes 65568 | tf_op jit(solution)/shard_map/ppermute | solution.py:33
  76.4 2.4 %feed_own.1 = (f32[128,384]{1,0:T(8,128)S(1)}, bf16[128,384]{1,0:T(8,128)(2,1)S(1)}, bf16[128,384]{1,0:T(8,128)(2,1)S(1)}, bf16[128,384]{1,0:T(8,128)(2,1)S(1)},...) custom-call(s32[3]{0:T(128)S(1)} %pad_add_fusion.1.place.refs_0_, ...), custom_call_target="tpu_custom_call" | custom-call | flops 2000000000 | bytes 10000000 | tf_op jit(solution)/shard_map/feed_own/pallas_call | solution.py:38
  81.1 3.0 %collective-permute-start.17 = (bf16[64,1536]{1,0:T(8,128)(2,1)S(1)}, bf16[64,1536]{1,0:T(8,128)(2,1)S(1)}, u32[]{:S(2)}, u32[]{:S(2)}) collective-permute-start(bf16[64,1536]{1,0:T(8,128)(2,1)S(1)} %get-tuple-element.88), channel_id=1, source_target_pairs={{0,3},{1,0},{2,1},{3,2},{4,7},{5,4},{6,5},{7,6},{8,11},{9,8},{10,9... | collective-permute-start | bytes 589832 | tf_op jit(solution)/shard_map/ppermute | solution.py:23
  84.1 4.7 %feed_near.1 = (f32[256,384]{1,0:T(8,128)S(1)}, bf16[384,384]{1,0:T(8,128)(2,1)S(1)}, bf16[384,384]{1,0:T(8,128)(2,1)S(1)}, bf16[384,384]{1,0:T(8,128)(2,1)S(1)}, bf16[64,256]{1,0:T(8,128)(2,1)}) custom-call(s32[3]{0:T(128)S(1)} %pad_add_fusion.1.place.refs_0_, bf16[128,1536]{1,0:T(8,128)(2,1)S(1)} %collective-permute-done.14.a.refs_1_, ...), custom_call_target="tpu_custom_call" | custom-call | flops 2000000000 | bytes 10000000 | tf_op jit(solution)/shard_map/feed_near/pallas_call | solution.py:38
  88.9 3.2 %collective-permute-start.19 = (bf16[384,384]{1,0:T(8,128)(2,1)S(1)}, bf16[384,384]{1,0:T(8,128)(2,1)S(1)}, u32[]{:S(2)}, u32[]{:S(2)}) collective-permute-start(bf16[384,384]{1,0:T(8,128)(2,1)S(1)} %get-tuple-element.91), channel_id=1, source_target_pairs={{0,3},{1,0},{2,1},{3,2},{4,7},{5,4},{6,5},{7,6},{8,11},{9,8},{10,9... | collective-permute-start | bytes 884744 | tf_op jit(solution)/shard_map/ppermute | solution.py:23
  93.0 2.4 %feed_far.1 = (f32[128,384]{1,0:T(8,128)S(1)}, bf16[128,384]{1,0:T(8,128)(2,1)S(1)}, bf16[128,384]{1,0:T(8,128)(2,1)S(1)}, bf16[128,384]{1,0:T(8,128)(2,1)S(1)}) custom-call(s32[3]{0:T(128)S(1)} %pad_add_fusion.1.place.refs_0_, bf16[64,1536]{1,0:T(8,128)(2,1)S(1)} %collective-permute-done.17.refs_1_, bf16[64,1536]{1,0:T(8,128)(2,1)S(1)} %collective-permute-done.18.refs_2_, ...), custom_call_target="tpu_custom_call" | custom-call | flops 2000000000 | bytes 10000000 | tf_op jit(solution)/shard_map/feed_far/pallas_call | solution.py:38
  95.4 2.4 %collective-permute-start.20 = (bf16[128,384]{1,0:T(8,128)(2,1)S(1)}, bf16[128,384]{1,0:T(8,128)(2,1)S(1)}, u32[]{:S(2)}, u32[]{:S(2)}) collective-permute-start(bf16[128,384]{1,0:T(8,128)(2,1)S(1)} %get-tuple-element.92), channel_id=1, source_target_pairs={{0,3},{1,0},{2,1},{3,2},{4,7},{5,4},{6,5},{7,6},{8,11},{9,8},{10,9... | collective-permute-start | bytes 294920 | tf_op jit(solution)/shard_map/ppermute | solution.py:23
  97.9 2.3 %collective-permute-start.22 = (bf16[128,384]{1,0:T(8,128)(2,1)S(1)}, bf16[128,384]{1,0:T(8,128)(2,1)S(1)}, u32[]{:S(2)}, u32[]{:S(2)}) collective-permute-start(bf16[128,384]{1,0:T(8,128)(2,1)S(1)} %get-tuple-element.94), channel_id=1, source_target_pairs={{0,2},{1,3},{2,0},{3,1},{4,6},{5,7},{6,4},{7,5},{8,10},{9,11},{10,... | collective-permute-start | bytes 294920 | tf_op jit(solution)/shard_map/ppermute | solution.py:23
  100.2 6.1 %collective-permute-done.19.refs_3_ = bf16[384,384]{1,0:T(8,128)(2,1)S(1)} collective-permute-done((bf16[384,384]{1,0:T(8,128)(2,1)S(1)}, bf16[384,384]{1,0:T(8,128)(2,1)S(1)}, u32[]{:S(2)}, u32[]{:S(2)}) %collective-permute-start.19) | collective-permute-done | bytes 294944 | tf_op jit(solution)/shard_map/ppermute | solution.py:23
  108.1 2.0 %collective-permute-done.22.refs_6_ = bf16[128,384]{1,0:T(8,128)(2,1)S(1)} collective-permute-done((bf16[128,384]{1,0:T(8,128)(2,1)S(1)}, bf16[128,384]{1,0:T(8,128)(2,1)S(1)}, u32[]{:S(2)}, u32[]{:S(2)}) %collective-permute-start.22) | collective-permute-done | bytes 98336 | tf_op jit(solution)/shard_map/ppermute | solution.py:23
  110.0 2.5 %collective-permute-done.24.refs_8_ = bf16[128,384]{1,0:T(8,128)(2,1)S(1)} collective-permute-done((bf16[128,384]{1,0:T(8,128)(2,1)S(1)}, bf16[128,384]{1,0:T(8,128)(2,1)S(1)}, u32[]{:S(2)}, u32[]{:S(2)}) %collective-permute-start.24) | collective-permute-done | bytes 98336 | tf_op jit(solution)/shard_map/ppermute | solution.py:23
  (75 shorter events, 35.3 us)
Async XLA Ops:
  0.6 15.8 %collective-permute-start.1 = (bf16[512,384]{1,0:T(8,128)(2,1)}, bf16[512,384]{1,0:T(8,128)(2,1)S(1)}, u32[]{:S(2)}, u32[]{:S(2)}) collective-permute-start(bf16[512,384]{1,0:T(8,128)(2,1)} %source.1), channel_id=1, source_target_pairs={{0,2},{1,3},{2,0},{3,1},{4,6},{5,7},{6,4},{7,5},{8,10},{9,11},{10,... | collective-permute-start | bytes 1179656 | tf_op jit(solution)/shard_map/ppermute | solution.py:23
  3.9 18.2 %collective-permute-start = (bf16[512,384]{1,0:T(8,128)(2,1)}, bf16[512,384]{1,0:T(8,128)(2,1)S(1)}, u32[]{:S(2)}, u32[]{:S(2)}) collective-permute-start(bf16[512,384]{1,0:T(8,128)(2,1)} %source.1), channel_id=1, source_target_pairs={{0,3},{1,0},{2,1},{3,2},{4,7},{5,4},{6,5},{7,6},{8,11},{9,8},{10,9... | collective-permute-start | bytes 1179656 | tf_op jit(solution)/shard_map/ppermute | solution.py:23
  5.0 17.1 %collective-permute-start.2 = (bf16[512,384]{1,0:T(8,128)(2,1)}, bf16[512,384]{1,0:T(8,128)(2,1)S(1)}, u32[]{:S(2)}, u32[]{:S(2)}) collective-permute-start(bf16[512,384]{1,0:T(8,128)(2,1)} %source.1), channel_id=1, source_target_pairs={{0,1},{1,2},{2,3},{3,0},{4,5},{5,6},{6,7},{7,4},{8,9},{9,10},{10,1... | collective-permute-start | bytes 1179656 | tf_op jit(solution)/shard_map/ppermute | solution.py:23
  23.8 8.4 %collective-permute-start.3 = (bf16[256,128]{1,0:T(8,128)(2,1)S(1)}, bf16[256,128]{1,0:T(8,128)(2,1)S(1)}, u32[]{:S(2)}, u32[]{:S(2)}) collective-permute-start(bf16[256,128]{1,0:T(8,128)(2,1)S(1)} %get-tuple-element.57.a), channel_id=1, source_target_pairs={{0,8},{4,12},{8,16},{12,20},{16,24},{20,28},{24,32},{28,36},{32,40... | collective-permute-start | bytes 196616 | tf_op jit(solution)/shard_map/ppermute | solution.py:28
  32.3 7.0 %collective-permute-start.6 = (bf16[512,128]{1,0:T(8,128)(2,1)S(1)}, bf16[512,128]{1,0:T(8,128)(2,1)S(1)}, u32[]{:S(2)}, u32[]{:S(2)}) collective-permute-start(bf16[512,128]{1,0:T(8,128)(2,1)S(1)} %join.1.y0), channel_id=1, source_target_pairs={{0,1},{1,2},{2,3},{3,0},{4,5},{5,6},{6,7},{7,4},{8,9},{9,10},{10,1... | collective-permute-start | bytes 393224 | tf_op jit(solution)/shard_map/ppermute | solution.py:23
  33.7 8.5 %collective-permute-start.5 = (bf16[512,128]{1,0:T(8,128)(2,1)S(1)}, bf16[512,128]{1,0:T(8,128)(2,1)S(1)}, u32[]{:S(2)}, u32[]{:S(2)}) collective-permute-start(bf16[512,128]{1,0:T(8,128)(2,1)S(1)} %join.1.y0), channel_id=1, source_target_pairs={{0,2},{1,3},{2,0},{3,1},{4,6},{5,7},{6,4},{7,5},{8,10},{9,11},{10,... | collective-permute-start | bytes 393224 | tf_op jit(solution)/shard_map/ppermute | solution.py:23
  36.5 5.7 %collective-permute-start.4 = (bf16[512,128]{1,0:T(8,128)(2,1)S(1)}, bf16[512,128]{1,0:T(8,128)(2,1)S(1)}, u32[]{:S(2)}, u32[]{:S(2)}) collective-permute-start(bf16[512,128]{1,0:T(8,128)(2,1)S(1)} %join.1.y0), channel_id=1, source_target_pairs={{0,3},{1,0},{2,1},{3,2},{4,7},{5,4},{6,5},{7,6},{8,11},{9,8},{10,9... | collective-permute-start | bytes 393224 | tf_op jit(solution)/shard_map/ppermute | solution.py:23
  47.2 14.1 %collective-permute-start.9 = (bf16[128,1536]{1,0:T(8,128)(2,1)S(1)}, bf16[128,1536]{1,0:T(8,128)(2,1)S(1)}, u32[]{:S(2)}, u32[]{:S(2)}) collective-permute-start(bf16[128,1536]{1,0:T(8,128)(2,1)S(1)} %attend2.1), channel_id=1, source_target_pairs={{0,2},{1,3},{2,0},{3,1},{4,6},{5,7},{6,4},{7,5},{8,10},{9,11},{10,... | collective-permute-start | bytes 1179656 | tf_op jit(solution)/shard_map/ppermute | solution.py:23
  50.5 8.2 %collective-permute-start.8 = (bf16[512,256]{1,0:T(8,128)(2,1)S(1)}, bf16[512,256]{1,0:T(8,128)(2,1)S(1)}, u32[]{:S(2)}, u32[]{:S(2)}) collective-permute-start(bf16[512,256]{1,0:T(8,128)(2,1)S(1)} %get-tuple-element.66), channel_id=1, source_target_pairs={{0,32},{4,36},{8,40},{12,44},{16,48},{20,52},{24,56},{28,60},{32,0... | collective-permute-start | bytes 786440 | tf_op jit(solution)/shard_map/ppermute | solution.py:33
  52.6 15.7 %collective-permute-start.10 = (bf16[128,1536]{1,0:T(8,128)(2,1)S(1)}, bf16[128,1536]{1,0:T(8,128)(2,1)S(1)}, u32[]{:S(2)}, u32[]{:S(2)}) collective-permute-start(bf16[128,1536]{1,0:T(8,128)(2,1)S(1)} %attend1.1), channel_id=1, source_target_pairs={{0,1},{1,2},{2,3},{3,0},{4,5},{5,6},{6,7},{7,4},{8,9},{9,10},{10,1... | collective-permute-start | bytes 1179656 | tf_op jit(solution)/shard_map/ppermute | solution.py:23
  55.6 12.8 %collective-permute-start.11 = (bf16[128,1536]{1,0:T(8,128)(2,1)S(1)}, bf16[128,1536]{1,0:T(8,128)(2,1)S(1)}, u32[]{:S(2)}, u32[]{:S(2)}) collective-permute-start(bf16[128,1536]{1,0:T(8,128)(2,1)S(1)} %attend3.1), channel_id=1, source_target_pairs={{0,3},{1,0},{2,1},{3,2},{4,7},{5,4},{6,5},{7,6},{8,11},{9,8},{10,9... | collective-permute-start | bytes 1179656 | tf_op jit(solution)/shard_map/ppermute | solution.py:23
  60.6 7.8 %collective-permute-start.12 = (bf16[256,256]{1,0:T(8,128)(2,1)S(1)}, bf16[256,256]{1,0:T(8,128)(2,1)S(1)}, u32[]{:S(2)}, u32[]{:S(2)}) collective-permute-start(bf16[256,256]{1,0:T(8,128)(2,1)S(1)} %get-tuple-element.70), channel_id=1, source_target_pairs={{0,96},{4,100},{8,104},{12,108},{16,112},{20,116},{24,120},{28,124... | collective-permute-start | bytes 393224 | tf_op jit(solution)/shard_map/ppermute | solution.py:33
  68.8 12.3 %collective-permute-start.15 = (bf16[128,1536]{1,0:T(8,128)(2,1)S(1)}, bf16[128,1536]{1,0:T(8,128)(2,1)S(1)}, u32[]{:S(2)}, u32[]{:S(2)}) collective-permute-start(bf16[128,1536]{1,0:T(8,128)(2,1)S(1)} %get-tuple-element.71.refs_1_), channel_id=1, source_target_pairs={{0,1},{1,2},{2,3},{3,0},{4,5},{5,6},{6,7},{7,4},{8,9},{9,10},{10,1... | collective-permute-start | bytes 1179656 | tf_op jit(solution)/shard_map/ppermute | solution.py:23
  70.0 11.1 %collective-permute-start.14 = (bf16[128,1536]{1,0:T(8,128)(2,1)S(1)}, bf16[128,1536]{1,0:T(8,128)(2,1)S(1)}, u32[]{:S(2)}, u32[]{:S(2)}) collective-permute-start(bf16[128,1536]{1,0:T(8,128)(2,1)S(1)} %get-tuple-element.71.refs_1_), channel_id=1, source_target_pairs={{0,3},{1,0},{2,1},{3,2},{4,7},{5,4},{6,5},{7,6},{8,11},{9,8},{10,9... | collective-permute-start | bytes 1179656 | tf_op jit(solution)/shard_map/ppermute | solution.py:23
  72.1 4.3 %collective-permute-start.13 = (bf16[128,256]{1,0:T(8,128)(2,1)S(1)}, bf16[128,256]{1,0:T(8,128)(2,1)S(1)}, u32[]{:S(2)}, u32[]{:S(2)}) collective-permute-start(bf16[128,256]{1,0:T(8,128)(2,1)S(1)} %get-tuple-element.73), channel_id=1, source_target_pairs={{0,8},{4,12},{8,0},{12,4},{16,24},{20,28},{24,16},{28,20},{32,40},... | collective-permute-start | bytes 196616 | tf_op jit(solution)/shard_map/ppermute | solution.py:33
  78.8 5.3 %collective-permute-start.16 = (bf16[64,256]{1,0:T(8,128)(2,1)S(1)}, bf16[64,256]{1,0:T(8,128)(2,1)S(1)}, u32[]{:S(2)}, u32[]{:S(2)}) collective-permute-start(bf16[64,256]{1,0:T(8,128)(2,1)S(1)} %get-tuple-element.83), channel_id=1, source_target_pairs={{0,24},{4,28},{8,16},{12,20},{16,8},{20,12},{24,0},{28,4},{32,56},... | collective-permute-start | bytes 98312 | tf_op jit(solution)/shard_map/ppermute | solution.py:33
  81.1 11.8 %collective-permute-start.17 = (bf16[64,1536]{1,0:T(8,128)(2,1)S(1)}, bf16[64,1536]{1,0:T(8,128)(2,1)S(1)}, u32[]{:S(2)}, u32[]{:S(2)}) collective-permute-start(bf16[64,1536]{1,0:T(8,128)(2,1)S(1)} %get-tuple-element.88), channel_id=1, source_target_pairs={{0,3},{1,0},{2,1},{3,2},{4,7},{5,4},{6,5},{7,6},{8,11},{9,8},{10,9... | collective-permute-start | bytes 589832 | tf_op jit(solution)/shard_map/ppermute | solution.py:23
  84.1 8.8 %collective-permute-start.18 = (bf16[64,1536]{1,0:T(8,128)(2,1)S(1)}, bf16[64,1536]{1,0:T(8,128)(2,1)S(1)}, u32[]{:S(2)}, u32[]{:S(2)}) collective-permute-start(bf16[64,1536]{1,0:T(8,128)(2,1)S(1)} %get-tuple-element.89), channel_id=1, source_target_pairs={{0,1},{1,2},{2,3},{3,0},{4,5},{5,6},{6,7},{7,4},{8,9},{9,10},{10,1... | collective-permute-start | bytes 589832 | tf_op jit(solution)/shard_map/ppermute | solution.py:23
  88.9 17.5 %collective-permute-start.19 = (bf16[384,384]{1,0:T(8,128)(2,1)S(1)}, bf16[384,384]{1,0:T(8,128)(2,1)S(1)}, u32[]{:S(2)}, u32[]{:S(2)}) collective-permute-start(bf16[384,384]{1,0:T(8,128)(2,1)S(1)} %get-tuple-element.91), channel_id=1, source_target_pairs={{0,3},{1,0},{2,1},{3,2},{4,7},{5,4},{6,5},{7,6},{8,11},{9,8},{10,9... | collective-permute-start | bytes 884744 | tf_op jit(solution)/shard_map/ppermute | solution.py:23
  92.1 14.2 %collective-permute-start.21 = (bf16[384,384]{1,0:T(8,128)(2,1)S(1)}, bf16[384,384]{1,0:T(8,128)(2,1)S(1)}, u32[]{:S(2)}, u32[]{:S(2)}) collective-permute-start(bf16[384,384]{1,0:T(8,128)(2,1)S(1)} %get-tuple-element.93), channel_id=1, source_target_pairs={{0,2},{1,3},{2,0},{3,1},{4,6},{5,7},{6,4},{7,5},{8,10},{9,11},{10,... | collective-permute-start | bytes 884744 | tf_op jit(solution)/shard_map/ppermute | solution.py:23
  92.1 16.0 %collective-permute-start.23 = (bf16[384,384]{1,0:T(8,128)(2,1)S(1)}, bf16[384,384]{1,0:T(8,128)(2,1)S(1)}, u32[]{:S(2)}, u32[]{:S(2)}) collective-permute-start(bf16[384,384]{1,0:T(8,128)(2,1)S(1)} %get-tuple-element.95), channel_id=1, source_target_pairs={{0,1},{1,2},{2,3},{3,0},{4,5},{5,6},{6,7},{7,4},{8,9},{9,10},{10,1... | collective-permute-start | bytes 884744 | tf_op jit(solution)/shard_map/ppermute | solution.py:23
  95.4 12.6 %collective-permute-start.20 = (bf16[128,384]{1,0:T(8,128)(2,1)S(1)}, bf16[128,384]{1,0:T(8,128)(2,1)S(1)}, u32[]{:S(2)}, u32[]{:S(2)}) collective-permute-start(bf16[128,384]{1,0:T(8,128)(2,1)S(1)} %get-tuple-element.92), channel_id=1, source_target_pairs={{0,3},{1,0},{2,1},{3,2},{4,7},{5,4},{6,5},{7,6},{8,11},{9,8},{10,9... | collective-permute-start | bytes 294920 | tf_op jit(solution)/shard_map/ppermute | solution.py:23
  97.9 12.2 %collective-permute-start.22 = (bf16[128,384]{1,0:T(8,128)(2,1)S(1)}, bf16[128,384]{1,0:T(8,128)(2,1)S(1)}, u32[]{:S(2)}, u32[]{:S(2)}) collective-permute-start(bf16[128,384]{1,0:T(8,128)(2,1)S(1)} %get-tuple-element.94), channel_id=1, source_target_pairs={{0,2},{1,3},{2,0},{3,1},{4,6},{5,7},{6,4},{7,5},{8,10},{9,11},{10,... | collective-permute-start | bytes 294920 | tf_op jit(solution)/shard_map/ppermute | solution.py:23
  106.3 6.3 %collective-permute-start.24 = (bf16[128,384]{1,0:T(8,128)(2,1)S(1)}, bf16[128,384]{1,0:T(8,128)(2,1)S(1)}, u32[]{:S(2)}, u32[]{:S(2)}) collective-permute-start(bf16[128,384]{1,0:T(8,128)(2,1)S(1)} %get-tuple-element.96), channel_id=1, source_target_pairs={{0,1},{1,2},{2,3},{3,0},{4,5},{5,6},{6,7},{7,4},{8,9},{9,10},{10,1... | collective-permute-start | bytes 294920 | tf_op jit(solution)/shard_map/ppermute | solution.py:23
  (7 other events, 70.0 us)

commit v5 on v4

--- a/solution.py
+++ b/solution.py
@@ -208,18 +208,22 @@
     return x * (0.5 * (1.0 + jnp.tanh(inner)))
 
 
-def feed_body(count, own, before, *refs):
+def feed_body(count, own, before, cached, *refs):
     place = refs[0]
     blocks = refs[1 : 1 + count]
     refs = refs[1 + count :]
-    res = earlier = None
+    if cached:
+        outs, (act, hold) = refs[-2 - cached : -2], refs[-2:]
+        if own:
+            merge(refs[0], refs[1], *outs)
+        else:
+            outs[0][...] = (refs[0][...].astype(f32) + refs[1][...].astype(f32)).astype(bf16)
+        refs = refs[2 : -2 - cached] + (act, hold)
+    res = None
     if own:
-        merge(refs[0], refs[1], refs[-4], refs[-3])
-        res, refs = refs[2], refs[3:-4] + refs[-2:]
-    elif before:
-        refs[-3][...] = (refs[0][...].astype(f32) + refs[1][...].astype(f32)).astype(bf16)
-        earlier, refs = refs[2:5], refs[5:-3] + refs[-2:]
-    wg, wu, wd, o0, o1, o2, o3, act, hold = refs
+        res, refs = refs[0], refs[1:]
+    earlier = dict(zip(before, refs[: len(before)]))
+    wg, wu, wd, o0, o1, o2, o3, act, hold = refs[len(before) :]
     f = place[0]
     rows, width = o0.shape
     n = jnp.concatenate([r[...] for r in blocks], axis=0) if count > 1 else blocks[0][...]
@@ -235,27 +239,31 @@
     o0[...] = hold[f]
     for d, o in ((1, o1), (2, o2), (3, o3)):
         lead = o.shape[0] - rows
-        if before:
-            o[:lead, :] = earlier[d - 1][...]
+        if d in earlier:
+            o[:lead, :] = earlier[d][...]
         o[lead:, :] = hold[lax.rem(f + d, 4)].astype(o.dtype)
 
 
-def finish_body(place, *refs):
-    ins, out = refs[:-1], refs[-1]
-    f = place[0]
-    step = out.shape[0] // 4
-    own, both, far = ins[:3]
+def early_sum_body(own, both, far, early2, early3, out):
+    step = own.shape[0]
     for r in range(4):
         total = (own[...], both[:step], far[...], both[step:])[r]
-        for e in range(1, 4):
-            early, late = ins[2 * e + 1 : 2 * e + 3]
+        for e, early in ((2, early2), (3, early3)):
             shift = (r - e) % 4
-            if shift == 2:
-                piece = late[...]
-            else:
+            if shift != 2:
                 row = (0, 1, None, 2)[shift] * step
-                piece = early[row : row + step]
-            total = total + piece.astype(f32)
+                total = total + early[row : row + step].astype(f32)
+        out[r] = total
+
+
+def finish_body(place, some, late2, late3, whole, out):
+    f = place[0]
+    step = some.shape[1]
+    for r in range(4):
+        row = (0, 1, 3, 2)[(r - 1) % 4] * step
+        total = some[r] + whole[row : row + step].astype(f32)
+        if r < 2:
+            total = total + (late2, late3)[r][...].astype(f32)
         rows = pl.ds(pl.multiple_of(lax.rem(f + r, 4) * step, step), step)
         out[rows, :] = total.astype(bf16)
 
@@ -420,23 +428,25 @@
     m3 = from_peer(normed2, 3)
     hidden_units = gate_weight.shape[1]
 
-    def feed(blocks, res=(), before=(), cached=()):
+    def feed(name, blocks, res=(), before=(), cached=()):
         rows = sum(block.shape[0] for block in blocks)
-        sent = rows + (step if before else 0)
-        outs = [sds((rows, width), f32)] + [sds((sent, width), bf16)] * 3
+        lead = {d: rows_before.shape[0] for d, rows_before in before}
+        outs = [sds((rows, width), f32)]
+        outs += [sds((rows + lead.get(d, 0), width), bf16) for d in (1, 2, 3)]
+        more = []
         if cached:
-            outs = outs + (halves(cached[0]) if res else [sds(cached[0].shape, bf16)])
+            more = halves(cached[0]) if res else [sds(cached[0].shape, bf16)]
         return run(
-            functools.partial(feed_body, len(blocks), bool(res), bool(before)),
-            outs,
-            "feed_own" if res else "feed_near" if before else "feed_far",
+            functools.partial(feed_body, len(blocks), bool(res), tuple(lead), len(more)),
+            outs + more,
+            name,
             [place],
-            [*blocks, *cached, *res, *before, gate_weight, up_weight, down_weight],
+            [*blocks, *cached, *res, *(b for _, b in before), gate_weight, up_weight, down_weight],
             [pltpu.VMEM((rows, hidden_units), bf16), pltpu.VMEM((4, rows, width), f32)],
             vmem=24 << 20,
         )
 
-    own0, *own_sent, stay, go = feed([normed2], res=[residual], cached=[stay, landed])
+    own0, *own_sent, stay, go = feed("feed_own", [normed2], res=[residual], cached=[stay, landed])
     landed = from_partner(go, 6)
     half_rows = step // 2
     m1, m3, _ = lax.optimization_barrier((m1, m3, own0))
@@ -446,17 +456,29 @@
     m1, m3, upper, lower = lax.optimization_barrier((m1, m3, upper, lower))
     m2 = [from_peer(upper, 1), from_peer(lower, 3)]
 
-    both0, *early, cache = feed([m1, m3], before=own_sent, cached=[stay, landed])
-    early = [from_peer(early[1], 2), from_peer(early[0], 3), from_peer(early[2], 1)]
-    far0, *late = feed(m2)
-    late = [from_peer(late[1], 2), from_peer(late[0], 3), from_peer(late[2], 1)]
-    got = [own0, both0, far0, early[2], late[2], early[0], late[0], early[1], late[1]]
+    both0, early1, early2, early3, cache = feed(
+        "feed_near", [m1, m3], before=list(zip((1, 2, 3), own_sent)), cached=[stay, landed]
+    )
+    early2 = from_peer(early2, 2)
+    early1 = from_peer(early1, 3)
+    far0, late1, late2, whole = feed("feed_far", m2, before=[(3, early3)])
+    whole = from_peer(whole, 1)
+    late2 = from_peer(late2, 2)
+    late1 = from_peer(late1, 3)
+    some = run(
+        early_sum_body,
+        sds((4, step, width), f32),
+        "early_sum",
+        [],
+        [own0, both0, far0, early2, early1],
+        flops=10_000_000_000,
+    )
     output = run(
         finish_body,
         sds((tokens, width), bf16),
         "finish",
         [place],
-        got,
+        [some, late2, late1, whole],
     )
     return (output, cache.reshape(2, part_rows, 2 * HD))
 

time: 114 us -> 110 us (0.965)
  waiting for transfers between devices: 40.2 us -> 37 us
    ppermute x19 -> x18, waiting for transfers between devices: 30.7 us -> 27.5 us  [from_peer(): lax.ppermute(block, 'feat', [(i, (i - distance) % n) for i in range(n)])]
    ppermute x19 -> x18, starting transfers between devices: 32.2 us -> 31.3 us  [from_peer(): lax.ppermute(block, 'feat', [(i, (i - distance) % n) for i in range(n)])]
    pallas_call x16 -> x17, Pallas kernels: 24.4 us -> 24.4 us  [run(): pl.pallas_call(body, out_shape=outs, in_specs=[SM] * len(scalars) + [VM]...]
  transfers between devices with their start and end apart: 25 -> 24, of which waited for: 13 -> 14; matrix products, arithmetic and copies ran while one was open for 9% -> 9% of each run, Pallas kernels for 16% -> 16%
where the time goes in v5:
time: 110 us
  starting transfers between devices  37.3 us (34%)
  waiting for transfers between devices  37 us (34%)
  Pallas kernels  24.4 us (22%)
  other arithmetic  7.74 us (7%)
  local copies, waits for them, and re-layouts  2.62 us (2%)
    ppermute x18, starting transfers between devices, from_peer(): lax.ppermute(block, 'feat', [(i, (i - distance) % n) for i in range(n)])  31.3 us
    ppermute x18, waiting for transfers between devices, from_peer(): lax.ppermute(block, 'feat', [(i, (i - distance) % n) for i in range(n)])  27.5 us
    pallas_call x17, Pallas kernels, run(): pl.pallas_call(body, out_shape=outs, in_specs=[SM] * len(scalars) + [VM]...  24.4 us
    ppermute x5, waiting for transfers between devices, from_partner(): return lax.ppermute(block, 'seq', [(i, i ^ bits) for i in range(n)])  6.75 us
    ppermute x1, starting transfers between devices, from_earlier(): lax.ppermute(block, 'seq', [(i - distance, i) for i in range(distance, n)])  3.83 us
    neg x1, other arithmetic, shards(): sine = jnp.concatenate([-sine, sine], axis=1)  2.98 us
    ppermute x1, waiting for transfers between devices, from_earlier(): lax.ppermute(block, 'seq', [(i - distance, i) for i in range(distance, n)])  2.78 us
  transfers between devices with their start and end apart: 24, of which 14 were waited for; matrix products, arithmetic and copies ran while one was open for 9% of the time, Pallas kernels for 16%

profile of v5, /device:TPU:6, one launch (start us, length us, event | category | flops | bytes accessed | tf_op | source)
XLA Modules:
  0.0 110.0 jit_solution(1530698411722647152)
XLA Ops:
  0.6 3.3 %collective-permute-start.1 = (bf16[512,384]{1,0:T(8,128)(2,1)}, bf16[512,384]{1,0:T(8,128)(2,1)S(1)}, u32[]{:S(2)}, u32[]{:S(2)}) collective-permute-start(bf16[512,384]{1,0:T(8,128)(2,1)} %source.1), channel_id=1, source_target_pairs={{0,2},{1,3},{2,0},{3,1},{4,6},{5,7},{6,4},{7,5},{8,10},{9,11},{10,... | collective-permute-start | bytes 1179656 | tf_op jit(solution)/shard_map/ppermute | solution.py:23
  11.0 3.0 %fusion = (f32[1024,64]{1,0:T(8,128)S(1)}, f32[1024,64]{1,0:T(8,128)}, f32[1024,64]{1,0:T(8,128)S(1)}) fusion(f32[64]{0:T(128)S(1)} %multiply_exponential_fusion, f32[1024]{0:T(1024)S(1)} %slice_convert_fusion), kind=kLoop, calls=%fused_computation.6 | loop fusion | flops 131072 | bytes 790784 | tf_op jit(solution)/shard_map/neg | solution.py:322
  16.4 5.7 %collective-permute-done.x1 = bf16[512,384]{1,0:T(8,128)(2,1)S(1)} collective-permute-done((bf16[512,384]{1,0:T(8,128)(2,1)}, bf16[512,384]{1,0:T(8,128)(2,1)S(1)}, u32[]{:S(2)}, u32[]{:S(2)}) %collective-permute-start) | collective-permute-done | bytes 393248 | tf_op jit(solution)/shard_map/ppermute | solution.py:23
  23.8 3.8 %collective-permute-start.3 = (bf16[256,128]{1,0:T(8,128)(2,1)S(1)}, bf16[256,128]{1,0:T(8,128)(2,1)S(1)}, u32[]{:S(2)}, u32[]{:S(2)}) collective-permute-start(bf16[256,128]{1,0:T(8,128)(2,1)S(1)} %get-tuple-element.57.a), channel_id=1, source_target_pairs={{0,8},{4,12},{8,16},{12,20},{16,24},{20,28},{24,32},{28,36},{32,40... | collective-permute-start | bytes 196616 | tf_op jit(solution)/shard_map/ppermute | solution.py:28
  29.5 2.8 %collective-permute-done.3.b = bf16[256,128]{1,0:T(8,128)(2,1)S(1)} collective-permute-done((bf16[256,128]{1,0:T(8,128)(2,1)S(1)}, bf16[256,128]{1,0:T(8,128)(2,1)S(1)}, u32[]{:S(2)}, u32[]{:S(2)}) %collective-permute-start.3) | collective-permute-done | bytes 65568 | tf_op jit(solution)/shard_map/ppermute | solution.py:28
  33.7 2.8 %collective-permute-start.5 = (bf16[512,128]{1,0:T(8,128)(2,1)S(1)}, bf16[512,128]{1,0:T(8,128)(2,1)S(1)}, u32[]{:S(2)}, u32[]{:S(2)}) collective-permute-start(bf16[512,128]{1,0:T(8,128)(2,1)S(1)} %join.1.y0), channel_id=1, source_target_pairs={{0,2},{1,3},{2,0},{3,1},{4,6},{5,7},{6,4},{7,5},{8,10},{9,11},{10,... | collective-permute-start | bytes 393224 | tf_op jit(solution)/shard_map/ppermute | solution.py:23
  39.3 2.9 %collective-permute-done.5.y2 = bf16[512,128]{1,0:T(8,128)(2,1)S(1)} collective-permute-done((bf16[512,128]{1,0:T(8,128)(2,1)S(1)}, bf16[512,128]{1,0:T(8,128)(2,1)S(1)}, u32[]{:S(2)}, u32[]{:S(2)}) %collective-permute-start.5) | collective-permute-done | bytes 131104 | tf_op jit(solution)/shard_map/ppermute | solution.py:23
  43.4 1.9 %collective-permute-done.7.sibling.theirs = bf16[1024,256]{1,0:T(8,128)(2,1)S(1)} collective-permute-done((bf16[1024,256]{1,0:T(8,128)(2,1)S(1)}, bf16[1024,256]{1,0:T(8,128)(2,1)S(1)}, u32[]{:S(2)}, u32[]{:S(2)}) %collective-permute-start.7) | collective-permute-done | bytes 524320 | tf_op jit(solution)/shard_map/ppermute | solution.py:33
  45.3 1.9 %attend2.1 = bf16[128,1536]{1,0:T(8,128)(2,1)S(1)} custom-call(s32[3]{0:T(128)S(1)} %pad_add_fusion.1.place.refs_0_, s32[8]{0:T(128)S(1)} %bitcast_subtract_fusion.offsets, bf16[512,384]{1,0:T(8,128)(2,1)S(1)} %queries.1.q, bf16[1024,256]{1,0:T(8,128)(2,1)S(1)} %rotate.1.rows.mine, bf16[1024,256]{1,0:T(8,128)(2,1)S(1)} %collective-permute-done.7.sibling.theirs, ...), custom_call_target="tpu_custom_call" | custom-call | flops 2000000000 | bytes 10000000 | tf_op jit(solution)/shard_map/attend2/pallas_call | solution.py:38
  47.2 2.6 %collective-permute-start.9 = (bf16[128,1536]{1,0:T(8,128)(2,1)S(1)}, bf16[128,1536]{1,0:T(8,128)(2,1)S(1)}, u32[]{:S(2)}, u32[]{:S(2)}) collective-permute-start(bf16[128,1536]{1,0:T(8,128)(2,1)S(1)} %attend2.1), channel_id=1, source_target_pairs={{0,2},{1,3},{2,0},{3,1},{4,6},{5,7},{6,4},{7,5},{8,10},{9,11},{10,... | collective-permute-start | bytes 1179656 | tf_op jit(solution)/shard_map/ppermute | solution.py:23
  50.7 1.9 %attend1.1 = bf16[128,1536]{1,0:T(8,128)(2,1)S(1)} custom-call(s32[3]{0:T(128)S(1)} %pad_add_fusion.1.place.refs_0_, s32[8]{0:T(128)S(1)} %bitcast_subtract_fusion.offsets, bf16[512,384]{1,0:T(8,128)(2,1)S(1)} %queries.1.q, bf16[1024,256]{1,0:T(8,128)(2,1)S(1)} %rotate.1.rows.mine, bf16[1024,256]{1,0:T(8,128)(2,1)S(1)} %collective-permute-done.7.sibling.theirs, ...), custom_call_target="tpu_custom_call" | custom-call | flops 2000000000 | bytes 10000000 | tf_op jit(solution)/shard_map/attend1/pallas_call | solution.py:38
  55.6 2.5 %collective-permute-start.11 = (bf16[128,1536]{1,0:T(8,128)(2,1)S(1)}, bf16[128,1536]{1,0:T(8,128)(2,1)S(1)}, u32[]{:S(2)}, u32[]{:S(2)}) collective-permute-start(bf16[128,1536]{1,0:T(8,128)(2,1)S(1)} %attend3.1), channel_id=1, source_target_pairs={{0,3},{1,0},{2,1},{3,2},{4,7},{5,4},{6,5},{7,6},{8,11},{9,8},{10,9... | collective-permute-start | bytes 1179656 | tf_op jit(solution)/shard_map/ppermute | solution.py:23
  58.6 1.9 %attend0.1 = (f32[128,1536]{1,0:T(8,128)S(1)}, bf16[256,256]{1,0:T(8,128)(2,1)S(1)}, bf16[256,256]{1,0:T(8,128)(2,1)S(1)}) custom-call(s32[3]{0:T(128)S(1)} %pad_add_fusion.1.place.refs_0_, s32[8]{0:T(128)S(1)} %bitcast_subtract_fusion.offsets, bf16[512,384]{1,0:T(8,128)(2,1)S(1)} %queries.1.q, bf16[1024,256]{1,0:T(8,128)(2,1)S(1)} %rotate.1.rows.mine, ...), custom_call_target="tpu_custom_call" | custom-call | flops 2000000000 | bytes 10000000 | tf_op jit(solution)/shard_map/attend0/pallas_call | solution.py:38
  61.2 7.1 %collective-permute-done.10.p2 = bf16[128,1536]{1,0:T(8,128)(2,1)S(1)} collective-permute-done((bf16[128,1536]{1,0:T(8,128)(2,1)S(1)}, bf16[128,1536]{1,0:T(8,128)(2,1)S(1)}, u32[]{:S(2)}, u32[]{:S(2)}) %collective-permute-start.10) | collective-permute-done | bytes 393248 | tf_op jit(solution)/shard_map/ppermute | solution.py:23
  70.0 2.1 %collective-permute-start.14 = (bf16[128,1536]{1,0:T(8,128)(2,1)S(1)}, bf16[128,1536]{1,0:T(8,128)(2,1)S(1)}, u32[]{:S(2)}, u32[]{:S(2)}) collective-permute-start(bf16[128,1536]{1,0:T(8,128)(2,1)S(1)} %get-tuple-element.71.refs_1_), channel_id=1, source_target_pairs={{0,3},{1,0},{2,1},{3,2},{4,7},{5,4},{6,5},{7,6},{8,11},{9,8},{10,9... | collective-permute-start | bytes 1179656 | tf_op jit(solution)/shard_map/ppermute | solution.py:23
  72.1 4.3 %collective-permute-done.13.refs_3_ = bf16[128,256]{1,0:T(8,128)(2,1)S(1)} collective-permute-done((bf16[128,256]{1,0:T(8,128)(2,1)S(1)}, bf16[128,256]{1,0:T(8,128)(2,1)S(1)}, u32[]{:S(2)}, u32[]{:S(2)}) %collective-permute-start.13) | collective-permute-done | bytes 65568 | tf_op jit(solution)/shard_map/ppermute | solution.py:33
  76.4 2.4 %feed_own.1 = (f32[128,384]{1,0:T(8,128)S(1)}, bf16[128,384]{1,0:T(8,128)(2,1)S(1)}, bf16[128,384]{1,0:T(8,128)(2,1)S(1)}, bf16[128,384]{1,0:T(8,128)(2,1)S(1)},...) custom-call(s32[3]{0:T(128)S(1)} %pad_add_fusion.1.place.refs_0_, ...), custom_call_target="tpu_custom_call" | custom-call | flops 2000000000 | bytes 10000000 | tf_op jit(solution)/shard_map/feed_own/pallas_call | solution.py:38
  81.1 3.0 %collective-permute-start.17 = (bf16[64,1536]{1,0:T(8,128)(2,1)S(1)}, bf16[64,1536]{1,0:T(8,128)(2,1)S(1)}, u32[]{:S(2)}, u32[]{:S(2)}) collective-permute-start(bf16[64,1536]{1,0:T(8,128)(2,1)S(1)} %get-tuple-element.88), channel_id=1, source_target_pairs={{0,3},{1,0},{2,1},{3,2},{4,7},{5,4},{6,5},{7,6},{8,11},{9,8},{10,9... | collective-permute-start | bytes 589832 | tf_op jit(solution)/shard_map/ppermute | solution.py:23
  84.2 4.7 %feed_near.1 = (f32[256,384]{1,0:T(8,128)S(1)}, bf16[384,384]{1,0:T(8,128)(2,1)S(1)}, bf16[384,384]{1,0:T(8,128)(2,1)S(1)}, bf16[384,384]{1,0:T(8,128)(2,1)S(1)}, bf16[64,256]{1,0:T(8,128)(2,1)}) custom-call(s32[3]{0:T(128)S(1)} %pad_add_fusion.1.place.refs_0_, bf16[128,1536]{1,0:T(8,128)(2,1)S(1)} %collective-permute-done.14.a.refs_1_, ...), custom_call_target="tpu_custom_call" | custom-call | flops 2000000000 | bytes 10000000 | tf_op jit(solution)/shard_map/feed_near/pallas_call | solution.py:38
  90.4 2.5 %collective-permute-start.20 = (bf16[384,384]{1,0:T(8,128)(2,1)S(1)}, bf16[384,384]{1,0:T(8,128)(2,1)S(1)}, u32[]{:S(2)}, u32[]{:S(2)}) collective-permute-start(bf16[384,384]{1,0:T(8,128)(2,1)S(1)} %get-tuple-element.93), channel_id=1, source_target_pairs={{0,1},{1,2},{2,3},{3,0},{4,5},{5,6},{6,7},{7,4},{8,9},{9,10},{10,1... | collective-permute-start | bytes 884744 | tf_op jit(solution)/shard_map/ppermute | solution.py:23
  93.0 2.4 %feed_far.1 = (f32[128,384]{1,0:T(8,128)S(1)}, bf16[128,384]{1,0:T(8,128)(2,1)S(1)}, bf16[128,384]{1,0:T(8,128)(2,1)S(1)}, bf16[512,384]{1,0:T(8,128)(2,1)S(1)}) custom-call(s32[3]{0:T(128)S(1)} %pad_add_fusion.1.place.refs_0_, bf16[64,1536]{1,0:T(8,128)(2,1)S(1)} %collective-permute-done.17.refs_1_, bf16[64,1536]{1,0:T(8,128)(2,1)S(1)} %collective-permute-done.18.refs_2_, ...), custom_call_target="tpu_custom_call" | custom-call | flops 2000000000 | bytes 10000000 | tf_op jit(solution)/shard_map/feed_far/pallas_call | solution.py:38
  97.0 2.3 %collective-permute-start.23 = (bf16[512,384]{1,0:T(8,128)(2,1)S(1)}, bf16[512,384]{1,0:T(8,128)(2,1)S(1)}, u32[]{:S(2)}, u32[]{:S(2)}) collective-permute-start(bf16[512,384]{1,0:T(8,128)(2,1)S(1)} %get-tuple-element.96), channel_id=1, source_target_pairs={{0,3},{1,0},{2,1},{3,2},{4,7},{5,4},{6,5},{7,6},{8,11},{9,8},{10,9... | collective-permute-start | bytes 1179656 | tf_op jit(solution)/shard_map/ppermute | solution.py:23
  100.4 5.0 %collective-permute-done.20.early3 = bf16[384,384]{1,0:T(8,128)(2,1)S(1)} collective-permute-done((bf16[384,384]{1,0:T(8,128)(2,1)S(1)}, bf16[384,384]{1,0:T(8,128)(2,1)S(1)}, u32[]{:S(2)}, u32[]{:S(2)}) %collective-permute-start.20) | collective-permute-done | bytes 294944 | tf_op jit(solution)/shard_map/ppermute | solution.py:23
  105.4 2.1 %collective-permute-done.21.late2 = bf16[128,384]{1,0:T(8,128)(2,1)S(1)} collective-permute-done((bf16[128,384]{1,0:T(8,128)(2,1)S(1)}, bf16[128,384]{1,0:T(8,128)(2,1)S(1)}, u32[]{:S(2)}, u32[]{:S(2)}) %collective-permute-start.21) | collective-permute-done | bytes 98336 | tf_op jit(solution)/shard_map/ppermute | solution.py:23
  (74 shorter events, 34.3 us)
Async XLA Ops:
  0.6 15.8 %collective-permute-start.1 = (bf16[512,384]{1,0:T(8,128)(2,1)}, bf16[512,384]{1,0:T(8,128)(2,1)S(1)}, u32[]{:S(2)}, u32[]{:S(2)}) collective-permute-start(bf16[512,384]{1,0:T(8,128)(2,1)} %source.1), channel_id=1, source_target_pairs={{0,2},{1,3},{2,0},{3,1},{4,6},{5,7},{6,4},{7,5},{8,10},{9,11},{10,... | collective-permute-start | bytes 1179656 | tf_op jit(solution)/shard_map/ppermute | solution.py:23
  3.9 18.2 %collective-permute-start = (bf16[512,384]{1,0:T(8,128)(2,1)}, bf16[512,384]{1,0:T(8,128)(2,1)S(1)}, u32[]{:S(2)}, u32[]{:S(2)}) collective-permute-start(bf16[512,384]{1,0:T(8,128)(2,1)} %source.1), channel_id=1, source_target_pairs={{0,3},{1,0},{2,1},{3,2},{4,7},{5,4},{6,5},{7,6},{8,11},{9,8},{10,9... | collective-permute-start | bytes 1179656 | tf_op jit(solution)/shard_map/ppermute | solution.py:23
  5.0 17.1 %collective-permute-start.2 = (bf16[512,384]{1,0:T(8,128)(2,1)}, bf16[512,384]{1,0:T(8,128)(2,1)S(1)}, u32[]{:S(2)}, u32[]{:S(2)}) collective-permute-start(bf16[512,384]{1,0:T(8,128)(2,1)} %source.1), channel_id=1, source_target_pairs={{0,1},{1,2},{2,3},{3,0},{4,5},{5,6},{6,7},{7,4},{8,9},{9,10},{10,1... | collective-permute-start | bytes 1179656 | tf_op jit(solution)/shard_map/ppermute | solution.py:23
  23.8 8.4 %collective-permute-start.3 = (bf16[256,128]{1,0:T(8,128)(2,1)S(1)}, bf16[256,128]{1,0:T(8,128)(2,1)S(1)}, u32[]{:S(2)}, u32[]{:S(2)}) collective-permute-start(bf16[256,128]{1,0:T(8,128)(2,1)S(1)} %get-tuple-element.57.a), channel_id=1, source_target_pairs={{0,8},{4,12},{8,16},{12,20},{16,24},{20,28},{24,32},{28,36},{32,40... | collective-permute-start | bytes 196616 | tf_op jit(solution)/shard_map/ppermute | solution.py:28
  32.3 7.0 %collective-permute-start.6 = (bf16[512,128]{1,0:T(8,128)(2,1)S(1)}, bf16[512,128]{1,0:T(8,128)(2,1)S(1)}, u32[]{:S(2)}, u32[]{:S(2)}) collective-permute-start(bf16[512,128]{1,0:T(8,128)(2,1)S(1)} %join.1.y0), channel_id=1, source_target_pairs={{0,1},{1,2},{2,3},{3,0},{4,5},{5,6},{6,7},{7,4},{8,9},{9,10},{10,1... | collective-permute-start | bytes 393224 | tf_op jit(solution)/shard_map/ppermute | solution.py:23
  33.7 8.5 %collective-permute-start.5 = (bf16[512,128]{1,0:T(8,128)(2,1)S(1)}, bf16[512,128]{1,0:T(8,128)(2,1)S(1)}, u32[]{:S(2)}, u32[]{:S(2)}) collective-permute-start(bf16[512,128]{1,0:T(8,128)(2,1)S(1)} %join.1.y0), channel_id=1, source_target_pairs={{0,2},{1,3},{2,0},{3,1},{4,6},{5,7},{6,4},{7,5},{8,10},{9,11},{10,... | collective-permute-start | bytes 393224 | tf_op jit(solution)/shard_map/ppermute | solution.py:23
  36.5 5.7 %collective-permute-start.4 = (bf16[512,128]{1,0:T(8,128)(2,1)S(1)}, bf16[512,128]{1,0:T(8,128)(2,1)S(1)}, u32[]{:S(2)}, u32[]{:S(2)}) collective-permute-start(bf16[512,128]{1,0:T(8,128)(2,1)S(1)} %join.1.y0), channel_id=1, source_target_pairs={{0,3},{1,0},{2,1},{3,2},{4,7},{5,4},{6,5},{7,6},{8,11},{9,8},{10,9... | collective-permute-start | bytes 393224 | tf_op jit(solution)/shard_map/ppermute | solution.py:23
  43.3 2.0 %collective-permute-start.7 = (bf16[1024,256]{1,0:T(8,128)(2,1)S(1)}, bf16[1024,256]{1,0:T(8,128)(2,1)S(1)}, u32[]{:S(2)}, u32[]{:S(2)}) collective-permute-start(bf16[1024,256]{1,0:T(8,128)(2,1)S(1)} %rotate.1.rows.mine), channel_id=1, source_target_pairs={{0,4},{4,0},{8,12},{12,8},{16,20},{20,16},{24,28},{28,24},{32,36},... | collective-permute-start | bytes 1572872 | tf_op jit(solution)/shard_map/ppermute | solution.py:33
  47.2 14.1 %collective-permute-start.9 = (bf16[128,1536]{1,0:T(8,128)(2,1)S(1)}, bf16[128,1536]{1,0:T(8,128)(2,1)S(1)}, u32[]{:S(2)}, u32[]{:S(2)}) collective-permute-start(bf16[128,1536]{1,0:T(8,128)(2,1)S(1)} %attend2.1), channel_id=1, source_target_pairs={{0,2},{1,3},{2,0},{3,1},{4,6},{5,7},{6,4},{7,5},{8,10},{9,11},{10,... | collective-permute-start | bytes 1179656 | tf_op jit(solution)/shard_map/ppermute | solution.py:23
  50.5 8.2 %collective-permute-start.8 = (bf16[512,256]{1,0:T(8,128)(2,1)S(1)}, bf16[512,256]{1,0:T(8,128)(2,1)S(1)}, u32[]{:S(2)}, u32[]{:S(2)}) collective-permute-start(bf16[512,256]{1,0:T(8,128)(2,1)S(1)} %get-tuple-element.66), channel_id=1, source_target_pairs={{0,32},{4,36},{8,40},{12,44},{16,48},{20,52},{24,56},{28,60},{32,0... | collective-permute-start | bytes 786440 | tf_op jit(solution)/shard_map/ppermute | solution.py:33
  52.6 15.7 %collective-permute-start.10 = (bf16[128,1536]{1,0:T(8,128)(2,1)S(1)}, bf16[128,1536]{1,0:T(8,128)(2,1)S(1)}, u32[]{:S(2)}, u32[]{:S(2)}) collective-permute-start(bf16[128,1536]{1,0:T(8,128)(2,1)S(1)} %attend1.1), channel_id=1, source_target_pairs={{0,1},{1,2},{2,3},{3,0},{4,5},{5,6},{6,7},{7,4},{8,9},{9,10},{10,1... | collective-permute-start | bytes 1179656 | tf_op jit(solution)/shard_map/ppermute | solution.py:23
  55.6 12.8 %collective-permute-start.11 = (bf16[128,1536]{1,0:T(8,128)(2,1)S(1)}, bf16[128,1536]{1,0:T(8,128)(2,1)S(1)}, u32[]{:S(2)}, u32[]{:S(2)}) collective-permute-start(bf16[128,1536]{1,0:T(8,128)(2,1)S(1)} %attend3.1), channel_id=1, source_target_pairs={{0,3},{1,0},{2,1},{3,2},{4,7},{5,4},{6,5},{7,6},{8,11},{9,8},{10,9... | collective-permute-start | bytes 1179656 | tf_op jit(solution)/shard_map/ppermute | solution.py:23
  60.6 7.8 %collective-permute-start.12 = (bf16[256,256]{1,0:T(8,128)(2,1)S(1)}, bf16[256,256]{1,0:T(8,128)(2,1)S(1)}, u32[]{:S(2)}, u32[]{:S(2)}) collective-permute-start(bf16[256,256]{1,0:T(8,128)(2,1)S(1)} %get-tuple-element.70), channel_id=1, source_target_pairs={{0,96},{4,100},{8,104},{12,108},{16,112},{20,116},{24,120},{28,124... | collective-permute-start | bytes 393224 | tf_op jit(solution)/shard_map/ppermute | solution.py:33
  68.8 12.3 %collective-permute-start.15 = (bf16[128,1536]{1,0:T(8,128)(2,1)S(1)}, bf16[128,1536]{1,0:T(8,128)(2,1)S(1)}, u32[]{:S(2)}, u32[]{:S(2)}) collective-permute-start(bf16[128,1536]{1,0:T(8,128)(2,1)S(1)} %get-tuple-element.71.refs_1_), channel_id=1, source_target_pairs={{0,1},{1,2},{2,3},{3,0},{4,5},{5,6},{6,7},{7,4},{8,9},{9,10},{10,1... | collective-permute-start | bytes 1179656 | tf_op jit(solution)/shard_map/ppermute | solution.py:23
  70.0 11.1 %collective-permute-start.14 = (bf16[128,1536]{1,0:T(8,128)(2,1)S(1)}, bf16[128,1536]{1,0:T(8,128)(2,1)S(1)}, u32[]{:S(2)}, u32[]{:S(2)}) collective-permute-start(bf16[128,1536]{1,0:T(8,128)(2,1)S(1)} %get-tuple-element.71.refs_1_), channel_id=1, source_target_pairs={{0,3},{1,0},{2,1},{3,2},{4,7},{5,4},{6,5},{7,6},{8,11},{9,8},{10,9... | collective-permute-start | bytes 1179656 | tf_op jit(solution)/shard_map/ppermute | solution.py:23
  72.1 4.3 %collective-permute-start.13 = (bf16[128,256]{1,0:T(8,128)(2,1)S(1)}, bf16[128,256]{1,0:T(8,128)(2,1)S(1)}, u32[]{:S(2)}, u32[]{:S(2)}) collective-permute-start(bf16[128,256]{1,0:T(8,128)(2,1)S(1)} %get-tuple-element.73), channel_id=1, source_target_pairs={{0,8},{4,12},{8,0},{12,4},{16,24},{20,28},{24,16},{28,20},{32,40},... | collective-permute-start | bytes 196616 | tf_op jit(solution)/shard_map/ppermute | solution.py:33
  78.8 5.3 %collective-permute-start.16 = (bf16[64,256]{1,0:T(8,128)(2,1)S(1)}, bf16[64,256]{1,0:T(8,128)(2,1)S(1)}, u32[]{:S(2)}, u32[]{:S(2)}) collective-permute-start(bf16[64,256]{1,0:T(8,128)(2,1)S(1)} %get-tuple-element.83), channel_id=1, source_target_pairs={{0,24},{4,28},{8,16},{12,20},{16,8},{20,12},{24,0},{28,4},{32,56},... | collective-permute-start | bytes 98312 | tf_op jit(solution)/shard_map/ppermute | solution.py:33
  81.1 11.8 %collective-permute-start.17 = (bf16[64,1536]{1,0:T(8,128)(2,1)S(1)}, bf16[64,1536]{1,0:T(8,128)(2,1)S(1)}, u32[]{:S(2)}, u32[]{:S(2)}) collective-permute-start(bf16[64,1536]{1,0:T(8,128)(2,1)S(1)} %get-tuple-element.88), channel_id=1, source_target_pairs={{0,3},{1,0},{2,1},{3,2},{4,7},{5,4},{6,5},{7,6},{8,11},{9,8},{10,9... | collective-permute-start | bytes 589832 | tf_op jit(solution)/shard_map/ppermute | solution.py:23
  84.2 8.8 %collective-permute-start.18 = (bf16[64,1536]{1,0:T(8,128)(2,1)S(1)}, bf16[64,1536]{1,0:T(8,128)(2,1)S(1)}, u32[]{:S(2)}, u32[]{:S(2)}) collective-permute-start(bf16[64,1536]{1,0:T(8,128)(2,1)S(1)} %get-tuple-element.89), channel_id=1, source_target_pairs={{0,1},{1,2},{2,3},{3,0},{4,5},{5,6},{6,7},{7,4},{8,9},{9,10},{10,1... | collective-permute-start | bytes 589832 | tf_op jit(solution)/shard_map/ppermute | solution.py:23
  88.9 11.5 %collective-permute-start.19 = (bf16[384,384]{1,0:T(8,128)(2,1)S(1)}, bf16[384,384]{1,0:T(8,128)(2,1)S(1)}, u32[]{:S(2)}, u32[]{:S(2)}) collective-permute-start(bf16[384,384]{1,0:T(8,128)(2,1)S(1)} %get-tuple-element.92), channel_id=1, source_target_pairs={{0,2},{1,3},{2,0},{3,1},{4,6},{5,7},{6,4},{7,5},{8,10},{9,11},{10,... | collective-permute-start | bytes 884744 | tf_op jit(solution)/shard_map/ppermute | solution.py:23
  90.4 14.9 %collective-permute-start.20 = (bf16[384,384]{1,0:T(8,128)(2,1)S(1)}, bf16[384,384]{1,0:T(8,128)(2,1)S(1)}, u32[]{:S(2)}, u32[]{:S(2)}) collective-permute-start(bf16[384,384]{1,0:T(8,128)(2,1)S(1)} %get-tuple-element.93), channel_id=1, source_target_pairs={{0,1},{1,2},{2,3},{3,0},{4,5},{5,6},{6,7},{7,4},{8,9},{9,10},{10,1... | collective-permute-start | bytes 884744 | tf_op jit(solution)/shard_map/ppermute | solution.py:23
  95.4 12.1 %collective-permute-start.21 = (bf16[128,384]{1,0:T(8,128)(2,1)S(1)}, bf16[128,384]{1,0:T(8,128)(2,1)S(1)}, u32[]{:S(2)}, u32[]{:S(2)}) collective-permute-start(bf16[128,384]{1,0:T(8,128)(2,1)S(1)} %get-tuple-element.94), channel_id=1, source_target_pairs={{0,2},{1,3},{2,0},{3,1},{4,6},{5,7},{6,4},{7,5},{8,10},{9,11},{10,... | collective-permute-start | bytes 294920 | tf_op jit(solution)/shard_map/ppermute | solution.py:23
  96.1 12.3 %collective-permute-start.22 = (bf16[128,384]{1,0:T(8,128)(2,1)S(1)}, bf16[128,384]{1,0:T(8,128)(2,1)S(1)}, u32[]{:S(2)}, u32[]{:S(2)}) collective-permute-start(bf16[128,384]{1,0:T(8,128)(2,1)S(1)} %get-tuple-element.95), channel_id=1, source_target_pairs={{0,1},{1,2},{2,3},{3,0},{4,5},{5,6},{6,7},{7,4},{8,9},{9,10},{10,1... | collective-permute-start | bytes 294920 | tf_op jit(solution)/shard_map/ppermute | solution.py:23
  97.0 11.6 %collective-permute-start.23 = (bf16[512,384]{1,0:T(8,128)(2,1)S(1)}, bf16[512,384]{1,0:T(8,128)(2,1)S(1)}, u32[]{:S(2)}, u32[]{:S(2)}) collective-permute-start(bf16[512,384]{1,0:T(8,128)(2,1)S(1)} %get-tuple-element.96), channel_id=1, source_target_pairs={{0,3},{1,0},{2,1},{3,2},{4,7},{5,4},{6,5},{7,6},{8,11},{9,8},{10,9... | collective-permute-start | bytes 1179656 | tf_op jit(solution)/shard_map/ppermute | solution.py:23
  (6 other events, 68.0 us)

commit v6 on v5

--- a/solution.py
+++ b/solution.py
@@ -26,6 +26,12 @@
 def from_earlier(block, distance):
     n = lax.axis_size("seq")
     return lax.ppermute(block, "seq", [(i - distance, i) for i in range(distance, n)])
+
+
+def to_side(block, distances):
+    n, m = lax.axis_size("seq"), lax.axis_size("feat")
+    route = [(i * m + j, i * m + (j + distances[i % 2]) % m) for i in range(n) for j in range(m)]
+    return lax.ppermute(block, ("seq", "feat"), route)
 
 
 def from_partner(block, bits):
@@ -197,10 +203,14 @@
         n_out[:, cols] = (res_out[g] * scale * gain[:, cols]).astype(bf16)
 
 
-def split_body(a, b, upper, lower):
-    half = upper.shape[0]
-    upper[...] = a[:half, :]
-    lower[...] = b[half:, :]
+def pick_body(place, ahead, behind, out):
+    @pl.when(place[2] == 0)
+    def _():
+        out[...] = behind[...]
+
+    @pl.when(place[2] == 1)
+    def _():
+        out[...] = ahead[...]
 
 
 def gelu(x):
@@ -241,29 +251,37 @@
         lead = o.shape[0] - rows
         if d in earlier:
             o[:lead, :] = earlier[d][...]
-        o[lead:, :] = hold[lax.rem(f + d, 4)].astype(o.dtype)
-
-
-def early_sum_body(own, both, far, early2, early3, out):
+        target = d if d == 2 else d + (2 - d) * 2 * place[2]
+        o[lead:, :] = hold[lax.rem(f + target, 4)].astype(o.dtype)
+
+
+def early_sum_body(place, own, both, far, early2, early1, out):
     step = own.shape[0]
-    for r in range(4):
-        total = (own[...], both[:step], far[...], both[step:])[r]
-        for e, early in ((2, early2), (3, early3)):
-            shift = (r - e) % 4
-            if shift != 2:
-                row = (0, 1, None, 2)[shift] * step
-                total = total + early[row : row + step].astype(f32)
-        out[r] = total
-
-
-def finish_body(place, some, late2, late3, whole, out):
-    f = place[0]
+    out[0] = own[...]
+    out[1] = both[:step]
+    out[2] = far[...]
+    out[3] = both[step:]
+    side = 3 - 2 * place[2]
+    for row, shift in enumerate((0, 1, 3)):
+        rows = slice(row * step, row * step + step)
+        r = (shift + 2) % 4
+        out[r] = out[r] + early2[rows].astype(f32)
+        r = lax.rem(shift + side, 4)
+        out[r] = out[r] + early1[rows].astype(f32)
+
+
+def finish_body(place, some, late2, late1, whole, out):
+    f, core = place[0], place[2]
     step = some.shape[1]
-    for r in range(4):
-        row = (0, 1, 3, 2)[(r - 1) % 4] * step
-        total = some[r] + whole[row : row + step].astype(f32)
-        if r < 2:
-            total = total + (late2, late3)[r][...].astype(f32)
+    side = 1 + 2 * core
+    for row, shift in enumerate((0, 1, 3, 2)):
+        r = lax.rem(shift + side, 4)
+        total = some[r] + whole[row * step : row * step + step].astype(f32)
+        if shift == 0:
+            total = total + late1[...].astype(f32)
+        elif shift != 2:
+            mine = core == (0 if shift == 3 else 1)
+            total = total + jnp.where(mine, late2[...].astype(f32), 0.0)
         rows = pl.ds(pl.multiple_of(lax.rem(f + r, 4) * step, step), step)
         out[rows, :] = total.astype(bf16)
 
@@ -444,32 +462,29 @@
             [*blocks, *cached, *res, *(b for _, b in before), gate_weight, up_weight, down_weight],
             [pltpu.VMEM((rows, hidden_units), bf16), pltpu.VMEM((4, rows, width), f32)],
             vmem=24 << 20,
+            flops=20_000_000_000 if before and cached else 2_000_000_000,
         )
 
     own0, *own_sent, stay, go = feed("feed_own", [normed2], res=[residual], cached=[stay, landed])
     landed = from_partner(go, 6)
-    half_rows = step // 2
     m1, m3, _ = lax.optimization_barrier((m1, m3, own0))
-    upper, lower = run(
-        split_body, [sds((half_rows, full), bf16)] * 2, "split", [], [m1, m3]
-    )
-    m1, m3, upper, lower = lax.optimization_barrier((m1, m3, upper, lower))
-    m2 = [from_peer(upper, 1), from_peer(lower, 3)]
-
+    passed = run(pick_body, sds((step, full), bf16), "pick", [place], [m1, m3])
+    m1, m3, passed = lax.optimization_barrier((m1, m3, passed))
+    m2 = to_side(passed, (1, 3))
     both0, early1, early2, early3, cache = feed(
         "feed_near", [m1, m3], before=list(zip((1, 2, 3), own_sent)), cached=[stay, landed]
     )
     early2 = from_peer(early2, 2)
-    early1 = from_peer(early1, 3)
-    far0, late1, late2, whole = feed("feed_far", m2, before=[(3, early3)])
-    whole = from_peer(whole, 1)
+    early1 = to_side(early1, (1, 3))
+    far0, late1, late2, whole = feed("feed_far", [m2], before=[(3, early3)])
+    whole = to_side(whole, (3, 1))
     late2 = from_peer(late2, 2)
-    late1 = from_peer(late1, 3)
+    late1 = to_side(late1, (1, 3))
     some = run(
         early_sum_body,
         sds((4, step, width), f32),
         "early_sum",
-        [],
+        [place],
         [own0, both0, far0, early2, early1],
         flops=10_000_000_000,
     )

time: 110 us -> 111 us (level)
  starting transfers between devices: 37.3 us -> 34.8 us
  waiting for transfers between devices: 37 us -> 38.6 us
  Pallas kernels: 24.4 us -> 25.6 us
    ppermute x18 -> x13, starting transfers between devices: 31.3 us -> 24.4 us  [from_peer(): lax.ppermute(block, 'feat', [(i, (i - distance) % n) for i in range(n)])]
    ppermute x0 -> x4, waiting for transfers between devices: none -> 6.26 us  [to_side(): return lax.ppermute(block, ('seq', 'feat'), route)]
    ppermute x18 -> x13, waiting for transfers between devices: 27.5 us -> 21.6 us  [from_peer(): lax.ppermute(block, 'feat', [(i, (i - distance) % n) for i in range(n)])]
    ppermute x0 -> x4, starting transfers between devices: none -> 4.34 us  [to_side(): return lax.ppermute(block, ('seq', 'feat'), route)]
    ppermute x5, waiting for transfers between devices: 6.75 us -> 8.03 us  [from_partner(): return lax.ppermute(block, 'seq', [(i, i ^ bits) for i in range(n)])]
    pallas_call x17, Pallas kernels: 24.4 us -> 25.6 us  [run(): pl.pallas_call(body, out_shape=outs, in_specs=[SM] * len(scalars) + [VM]...]
  transfers between devices with their start and end apart: 24 -> 23, of which waited for: 14 -> 14; matrix products, arithmetic and copies ran while one was open for 9% -> 9% of each run, Pallas kernels for 16% -> 17%
where the time goes in v6:
time: 111 us; the launch traced here: 110 us
  waiting for transfers between devices  38.6 us (35%)
  starting transfers between devices  34.8 us (31%)
  Pallas kernels  25.6 us (23%)
  other arithmetic  7.73 us (7%)
  local copies, waits for them, and re-layouts  2.62 us (2%)
    pallas_call x17, Pallas kernels, run(): pl.pallas_call(body, out_shape=outs, in_specs=[SM] * len(scalars) + [VM]...  25.6 us
    ppermute x13, starting transfers between devices, from_peer(): lax.ppermute(block, 'feat', [(i, (i - distance) % n) for i in range(n)])  24.4 us
    ppermute x13, waiting for transfers between devices, from_peer(): lax.ppermute(block, 'feat', [(i, (i - distance) % n) for i in range(n)])  21.6 us
    ppermute x5, waiting for transfers between devices, from_partner(): return lax.ppermute(block, 'seq', [(i, i ^ bits) for i in range(n)])  8.03 us
    ppermute x4, waiting for transfers between devices, to_side(): return lax.ppermute(block, ('seq', 'feat'), route)  6.26 us
    ppermute x4, starting transfers between devices, to_side(): return lax.ppermute(block, ('seq', 'feat'), route)  4.34 us
    ppermute x1, starting transfers between devices, from_earlier(): lax.ppermute(block, 'seq', [(i - distance, i) for i in range(distance, n)])  3.83 us
    neg x1, other arithmetic, shards(): sine = jnp.concatenate([-sine, sine], axis=1)  2.96 us
  transfers between devices with their start and end apart: 23, of which 14 were waited for; matrix products, arithmetic and copies ran while one was open for 9% of the time, Pallas kernels for 17%

profile of v6, /device:TPU:6, one launch (start us, length us, event | category | flops | bytes accessed | tf_op | source)
XLA Modules:
  0.0 110.3 jit_solution(15417376925379363701)
XLA Ops:
  0.6 3.3 %collective-permute-start.1 = (bf16[512,384]{1,0:T(8,128)(2,1)}, bf16[512,384]{1,0:T(8,128)(2,1)S(1)}, u32[]{:S(2)}, u32[]{:S(2)}) collective-permute-start(bf16[512,384]{1,0:T(8,128)(2,1)} %source.1), channel_id=1, source_target_pairs={{0,2},{1,3},{2,0},{3,1},{4,6},{5,7},{6,4},{7,5},{8,10},{9,11},{10,... | collective-permute-start | bytes 1179656 | tf_op jit(solution)/shard_map/ppermute | solution.py:23
  11.0 3.0 %fusion = (f32[1024,64]{1,0:T(8,128)S(1)}, f32[1024,64]{1,0:T(8,128)}, f32[1024,64]{1,0:T(8,128)S(1)}) fusion(f32[64]{0:T(128)S(1)} %multiply_exponential_fusion, f32[1024]{0:T(1024)S(1)} %slice_convert_fusion), kind=kLoop, calls=%fused_computation.6 | loop fusion | flops 131072 | bytes 790784 | tf_op jit(solution)/shard_map/neg | solution.py:340
  16.4 5.7 %collective-permute-done.x1 = bf16[512,384]{1,0:T(8,128)(2,1)S(1)} collective-permute-done((bf16[512,384]{1,0:T(8,128)(2,1)}, bf16[512,384]{1,0:T(8,128)(2,1)S(1)}, u32[]{:S(2)}, u32[]{:S(2)}) %collective-permute-start) | collective-permute-done | bytes 393248 | tf_op jit(solution)/shard_map/ppermute | solution.py:23
  23.8 3.8 %collective-permute-start.3 = (bf16[256,128]{1,0:T(8,128)(2,1)S(1)}, bf16[256,128]{1,0:T(8,128)(2,1)S(1)}, u32[]{:S(2)}, u32[]{:S(2)}) collective-permute-start(bf16[256,128]{1,0:T(8,128)(2,1)S(1)} %get-tuple-element.54.a), channel_id=1, source_target_pairs={{0,8},{4,12},{8,16},{12,20},{16,24},{20,28},{24,32},{28,36},{32,40... | collective-permute-start | bytes 196616 | tf_op jit(solution)/shard_map/ppermute | solution.py:28
  29.5 2.8 %collective-permute-done.3.b = bf16[256,128]{1,0:T(8,128)(2,1)S(1)} collective-permute-done((bf16[256,128]{1,0:T(8,128)(2,1)S(1)}, bf16[256,128]{1,0:T(8,128)(2,1)S(1)}, u32[]{:S(2)}, u32[]{:S(2)}) %collective-permute-start.3) | collective-permute-done | bytes 65568 | tf_op jit(solution)/shard_map/ppermute | solution.py:28
  33.7 2.8 %collective-permute-start.5 = (bf16[512,128]{1,0:T(8,128)(2,1)S(1)}, bf16[512,128]{1,0:T(8,128)(2,1)S(1)}, u32[]{:S(2)}, u32[]{:S(2)}) collective-permute-start(bf16[512,128]{1,0:T(8,128)(2,1)S(1)} %join.1.y0), channel_id=1, source_target_pairs={{0,2},{1,3},{2,0},{3,1},{4,6},{5,7},{6,4},{7,5},{8,10},{9,11},{10,... | collective-permute-start | bytes 393224 | tf_op jit(solution)/shard_map/ppermute | solution.py:23
  39.3 2.9 %collective-permute-done.5.y2 = bf16[512,128]{1,0:T(8,128)(2,1)S(1)} collective-permute-done((bf16[512,128]{1,0:T(8,128)(2,1)S(1)}, bf16[512,128]{1,0:T(8,128)(2,1)S(1)}, u32[]{:S(2)}, u32[]{:S(2)}) %collective-permute-start.5) | collective-permute-done | bytes 131104 | tf_op jit(solution)/shard_map/ppermute | solution.py:23
  43.4 1.9 %collective-permute-done.7.sibling.theirs = bf16[1024,256]{1,0:T(8,128)(2,1)S(1)} collective-permute-done((bf16[1024,256]{1,0:T(8,128)(2,1)S(1)}, bf16[1024,256]{1,0:T(8,128)(2,1)S(1)}, u32[]{:S(2)}, u32[]{:S(2)}) %collective-permute-start.7) | collective-permute-done | bytes 524320 | tf_op jit(solution)/shard_map/ppermute | solution.py:39
  45.3 1.9 %attend2.1 = bf16[128,1536]{1,0:T(8,128)(2,1)S(1)} custom-call(s32[3]{0:T(128)S(1)} %pad_add_fusion.1.place.refs_0_, s32[8]{0:T(128)S(1)} %bitcast_subtract_fusion.offsets, bf16[512,384]{1,0:T(8,128)(2,1)S(1)} %queries.1.q, bf16[1024,256]{1,0:T(8,128)(2,1)S(1)} %rotate.1.rows.mine, bf16[1024,256]{1,0:T(8,128)(2,1)S(1)} %collective-permute-done.7.sibling.theirs, ...), custom_call_target="tpu_custom_call" | custom-call | flops 2000000000 | bytes 10000000 | tf_op jit(solution)/shard_map/attend2/pallas_call | solution.py:44
  47.2 2.6 %collective-permute-start.9 = (bf16[128,1536]{1,0:T(8,128)(2,1)S(1)}, bf16[128,1536]{1,0:T(8,128)(2,1)S(1)}, u32[]{:S(2)}, u32[]{:S(2)}) collective-permute-start(bf16[128,1536]{1,0:T(8,128)(2,1)S(1)} %attend2.1), channel_id=1, source_target_pairs={{0,2},{1,3},{2,0},{3,1},{4,6},{5,7},{6,4},{7,5},{8,10},{9,11},{10,... | collective-permute-start | bytes 1179656 | tf_op jit(solution)/shard_map/ppermute | solution.py:23
  50.7 1.9 %attend1.1 = bf16[128,1536]{1,0:T(8,128)(2,1)S(1)} custom-call(s32[3]{0:T(128)S(1)} %pad_add_fusion.1.place.refs_0_, s32[8]{0:T(128)S(1)} %bitcast_subtract_fusion.offsets, bf16[512,384]{1,0:T(8,128)(2,1)S(1)} %queries.1.q, bf16[1024,256]{1,0:T(8,128)(2,1)S(1)} %rotate.1.rows.mine, bf16[1024,256]{1,0:T(8,128)(2,1)S(1)} %collective-permute-done.7.sibling.theirs, ...), custom_call_target="tpu_custom_call" | custom-call | flops 2000000000 | bytes 10000000 | tf_op jit(solution)/shard_map/attend1/pallas_call | solution.py:44
  53.7 1.9 %attend3.1 = bf16[128,1536]{1,0:T(8,128)(2,1)S(1)} custom-call(s32[3]{0:T(128)S(1)} %pad_add_fusion.1.place.refs_0_, s32[8]{0:T(128)S(1)} %bitcast_subtract_fusion.offsets, bf16[512,384]{1,0:T(8,128)(2,1)S(1)} %queries.1.q, bf16[1024,256]{1,0:T(8,128)(2,1)S(1)} %rotate.1.rows.mine, bf16[1024,256]{1,0:T(8,128)(2,1)S(1)} %collective-permute-done.7.sibling.theirs, ...), custom_call_target="tpu_custom_call" | custom-call | flops 2000000000 | bytes 10000000 | tf_op jit(solution)/shard_map/attend3/pallas_call | solution.py:44
  55.6 2.5 %collective-permute-start.11 = (bf16[128,1536]{1,0:T(8,128)(2,1)S(1)}, bf16[128,1536]{1,0:T(8,128)(2,1)S(1)}, u32[]{:S(2)}, u32[]{:S(2)}) collective-permute-start(bf16[128,1536]{1,0:T(8,128)(2,1)S(1)} %attend3.1), channel_id=1, source_target_pairs={{0,3},{1,0},{2,1},{3,2},{4,7},{5,4},{6,5},{7,6},{8,11},{9,8},{10,9... | collective-permute-start | bytes 1179656 | tf_op jit(solution)/shard_map/ppermute | solution.py:23
  58.6 1.9 %attend0.1 = (f32[128,1536]{1,0:T(8,128)S(1)}, bf16[256,256]{1,0:T(8,128)(2,1)S(1)}, bf16[256,256]{1,0:T(8,128)(2,1)S(1)}) custom-call(s32[3]{0:T(128)S(1)} %pad_add_fusion.1.place.refs_0_, s32[8]{0:T(128)S(1)} %bitcast_subtract_fusion.offsets, bf16[512,384]{1,0:T(8,128)(2,1)S(1)} %queries.1.q, bf16[1024,256]{1,0:T(8,128)(2,1)S(1)} %rotate.1.rows.mine, ...), custom_call_target="tpu_custom_call" | custom-call | flops 2000000000 | bytes 10000000 | tf_op jit(solution)/shard_map/attend0/pallas_call | solution.py:44
  61.2 7.1 %collective-permute-done.10.p2 = bf16[128,1536]{1,0:T(8,128)(2,1)S(1)} collective-permute-done((bf16[128,1536]{1,0:T(8,128)(2,1)S(1)}, bf16[128,1536]{1,0:T(8,128)(2,1)S(1)}, u32[]{:S(2)}, u32[]{:S(2)}) %collective-permute-start.10) | collective-permute-done | bytes 393248 | tf_op jit(solution)/shard_map/ppermute | solution.py:23
  70.0 2.1 %collective-permute-start.14 = (bf16[128,1536]{1,0:T(8,128)(2,1)S(1)}, bf16[128,1536]{1,0:T(8,128)(2,1)S(1)}, u32[]{:S(2)}, u32[]{:S(2)}) collective-permute-start(bf16[128,1536]{1,0:T(8,128)(2,1)S(1)} %get-tuple-element.68.refs_1_), channel_id=1, source_target_pairs={{0,3},{1,0},{2,1},{3,2},{4,7},{5,4},{6,5},{7,6},{8,11},{9,8},{10,9... | collective-permute-start | bytes 1179656 | tf_op jit(solution)/shard_map/ppermute | solution.py:23
  72.1 4.3 %collective-permute-done.13.refs_3_ = bf16[128,256]{1,0:T(8,128)(2,1)S(1)} collective-permute-done((bf16[128,256]{1,0:T(8,128)(2,1)S(1)}, bf16[128,256]{1,0:T(8,128)(2,1)S(1)}, u32[]{:S(2)}, u32[]{:S(2)}) %collective-permute-start.13) | collective-permute-done | bytes 65568 | tf_op jit(solution)/shard_map/ppermute | solution.py:39
  76.4 2.4 %feed_own.1 = (f32[128,384]{1,0:T(8,128)S(1)}, bf16[128,384]{1,0:T(8,128)(2,1)S(1)}, bf16[128,384]{1,0:T(8,128)(2,1)S(1)}, bf16[128,384]{1,0:T(8,128)(2,1)S(1)},...) custom-call(s32[3]{0:T(128)S(1)} %pad_add_fusion.1.place.refs_0_, ...), custom_call_target="tpu_custom_call" | custom-call | flops 2000000000 | bytes 10000000 | tf_op jit(solution)/shard_map/feed_own/pallas_call | solution.py:44
  84.0 4.7 %feed_near.1 = (f32[256,384]{1,0:T(8,128)S(1)}, bf16[384,384]{1,0:T(8,128)(2,1)S(1)}, bf16[384,384]{1,0:T(8,128)(2,1)S(1)}, bf16[384,384]{1,0:T(8,128)(2,1)S(1)}, bf16[64,256]{1,0:T(8,128)(2,1)}) custom-call(s32[3]{0:T(128)S(1)} %pad_add_fusion.1.place.refs_0_, bf16[128,1536]{1,0:T(8,128)(2,1)S(1)} %collective-permute-done.14.ahead.refs_1_, ...), custom_call_target="tpu_custom_call" | custom-call | flops 20000000000 | bytes 100000000 | tf_op jit(solution)/shard_map/feed_near/pallas_call | solution.py:44
  88.7 2.2 %collective-permute-start.18 = (bf16[384,384]{1,0:T(8,128)(2,1)S(1)}, bf16[384,384]{1,0:T(8,128)(2,1)S(1)}, u32[]{:S(2)}, u32[]{:S(2)}) collective-permute-start(bf16[384,384]{1,0:T(8,128)(2,1)S(1)} %get-tuple-element.86), channel_id=1, source_target_pairs={{0,2},{1,3},{2,0},{3,1},{4,6},{5,7},{6,4},{7,5},{8,10},{9,11},{10,... | collective-permute-start | bytes 884744 | tf_op jit(solution)/shard_map/ppermute | solution.py:23
  90.9 2.4 %feed_far.1 = (f32[128,384]{1,0:T(8,128)S(1)}, bf16[128,384]{1,0:T(8,128)(2,1)S(1)}, bf16[128,384]{1,0:T(8,128)(2,1)S(1)}, bf16[512,384]{1,0:T(8,128)(2,1)S(1)}) custom-call(s32[3]{0:T(128)S(1)} %pad_add_fusion.1.place.refs_0_, bf16[128,1536]{1,0:T(8,128)(2,1)S(1)} %collective-permute-done.17.refs_1_, bf16[384,384]{1,0:T(8,128)(2,1)S(1)} %get-tuple-element.84.refs_2_, ...), custom_call_target="tpu_custom_call" | custom-call | flops 2000000000 | bytes 10000000 | tf_op jit(solution)/shard_map/feed_far/pallas_call | solution.py:44
  93.4 2.0 %collective-permute-start.20 = (bf16[128,384]{1,0:T(8,128)(2,1)S(1)}, bf16[128,384]{1,0:T(8,128)(2,1)S(1)}, u32[]{:S(2)}, u32[]{:S(2)}) collective-permute-start(bf16[128,384]{1,0:T(8,128)(2,1)S(1)} %get-tuple-element.88), channel_id=1, source_target_pairs={{0,2},{1,3},{2,0},{3,1},{4,6},{5,7},{6,4},{7,5},{8,10},{9,11},{10,... | collective-permute-start | bytes 294920 | tf_op jit(solution)/shard_map/ppermute | solution.py:23
  95.4 2.1 %collective-permute-start.21 = (bf16[128,384]{1,0:T(8,128)(2,1)S(1)}, bf16[128,384]{1,0:T(8,128)(2,1)S(1)}, u32[]{:S(2)}, u32[]{:S(2)}) collective-permute-start(bf16[128,384]{1,0:T(8,128)(2,1)S(1)} %get-tuple-element.89), channel_id=1, source_target_pairs={{0,1},{1,2},{2,3},{3,0},{4,7},{5,4},{6,5},{7,6},{8,9},{9,10},{10,1... | collective-permute-start | bytes 294920 | tf_op jit(solution)/shard_map/ppermute | solution.py:34
  100.2 5.5 %collective-permute-done.19.early1 = bf16[384,384]{1,0:T(8,128)(2,1)S(1)} collective-permute-done((bf16[384,384]{1,0:T(8,128)(2,1)S(1)}, bf16[384,384]{1,0:T(8,128)(2,1)S(1)}, u32[]{:S(2)}, u32[]{:S(2)}) %collective-permute-start.19) | collective-permute-done | bytes 294944 | tf_op jit(solution)/shard_map/ppermute | solution.py:34
  (72 shorter events, 35.8 us)
Async XLA Ops:
  0.6 15.8 %collective-permute-start.1 = (bf16[512,384]{1,0:T(8,128)(2,1)}, bf16[512,384]{1,0:T(8,128)(2,1)S(1)}, u32[]{:S(2)}, u32[]{:S(2)}) collective-permute-start(bf16[512,384]{1,0:T(8,128)(2,1)} %source.1), channel_id=1, source_target_pairs={{0,2},{1,3},{2,0},{3,1},{4,6},{5,7},{6,4},{7,5},{8,10},{9,11},{10,... | collective-permute-start | bytes 1179656 | tf_op jit(solution)/shard_map/ppermute | solution.py:23
  3.9 18.2 %collective-permute-start = (bf16[512,384]{1,0:T(8,128)(2,1)}, bf16[512,384]{1,0:T(8,128)(2,1)S(1)}, u32[]{:S(2)}, u32[]{:S(2)}) collective-permute-start(bf16[512,384]{1,0:T(8,128)(2,1)} %source.1), channel_id=1, source_target_pairs={{0,3},{1,0},{2,1},{3,2},{4,7},{5,4},{6,5},{7,6},{8,11},{9,8},{10,9... | collective-permute-start | bytes 1179656 | tf_op jit(solution)/shard_map/ppermute | solution.py:23
  5.0 17.1 %collective-permute-start.2 = (bf16[512,384]{1,0:T(8,128)(2,1)}, bf16[512,384]{1,0:T(8,128)(2,1)S(1)}, u32[]{:S(2)}, u32[]{:S(2)}) collective-permute-start(bf16[512,384]{1,0:T(8,128)(2,1)} %source.1), channel_id=1, source_target_pairs={{0,1},{1,2},{2,3},{3,0},{4,5},{5,6},{6,7},{7,4},{8,9},{9,10},{10,1... | collective-permute-start | bytes 1179656 | tf_op jit(solution)/shard_map/ppermute | solution.py:23
  23.8 8.4 %collective-permute-start.3 = (bf16[256,128]{1,0:T(8,128)(2,1)S(1)}, bf16[256,128]{1,0:T(8,128)(2,1)S(1)}, u32[]{:S(2)}, u32[]{:S(2)}) collective-permute-start(bf16[256,128]{1,0:T(8,128)(2,1)S(1)} %get-tuple-element.54.a), channel_id=1, source_target_pairs={{0,8},{4,12},{8,16},{12,20},{16,24},{20,28},{24,32},{28,36},{32,40... | collective-permute-start | bytes 196616 | tf_op jit(solution)/shard_map/ppermute | solution.py:28
  32.3 7.0 %collective-permute-start.6 = (bf16[512,128]{1,0:T(8,128)(2,1)S(1)}, bf16[512,128]{1,0:T(8,128)(2,1)S(1)}, u32[]{:S(2)}, u32[]{:S(2)}) collective-permute-start(bf16[512,128]{1,0:T(8,128)(2,1)S(1)} %join.1.y0), channel_id=1, source_target_pairs={{0,1},{1,2},{2,3},{3,0},{4,5},{5,6},{6,7},{7,4},{8,9},{9,10},{10,1... | collective-permute-start | bytes 393224 | tf_op jit(solution)/shard_map/ppermute | solution.py:23
  33.7 8.5 %collective-permute-start.5 = (bf16[512,128]{1,0:T(8,128)(2,1)S(1)}, bf16[512,128]{1,0:T(8,128)(2,1)S(1)}, u32[]{:S(2)}, u32[]{:S(2)}) collective-permute-start(bf16[512,128]{1,0:T(8,128)(2,1)S(1)} %join.1.y0), channel_id=1, source_target_pairs={{0,2},{1,3},{2,0},{3,1},{4,6},{5,7},{6,4},{7,5},{8,10},{9,11},{10,... | collective-permute-start | bytes 393224 | tf_op jit(solution)/shard_map/ppermute | solution.py:23
  36.5 5.7 %collective-permute-start.4 = (bf16[512,128]{1,0:T(8,128)(2,1)S(1)}, bf16[512,128]{1,0:T(8,128)(2,1)S(1)}, u32[]{:S(2)}, u32[]{:S(2)}) collective-permute-start(bf16[512,128]{1,0:T(8,128)(2,1)S(1)} %join.1.y0), channel_id=1, source_target_pairs={{0,3},{1,0},{2,1},{3,2},{4,7},{5,4},{6,5},{7,6},{8,11},{9,8},{10,9... | collective-permute-start | bytes 393224 | tf_op jit(solution)/shard_map/ppermute | solution.py:23
  43.3 2.0 %collective-permute-start.7 = (bf16[1024,256]{1,0:T(8,128)(2,1)S(1)}, bf16[1024,256]{1,0:T(8,128)(2,1)S(1)}, u32[]{:S(2)}, u32[]{:S(2)}) collective-permute-start(bf16[1024,256]{1,0:T(8,128)(2,1)S(1)} %rotate.1.rows.mine), channel_id=1, source_target_pairs={{0,4},{4,0},{8,12},{12,8},{16,20},{20,16},{24,28},{28,24},{32,36},... | collective-permute-start | bytes 1572872 | tf_op jit(solution)/shard_map/ppermute | solution.py:39
  47.2 14.1 %collective-permute-start.9 = (bf16[128,1536]{1,0:T(8,128)(2,1)S(1)}, bf16[128,1536]{1,0:T(8,128)(2,1)S(1)}, u32[]{:S(2)}, u32[]{:S(2)}) collective-permute-start(bf16[128,1536]{1,0:T(8,128)(2,1)S(1)} %attend2.1), channel_id=1, source_target_pairs={{0,2},{1,3},{2,0},{3,1},{4,6},{5,7},{6,4},{7,5},{8,10},{9,11},{10,... | collective-permute-start | bytes 1179656 | tf_op jit(solution)/shard_map/ppermute | solution.py:23
  50.5 8.2 %collective-permute-start.8 = (bf16[512,256]{1,0:T(8,128)(2,1)S(1)}, bf16[512,256]{1,0:T(8,128)(2,1)S(1)}, u32[]{:S(2)}, u32[]{:S(2)}) collective-permute-start(bf16[512,256]{1,0:T(8,128)(2,1)S(1)} %get-tuple-element.63), channel_id=1, source_target_pairs={{0,32},{4,36},{8,40},{12,44},{16,48},{20,52},{24,56},{28,60},{32,0... | collective-permute-start | bytes 786440 | tf_op jit(solution)/shard_map/ppermute | solution.py:39
  52.6 15.7 %collective-permute-start.10 = (bf16[128,1536]{1,0:T(8,128)(2,1)S(1)}, bf16[128,1536]{1,0:T(8,128)(2,1)S(1)}, u32[]{:S(2)}, u32[]{:S(2)}) collective-permute-start(bf16[128,1536]{1,0:T(8,128)(2,1)S(1)} %attend1.1), channel_id=1, source_target_pairs={{0,1},{1,2},{2,3},{3,0},{4,5},{5,6},{6,7},{7,4},{8,9},{9,10},{10,1... | collective-permute-start | bytes 1179656 | tf_op jit(solution)/shard_map/ppermute | solution.py:23
  55.6 12.8 %collective-permute-start.11 = (bf16[128,1536]{1,0:T(8,128)(2,1)S(1)}, bf16[128,1536]{1,0:T(8,128)(2,1)S(1)}, u32[]{:S(2)}, u32[]{:S(2)}) collective-permute-start(bf16[128,1536]{1,0:T(8,128)(2,1)S(1)} %attend3.1), channel_id=1, source_target_pairs={{0,3},{1,0},{2,1},{3,2},{4,7},{5,4},{6,5},{7,6},{8,11},{9,8},{10,9... | collective-permute-start | bytes 1179656 | tf_op jit(solution)/shard_map/ppermute | solution.py:23
  58.6 17.7 %copy-start.2 = (bf16[1152,1536]{1,0:T(8,128)(2,1)S(1)}, bf16[1152,1536]{1,0:T(8,128)(2,1)}, u32[]{:S(2)}) copy-start(bf16[1152,1536]{1,0:T(8,128)(2,1)} %refs_5_.3) | copy-start | bytes 10616836
  60.6 7.8 %collective-permute-start.12 = (bf16[256,256]{1,0:T(8,128)(2,1)S(1)}, bf16[256,256]{1,0:T(8,128)(2,1)S(1)}, u32[]{:S(2)}, u32[]{:S(2)}) collective-permute-start(bf16[256,256]{1,0:T(8,128)(2,1)S(1)} %get-tuple-element.67), channel_id=1, source_target_pairs={{0,96},{4,100},{8,104},{12,108},{16,112},{20,116},{24,120},{28,124... | collective-permute-start | bytes 393224 | tf_op jit(solution)/shard_map/ppermute | solution.py:39
  68.8 12.3 %collective-permute-start.15 = (bf16[128,1536]{1,0:T(8,128)(2,1)S(1)}, bf16[128,1536]{1,0:T(8,128)(2,1)S(1)}, u32[]{:S(2)}, u32[]{:S(2)}) collective-permute-start(bf16[128,1536]{1,0:T(8,128)(2,1)S(1)} %get-tuple-element.68.refs_1_), channel_id=1, source_target_pairs={{0,1},{1,2},{2,3},{3,0},{4,5},{5,6},{6,7},{7,4},{8,9},{9,10},{10,1... | collective-permute-start | bytes 1179656 | tf_op jit(solution)/shard_map/ppermute | solution.py:23
  70.0 11.1 %collective-permute-start.14 = (bf16[128,1536]{1,0:T(8,128)(2,1)S(1)}, bf16[128,1536]{1,0:T(8,128)(2,1)S(1)}, u32[]{:S(2)}, u32[]{:S(2)}) collective-permute-start(bf16[128,1536]{1,0:T(8,128)(2,1)S(1)} %get-tuple-element.68.refs_1_), channel_id=1, source_target_pairs={{0,3},{1,0},{2,1},{3,2},{4,7},{5,4},{6,5},{7,6},{8,11},{9,8},{10,9... | collective-permute-start | bytes 1179656 | tf_op jit(solution)/shard_map/ppermute | solution.py:23
  72.1 4.3 %collective-permute-start.13 = (bf16[128,256]{1,0:T(8,128)(2,1)S(1)}, bf16[128,256]{1,0:T(8,128)(2,1)S(1)}, u32[]{:S(2)}, u32[]{:S(2)}) collective-permute-start(bf16[128,256]{1,0:T(8,128)(2,1)S(1)} %get-tuple-element.70), channel_id=1, source_target_pairs={{0,8},{4,12},{8,0},{12,4},{16,24},{20,28},{24,16},{28,20},{32,40},... | collective-permute-start | bytes 196616 | tf_op jit(solution)/shard_map/ppermute | solution.py:39
  78.8 5.2 %collective-permute-start.16 = (bf16[64,256]{1,0:T(8,128)(2,1)S(1)}, bf16[64,256]{1,0:T(8,128)(2,1)S(1)}, u32[]{:S(2)}, u32[]{:S(2)}) collective-permute-start(bf16[64,256]{1,0:T(8,128)(2,1)S(1)} %get-tuple-element.78), channel_id=1, source_target_pairs={{0,24},{4,28},{8,16},{12,20},{16,8},{20,12},{24,0},{28,4},{32,56},... | collective-permute-start | bytes 98312 | tf_op jit(solution)/shard_map/ppermute | solution.py:39
  81.7 9.2 %collective-permute-start.17 = (bf16[128,1536]{1,0:T(8,128)(2,1)S(1)}, bf16[128,1536]{1,0:T(8,128)(2,1)S(1)}, u32[]{:S(2)}, u32[]{:S(2)}) collective-permute-start(bf16[128,1536]{1,0:T(8,128)(2,1)S(1)} %pick.1), channel_id=1, source_target_pairs={{0,1},{1,2},{2,3},{3,0},{4,7},{5,4},{6,5},{7,6},{8,9},{9,10},{10,1... | collective-permute-start | bytes 1179656 | tf_op jit(solution)/shard_map/ppermute | solution.py:34
  88.7 11.5 %collective-permute-start.18 = (bf16[384,384]{1,0:T(8,128)(2,1)S(1)}, bf16[384,384]{1,0:T(8,128)(2,1)S(1)}, u32[]{:S(2)}, u32[]{:S(2)}) collective-permute-start(bf16[384,384]{1,0:T(8,128)(2,1)S(1)} %get-tuple-element.86), channel_id=1, source_target_pairs={{0,2},{1,3},{2,0},{3,1},{4,6},{5,7},{6,4},{7,5},{8,10},{9,11},{10,... | collective-permute-start | bytes 884744 | tf_op jit(solution)/shard_map/ppermute | solution.py:23
  90.9 14.8 %collective-permute-start.19 = (bf16[384,384]{1,0:T(8,128)(2,1)S(1)}, bf16[384,384]{1,0:T(8,128)(2,1)S(1)}, u32[]{:S(2)}, u32[]{:S(2)}) collective-permute-start(bf16[384,384]{1,0:T(8,128)(2,1)S(1)} %get-tuple-element.87), channel_id=1, source_target_pairs={{0,1},{1,2},{2,3},{3,0},{4,7},{5,4},{6,5},{7,6},{8,9},{9,10},{10,1... | collective-permute-start | bytes 884744 | tf_op jit(solution)/shard_map/ppermute | solution.py:34
  93.4 14.7 %collective-permute-start.20 = (bf16[128,384]{1,0:T(8,128)(2,1)S(1)}, bf16[128,384]{1,0:T(8,128)(2,1)S(1)}, u32[]{:S(2)}, u32[]{:S(2)}) collective-permute-start(bf16[128,384]{1,0:T(8,128)(2,1)S(1)} %get-tuple-element.88), channel_id=1, source_target_pairs={{0,2},{1,3},{2,0},{3,1},{4,6},{5,7},{6,4},{7,5},{8,10},{9,11},{10,... | collective-permute-start | bytes 294920 | tf_op jit(solution)/shard_map/ppermute | solution.py:23
  95.4 13.5 %collective-permute-start.21 = (bf16[128,384]{1,0:T(8,128)(2,1)S(1)}, bf16[128,384]{1,0:T(8,128)(2,1)S(1)}, u32[]{:S(2)}, u32[]{:S(2)}) collective-permute-start(bf16[128,384]{1,0:T(8,128)(2,1)S(1)} %get-tuple-element.89), channel_id=1, source_target_pairs={{0,1},{1,2},{2,3},{3,0},{4,7},{5,4},{6,5},{7,6},{8,9},{9,10},{10,1... | collective-permute-start | bytes 294920 | tf_op jit(solution)/shard_map/ppermute | solution.py:34
  97.5 11.3 %collective-permute-start.22 = (bf16[512,384]{1,0:T(8,128)(2,1)S(1)}, bf16[512,384]{1,0:T(8,128)(2,1)S(1)}, u32[]{:S(2)}, u32[]{:S(2)}) collective-permute-start(bf16[512,384]{1,0:T(8,128)(2,1)S(1)} %get-tuple-element.90), channel_id=1, source_target_pairs={{0,3},{1,0},{2,1},{3,2},{4,5},{5,6},{6,7},{7,4},{8,11},{9,8},{10,9... | collective-permute-start | bytes 1179656 | tf_op jit(solution)/shard_map/ppermute | solution.py:34
  (5 other events, 50.3 us)

commit v7 on v6

--- a/solution.py
+++ b/solution.py
@@ -37,6 +37,10 @@
 def from_partner(block, bits):
     n = lax.axis_size("seq")
     return lax.ppermute(block, "seq", [(i, i ^ bits) for i in range(n)])
+
+
+def lag(slot, core):
+    return (0, 3 - 2 * core, 2, 1 + 2 * core)[slot]
 
 
 def run(body, outs, name, scalars, arrays, scratch=(), vmem=16 << 20, flops=2_000_000_000):
@@ -68,7 +72,7 @@
 
 
 def norm_kv_body(place, x0, x1, x2, x3, gain, wkv, n_out, kv_out, kept):
-    f = place[0]
+    f, core = place[0], place[2]
     xs = (x0, x1, x2, x3)
     tokens, width = x0.shape
     step = 128
@@ -81,16 +85,16 @@
             total = part if total is None else total + part
         scale = lax.rsqrt(total / (width * 4) + epsilon)
         for d, x in enumerate(xs):
-            g = lax.rem(f + d, 4)
+            g = lax.rem(f + lag(d, core), 4)
             v = x[rows, :].astype(f32) * scale * gain[pl.ds(g, 1), :]
             n_out[d, rows, :] = v.astype(bf16)
     own = kept.shape[1]
     own_rows = pl.ds(pl.multiple_of(f * own, own), own)
     for d, x in enumerate(xs):
-        kept[lax.rem(f + d, 4)] = x[own_rows, :]
+        kept[lax.rem(f + lag(d, core), 4)] = x[own_rows, :]
     acc = None
     for d in range(4):
-        g = lax.rem(f + d, 4)
+        g = lax.rem(f + lag(d, core), 4)
         start = pl.multiple_of(g * width, 128)
         part = dot(n_out[d], wkv[pl.ds(start, width), :])
         acc = part if acc is None else acc + part
@@ -100,11 +104,11 @@
 
 
 def query_body(place, n_in, wq, cosine, sine, q_out):
-    f = place[0]
+    f, core = place[0], place[2]
     width = n_in.shape[2]
     acc = None
     for d in range(4):
-        g = lax.rem(f + d, 4)
+        g = lax.rem(f + lag(d, core), 4)
         start = pl.multiple_of(g * width, 128)
         part = dot(n_in[d], wq[pl.ds(start, width), :])
         acc = part if acc is None else acc + part
@@ -152,7 +156,7 @@
         rows = pl.ds(pl.multiple_of(slot * tokens, tokens), tokens)
         win[rows, :] = part[row * tokens : (row + 1) * tokens, :]
     step = 128
-    b = lax.rem(f + d, 4)
+    b = lax.rem(f + (d if d % 2 == 0 else d + (2 - d) * 2 * core), 4)
     row0 = pl.multiple_of(b * step, step)
     key0 = pl.multiple_of(core * tokens + b * step, step)
     pos = first + row0 + lax.broadcasted_iota(jnp.int32, (step, 1), 0)
@@ -201,16 +205,6 @@
     for g in range(4):
         cols = slice(g * width, (g + 1) * width)
         n_out[:, cols] = (res_out[g] * scale * gain[:, cols]).astype(bf16)
-
-
-def pick_body(place, ahead, behind, out):
-    @pl.when(place[2] == 0)
-    def _():
-        out[...] = behind[...]
-
-    @pl.when(place[2] == 1)
-    def _():
-        out[...] = ahead[...]
 
 
 def gelu(x):
@@ -257,31 +251,27 @@
 
 def early_sum_body(place, own, both, far, early2, early1, out):
     step = own.shape[0]
+    core = place[2]
+    near, other = lag(1, core), lag(3, core)
     out[0] = own[...]
-    out[1] = both[:step]
+    out[near] = both[:step]
     out[2] = far[...]
-    out[3] = both[step:]
-    side = 3 - 2 * place[2]
-    for row, shift in enumerate((0, 1, 3)):
+    out[other] = both[step:]
+    for row, shift in enumerate((0, near, other)):
         rows = slice(row * step, row * step + step)
-        r = (shift + 2) % 4
+        r = lax.rem(shift + 2, 4)
         out[r] = out[r] + early2[rows].astype(f32)
-        r = lax.rem(shift + side, 4)
+        r = lax.rem(shift + near, 4)
         out[r] = out[r] + early1[rows].astype(f32)
 
 
 def finish_body(place, some, late2, late1, whole, out):
     f, core = place[0], place[2]
     step = some.shape[1]
-    side = 1 + 2 * core
-    for row, shift in enumerate((0, 1, 3, 2)):
-        r = lax.rem(shift + side, 4)
+    for row, (r, more) in enumerate(((lag(3, core), late1), (0, late2), (2, None), (lag(1, core), None))):
         total = some[r] + whole[row * step : row * step + step].astype(f32)
-        if shift == 0:
-            total = total + late1[...].astype(f32)
-        elif shift != 2:
-            mine = core == (0 if shift == 3 else 1)
-            total = total + jnp.where(mine, late2[...].astype(f32), 0.0)
+        if more is not None:
+            total = total + more[...].astype(f32)
         rows = pl.ds(pl.multiple_of(lax.rem(f + r, 4) * step, step), step)
         out[rows, :] = total.astype(bf16)
 
@@ -319,9 +309,9 @@
     sds = jax.ShapeDtypeStruct
 
     x0 = run(copy_body, sds(hidden.shape, bf16), "take_own", [], [hidden])
+    x1 = to_side(hidden, (1, 3))
     x2 = from_peer(hidden, 2)
-    x1 = from_peer(hidden, 1)
-    x3 = from_peer(hidden, 3)
+    x3 = to_side(hidden, (3, 1))
 
     offsets = jnp.cumsum(lengths) - lengths
     ticks = jnp.arange(tokens, dtype=jnp.int32)
@@ -430,8 +420,8 @@
     )
     landed = from_partner(image_sent, 8)
 
-    p1 = from_peer(attend(1, bf16), 3)
-    p3 = from_peer(attend(3, bf16), 1)
+    p1 = to_side(attend(1, bf16), (1, 3))
+    p3 = to_side(attend(3, bf16), (3, 1))
     p0, stay, go = attend(0, f32, [image_kept, landed])
     landed = from_partner(go, 24)
     residual, normed2, go, stay = run(
@@ -439,11 +429,11 @@
         [sds((4, step, width), f32), sds((step, full), bf16), *halves(stay)],
         "residual",
         [],
-        [kept, p0, p2, p1, p3, gain2, stay, landed],
+        [kept, p0, p1, p2, p3, gain2, stay, landed],
     )
     landed = from_partner(go, 2)
-    m1 = from_peer(normed2, 1)
-    m3 = from_peer(normed2, 3)
+    m1 = to_side(normed2, (1, 3))
+    m3 = to_side(normed2, (3, 1))
     hidden_units = gate_weight.shape[1]
 
     def feed(name, blocks, res=(), before=(), cached=()):
@@ -467,10 +457,8 @@
 
     own0, *own_sent, stay, go = feed("feed_own", [normed2], res=[residual], cached=[stay, landed])
     landed = from_partner(go, 6)
-    m1, m3, _ = lax.optimization_barrier((m1, m3, own0))
-    passed = run(pick_body, sds((step, full), bf16), "pick", [place], [m1, m3])
-    m1, m3, passed = lax.optimization_barrier((m1, m3, passed))
-    m2 = to_side(passed, (1, 3))
+    m1, _ = lax.optimization_barrier((m1, own0))
+    m2 = to_side(m1, (1, 3))
     both0, early1, early2, early3, cache = feed(
         "feed_near", [m1, m3], before=list(zip((1, 2, 3), own_sent)), cached=[stay, landed]
     )

time: 111 us -> 110 us (level)
  waiting for transfers between devices: 38.6 us -> 36.2 us
  starting transfers between devices: 34.8 us -> 36.3 us
    ppermute x13 -> x7, waiting for transfers between devices: 21.6 us -> 10.2 us  [from_peer(): lax.ppermute(block, 'feat', [(i, (i - distance) % n) for i in range(n)])]
    ppermute x4 -> x10, starting transfers between devices: 4.34 us -> 14.8 us  [to_side(): return lax.ppermute(block, ('seq', 'feat'), route)]
    ppermute x13 -> x7, starting transfers between devices: 24.4 us -> 15.1 us  [from_peer(): lax.ppermute(block, 'feat', [(i, (i - distance) % n) for i in range(n)])]
    ppermute x4 -> x10, waiting for transfers between devices: 6.26 us -> 13.5 us  [to_side(): return lax.ppermute(block, ('seq', 'feat'), route)]
    ppermute x5, waiting for transfers between devices: 8.03 us -> 9.77 us  [from_partner(): return lax.ppermute(block, 'seq', [(i, i ^ bits) for i in range(n)])]
    pallas_call x17 -> x16, Pallas kernels: 25.6 us -> 25 us  [run(): pl.pallas_call(body, out_shape=outs, in_specs=[SM] * len(scalars) + [VM]...]
  transfers between devices with their start and end apart: 23 -> 23, of which waited for: 14 -> 15; matrix products, arithmetic and copies ran while one was open for 9% -> 9% of each run, Pallas kernels for 17% -> 17%
where the time goes in v7:
time: 110 us; the launch traced here: 109 us
  starting transfers between devices  36.3 us (33%)
  waiting for transfers between devices  36.2 us (33%)
  Pallas kernels  25 us (23%)
  other arithmetic  7.73 us (7%)
  local copies, waits for them, and re-layouts  2.61 us (2%)
    pallas_call x16, Pallas kernels, run(): pl.pallas_call(body, out_shape=outs, in_specs=[SM] * len(scalars) + [VM]...  25 us
    ppermute x7, starting transfers between devices, from_peer(): lax.ppermute(block, 'feat', [(i, (i - distance) % n) for i in range(n)])  15.1 us
    ppermute x10, starting transfers between devices, to_side(): return lax.ppermute(block, ('seq', 'feat'), route)  14.8 us
    ppermute x10, waiting for transfers between devices, to_side(): return lax.ppermute(block, ('seq', 'feat'), route)  13.5 us
    ppermute x7, waiting for transfers between devices, from_peer(): lax.ppermute(block, 'feat', [(i, (i - distance) % n) for i in range(n)])  10.2 us
    ppermute x5, waiting for transfers between devices, from_partner(): return lax.ppermute(block, 'seq', [(i, i ^ bits) for i in range(n)])  9.77 us
    ppermute x1, starting transfers between devices, from_earlier(): lax.ppermute(block, 'seq', [(i - distance, i) for i in range(distance, n)])  3.83 us
    neg x1, other arithmetic, shards(): sine = jnp.concatenate([-sine, sine], axis=1)  2.96 us
  transfers between devices with their start and end apart: 23, of which 15 were waited for; matrix products, arithmetic and copies ran while one was open for 9% of the time, Pallas kernels for 17%

profile of v7, /device:TPU:6, one launch (start us, length us, event | category | flops | bytes accessed | tf_op | source)
XLA Modules:
  0.0 108.7 jit_solution(12883403063976610901)
XLA Ops:
  0.6 3.3 %collective-permute-start.1 = (bf16[512,384]{1,0:T(8,128)(2,1)}, bf16[512,384]{1,0:T(8,128)(2,1)S(1)}, u32[]{:S(2)}, u32[]{:S(2)}) collective-permute-start(bf16[512,384]{1,0:T(8,128)(2,1)} %source.1), channel_id=1, source_target_pairs={{0,2},{1,3},{2,0},{3,1},{4,6},{5,7},{6,4},{7,5},{8,10},{9,11},{10,... | collective-permute-start | bytes 1179656 | tf_op jit(solution)/shard_map/ppermute | solution.py:23
  4.6 2.6 %collective-permute-start.2 = (bf16[512,384]{1,0:T(8,128)(2,1)}, bf16[512,384]{1,0:T(8,128)(2,1)S(1)}, u32[]{:S(2)}, u32[]{:S(2)}) collective-permute-start(bf16[512,384]{1,0:T(8,128)(2,1)} %source.1), channel_id=1, source_target_pairs={{0,3},{1,0},{2,1},{3,2},{4,5},{5,6},{6,7},{7,4},{8,11},{9,8},{10,9... | collective-permute-start | bytes 1179656 | tf_op jit(solution)/shard_map/ppermute | solution.py:34
  12.2 3.0 %fusion = (f32[1024,64]{1,0:T(8,128)S(1)}, f32[1024,64]{1,0:T(8,128)}, f32[1024,64]{1,0:T(8,128)S(1)}) fusion(f32[64]{0:T(128)S(1)} %multiply_exponential_fusion, f32[1024]{0:T(1024)S(1)} %slice_convert_fusion), kind=kLoop, calls=%fused_computation.6 | loop fusion | flops 131072 | bytes 790784 | tf_op jit(solution)/shard_map/neg | solution.py:330
  17.6 4.1 %collective-permute-done.x1 = bf16[512,384]{1,0:T(8,128)(2,1)S(1)} collective-permute-done((bf16[512,384]{1,0:T(8,128)(2,1)}, bf16[512,384]{1,0:T(8,128)(2,1)S(1)}, u32[]{:S(2)}, u32[]{:S(2)}) %collective-permute-start) | collective-permute-done | bytes 393248 | tf_op jit(solution)/shard_map/ppermute | solution.py:34
  23.8 3.8 %collective-permute-start.3 = (bf16[256,128]{1,0:T(8,128)(2,1)S(1)}, bf16[256,128]{1,0:T(8,128)(2,1)S(1)}, u32[]{:S(2)}, u32[]{:S(2)}) collective-permute-start(bf16[256,128]{1,0:T(8,128)(2,1)S(1)} %get-tuple-element.50.a), channel_id=1, source_target_pairs={{0,8},{4,12},{8,16},{12,20},{16,24},{20,28},{24,32},{28,36},{32,40... | collective-permute-start | bytes 196616 | tf_op jit(solution)/shard_map/ppermute | solution.py:28
  27.6 1.8 %queries.1.q = bf16[512,384]{1,0:T(8,128)(2,1)S(1)} custom-call(s32[3]{0:T(128)S(1)} %pad_add_fusion.1.place.refs_0_, bf16[4,512,384]{2,1,0:T(8,128)(2,1)S(1)} %get-tuple-element.51.n_in, bf16[1536,384]{1,0:T(8,128)(2,1)S(1)} %copy-done.3, f32[1024,128]{1,0:T(8,128)S(1)} %pad_maximum_fusion.cosine, f32[1024,128]{1,0:T(8,128)S(1)} %pad_maximum_fusion.1.sine), custom_call_target="tpu_custom_call" | custom-call | flops 2000000000 | bytes 10000000 | tf_op jit(solution)/shard_map/queries/pallas_call | solution.py:48
  29.5 2.8 %collective-permute-done.3.b = bf16[256,128]{1,0:T(8,128)(2,1)S(1)} collective-permute-done((bf16[256,128]{1,0:T(8,128)(2,1)S(1)}, bf16[256,128]{1,0:T(8,128)(2,1)S(1)}, u32[]{:S(2)}, u32[]{:S(2)}) %collective-permute-start.3) | collective-permute-done | bytes 65568 | tf_op jit(solution)/shard_map/ppermute | solution.py:28
  33.7 2.8 %collective-permute-start.5 = (bf16[512,128]{1,0:T(8,128)(2,1)S(1)}, bf16[512,128]{1,0:T(8,128)(2,1)S(1)}, u32[]{:S(2)}, u32[]{:S(2)}) collective-permute-start(bf16[512,128]{1,0:T(8,128)(2,1)S(1)} %join.1.y0), channel_id=1, source_target_pairs={{0,2},{1,3},{2,0},{3,1},{4,6},{5,7},{6,4},{7,5},{8,10},{9,11},{10,... | collective-permute-start | bytes 393224 | tf_op jit(solution)/shard_map/ppermute | solution.py:23
  39.2 2.9 %collective-permute-done.5.y2 = bf16[512,128]{1,0:T(8,128)(2,1)S(1)} collective-permute-done((bf16[512,128]{1,0:T(8,128)(2,1)S(1)}, bf16[512,128]{1,0:T(8,128)(2,1)S(1)}, u32[]{:S(2)}, u32[]{:S(2)}) %collective-permute-start.5) | collective-permute-done | bytes 131104 | tf_op jit(solution)/shard_map/ppermute | solution.py:23
  43.4 1.9 %collective-permute-done.7.sibling.theirs = bf16[1024,256]{1,0:T(8,128)(2,1)S(1)} collective-permute-done((bf16[1024,256]{1,0:T(8,128)(2,1)S(1)}, bf16[1024,256]{1,0:T(8,128)(2,1)S(1)}, u32[]{:S(2)}, u32[]{:S(2)}) %collective-permute-start.7) | collective-permute-done | bytes 524320 | tf_op jit(solution)/shard_map/ppermute | solution.py:39
  45.3 1.9 %attend1.1 = bf16[128,1536]{1,0:T(8,128)(2,1)S(1)} custom-call(s32[3]{0:T(128)S(1)} %pad_add_fusion.1.place.refs_0_, s32[8]{0:T(128)S(1)} %bitcast_subtract_fusion.offsets, bf16[512,384]{1,0:T(8,128)(2,1)S(1)} %queries.1.q, bf16[1024,256]{1,0:T(8,128)(2,1)S(1)} %rotate.1.rows.mine, bf16[1024,256]{1,0:T(8,128)(2,1)S(1)} %collective-permute-done.7.sibling.theirs, ...), custom_call_target="tpu_custom_call" | custom-call | flops 2000000000 | bytes 10000000 | tf_op jit(solution)/shard_map/attend1/pallas_call | solution.py:48
  49.4 1.9 %attend2.1 = bf16[128,1536]{1,0:T(8,128)(2,1)S(1)} custom-call(s32[3]{0:T(128)S(1)} %pad_add_fusion.1.place.refs_0_, s32[8]{0:T(128)S(1)} %bitcast_subtract_fusion.offsets, bf16[512,384]{1,0:T(8,128)(2,1)S(1)} %queries.1.q, bf16[1024,256]{1,0:T(8,128)(2,1)S(1)} %rotate.1.rows.mine, bf16[1024,256]{1,0:T(8,128)(2,1)S(1)} %collective-permute-done.7.sibling.theirs, ...), custom_call_target="tpu_custom_call" | custom-call | flops 2000000000 | bytes 10000000 | tf_op jit(solution)/shard_map/attend2/pallas_call | solution.py:48
  51.3 3.3 %collective-permute-start.10 = (bf16[128,1536]{1,0:T(8,128)(2,1)S(1)}, bf16[128,1536]{1,0:T(8,128)(2,1)S(1)}, u32[]{:S(2)}, u32[]{:S(2)}) collective-permute-start(bf16[128,1536]{1,0:T(8,128)(2,1)S(1)} %attend2.1), channel_id=1, source_target_pairs={{0,2},{1,3},{2,0},{3,1},{4,6},{5,7},{6,4},{7,5},{8,10},{9,11},{10,... | collective-permute-start | bytes 1179656 | tf_op jit(solution)/shard_map/ppermute | solution.py:23
  54.6 1.9 %attend3.1 = bf16[128,1536]{1,0:T(8,128)(2,1)S(1)} custom-call(s32[3]{0:T(128)S(1)} %pad_add_fusion.1.place.refs_0_, s32[8]{0:T(128)S(1)} %bitcast_subtract_fusion.offsets, bf16[512,384]{1,0:T(8,128)(2,1)S(1)} %queries.1.q, bf16[1024,256]{1,0:T(8,128)(2,1)S(1)} %rotate.1.rows.mine, bf16[1024,256]{1,0:T(8,128)(2,1)S(1)} %collective-permute-done.7.sibling.theirs, ...), custom_call_target="tpu_custom_call" | custom-call | flops 2000000000 | bytes 10000000 | tf_op jit(solution)/shard_map/attend3/pallas_call | solution.py:48
  58.1 1.9 %attend0.1 = (f32[128,1536]{1,0:T(8,128)S(1)}, bf16[256,256]{1,0:T(8,128)(2,1)S(1)}, bf16[256,256]{1,0:T(8,128)(2,1)S(1)}) custom-call(s32[3]{0:T(128)S(1)} %pad_add_fusion.1.place.refs_0_, s32[8]{0:T(128)S(1)} %bitcast_subtract_fusion.offsets, bf16[512,384]{1,0:T(8,128)(2,1)S(1)} %queries.1.q, bf16[1024,256]{1,0:T(8,128)(2,1)S(1)} %rotate.1.rows.mine, ...), custom_call_target="tpu_custom_call" | custom-call | flops 2000000000 | bytes 10000000 | tf_op jit(solution)/shard_map/attend0/pallas_call | solution.py:48
  61.0 4.9 %collective-permute-done.10.p2 = bf16[128,1536]{1,0:T(8,128)(2,1)S(1)} collective-permute-done((bf16[128,1536]{1,0:T(8,128)(2,1)S(1)}, bf16[128,1536]{1,0:T(8,128)(2,1)S(1)}, u32[]{:S(2)}, u32[]{:S(2)}) %collective-permute-start.10) | collective-permute-done | bytes 393248 | tf_op jit(solution)/shard_map/ppermute | solution.py:23
  69.4 1.9 %collective-permute-start.15 = (bf16[128,1536]{1,0:T(8,128)(2,1)S(1)}, bf16[128,1536]{1,0:T(8,128)(2,1)S(1)}, u32[]{:S(2)}, u32[]{:S(2)}) collective-permute-start(bf16[128,1536]{1,0:T(8,128)(2,1)S(1)} %get-tuple-element.64.refs_1_), channel_id=1, source_target_pairs={{0,3},{1,0},{2,1},{3,2},{4,5},{5,6},{6,7},{7,4},{8,11},{9,8},{10,9... | collective-permute-start | bytes 1179656 | tf_op jit(solution)/shard_map/ppermute | solution.py:34
  71.3 4.3 %collective-permute-done.13.refs_3_ = bf16[128,256]{1,0:T(8,128)(2,1)S(1)} collective-permute-done((bf16[128,256]{1,0:T(8,128)(2,1)S(1)}, bf16[128,256]{1,0:T(8,128)(2,1)S(1)}, u32[]{:S(2)}, u32[]{:S(2)}) %collective-permute-start.13) | collective-permute-done | bytes 65568 | tf_op jit(solution)/shard_map/ppermute | solution.py:39
  75.6 2.4 %feed_own.1 = (f32[128,384]{1,0:T(8,128)S(1)}, bf16[128,384]{1,0:T(8,128)(2,1)S(1)}, bf16[128,384]{1,0:T(8,128)(2,1)S(1)}, bf16[128,384]{1,0:T(8,128)(2,1)S(1)},...) custom-call(s32[3]{0:T(128)S(1)} %pad_add_fusion.1.place.refs_0_, ...), custom_call_target="tpu_custom_call" | custom-call | flops 2000000000 | bytes 10000000 | tf_op jit(solution)/shard_map/feed_own/pallas_call | solution.py:48
  79.9 3.4 %collective-permute-done.16.refs_4_ = bf16[64,256]{1,0:T(8,128)(2,1)S(1)} collective-permute-done((bf16[64,256]{1,0:T(8,128)(2,1)S(1)}, bf16[64,256]{1,0:T(8,128)(2,1)S(1)}, u32[]{:S(2)}, u32[]{:S(2)}) %collective-permute-start.16) | collective-permute-done | bytes 32800 | tf_op jit(solution)/shard_map/ppermute | solution.py:39
  83.2 4.7 %feed_near.1 = (f32[256,384]{1,0:T(8,128)S(1)}, bf16[384,384]{1,0:T(8,128)(2,1)S(1)}, bf16[384,384]{1,0:T(8,128)(2,1)S(1)}, bf16[384,384]{1,0:T(8,128)(2,1)S(1)}, bf16[64,256]{1,0:T(8,128)(2,1)}) custom-call(s32[3]{0:T(128)S(1)} %pad_add_fusion.1.place.refs_0_, bf16[128,1536]{1,0:T(8,128)(2,1)S(1)} %collective-permute-done.14.refs_1_, ...), custom_call_target="tpu_custom_call" | custom-call | flops 20000000000 | bytes 100000000 | tf_op jit(solution)/shard_map/feed_near/pallas_call | solution.py:48
  90.9 2.4 %feed_far.1 = (f32[128,384]{1,0:T(8,128)S(1)}, bf16[128,384]{1,0:T(8,128)(2,1)S(1)}, bf16[128,384]{1,0:T(8,128)(2,1)S(1)}, bf16[512,384]{1,0:T(8,128)(2,1)S(1)}) custom-call(s32[3]{0:T(128)S(1)} %pad_add_fusion.1.place.refs_0_, bf16[128,1536]{1,0:T(8,128)(2,1)S(1)} %collective-permute-done.17.refs_1_, bf16[384,384]{1,0:T(8,128)(2,1)S(1)} %get-tuple-element.76.refs_2_, ...), custom_call_target="tpu_custom_call" | custom-call | flops 2000000000 | bytes 10000000 | tf_op jit(solution)/shard_map/feed_far/pallas_call | solution.py:48
  96.0 2.2 %collective-permute-start.22 = (bf16[512,384]{1,0:T(8,128)(2,1)S(1)}, bf16[512,384]{1,0:T(8,128)(2,1)S(1)}, u32[]{:S(2)}, u32[]{:S(2)}) collective-permute-start(bf16[512,384]{1,0:T(8,128)(2,1)S(1)} %get-tuple-element.82), channel_id=1, source_target_pairs={{0,3},{1,0},{2,1},{3,2},{4,5},{5,6},{6,7},{7,4},{8,11},{9,8},{10,9... | collective-permute-start | bytes 1179656 | tf_op jit(solution)/shard_map/ppermute | solution.py:34
  98.2 6.2 %collective-permute-done.19.early1 = bf16[384,384]{1,0:T(8,128)(2,1)S(1)} collective-permute-done((bf16[384,384]{1,0:T(8,128)(2,1)S(1)}, bf16[384,384]{1,0:T(8,128)(2,1)S(1)}, u32[]{:S(2)}, u32[]{:S(2)}) %collective-permute-start.19) | collective-permute-done | bytes 294944 | tf_op jit(solution)/shard_map/ppermute | solution.py:34
  (71 shorter events, 35.6 us)
Async XLA Ops:
  0.6 17.0 %collective-permute-start.1 = (bf16[512,384]{1,0:T(8,128)(2,1)}, bf16[512,384]{1,0:T(8,128)(2,1)S(1)}, u32[]{:S(2)}, u32[]{:S(2)}) collective-permute-start(bf16[512,384]{1,0:T(8,128)(2,1)} %source.1), channel_id=1, source_target_pairs={{0,2},{1,3},{2,0},{3,1},{4,6},{5,7},{6,4},{7,5},{8,10},{9,11},{10,... | collective-permute-start | bytes 1179656 | tf_op jit(solution)/shard_map/ppermute | solution.py:23
  3.9 17.8 %collective-permute-start = (bf16[512,384]{1,0:T(8,128)(2,1)}, bf16[512,384]{1,0:T(8,128)(2,1)S(1)}, u32[]{:S(2)}, u32[]{:S(2)}) collective-permute-start(bf16[512,384]{1,0:T(8,128)(2,1)} %source.1), channel_id=1, source_target_pairs={{0,1},{1,2},{2,3},{3,0},{4,7},{5,4},{6,5},{7,6},{8,9},{9,10},{10,1... | collective-permute-start | bytes 1179656 | tf_op jit(solution)/shard_map/ppermute | solution.py:34
  4.6 17.5 %collective-permute-start.2 = (bf16[512,384]{1,0:T(8,128)(2,1)}, bf16[512,384]{1,0:T(8,128)(2,1)S(1)}, u32[]{:S(2)}, u32[]{:S(2)}) collective-permute-start(bf16[512,384]{1,0:T(8,128)(2,1)} %source.1), channel_id=1, source_target_pairs={{0,3},{1,0},{2,1},{3,2},{4,5},{5,6},{6,7},{7,4},{8,11},{9,8},{10,9... | collective-permute-start | bytes 1179656 | tf_op jit(solution)/shard_map/ppermute | solution.py:34
  23.8 8.4 %collective-permute-start.3 = (bf16[256,128]{1,0:T(8,128)(2,1)S(1)}, bf16[256,128]{1,0:T(8,128)(2,1)S(1)}, u32[]{:S(2)}, u32[]{:S(2)}) collective-permute-start(bf16[256,128]{1,0:T(8,128)(2,1)S(1)} %get-tuple-element.50.a), channel_id=1, source_target_pairs={{0,8},{4,12},{8,16},{12,20},{16,24},{20,28},{24,32},{28,36},{32,40... | collective-permute-start | bytes 196616 | tf_op jit(solution)/shard_map/ppermute | solution.py:28
  32.3 7.0 %collective-permute-start.6 = (bf16[512,128]{1,0:T(8,128)(2,1)S(1)}, bf16[512,128]{1,0:T(8,128)(2,1)S(1)}, u32[]{:S(2)}, u32[]{:S(2)}) collective-permute-start(bf16[512,128]{1,0:T(8,128)(2,1)S(1)} %join.1.y0), channel_id=1, source_target_pairs={{0,1},{1,2},{2,3},{3,0},{4,5},{5,6},{6,7},{7,4},{8,9},{9,10},{10,1... | collective-permute-start | bytes 393224 | tf_op jit(solution)/shard_map/ppermute | solution.py:23
  33.7 8.5 %collective-permute-start.5 = (bf16[512,128]{1,0:T(8,128)(2,1)S(1)}, bf16[512,128]{1,0:T(8,128)(2,1)S(1)}, u32[]{:S(2)}, u32[]{:S(2)}) collective-permute-start(bf16[512,128]{1,0:T(8,128)(2,1)S(1)} %join.1.y0), channel_id=1, source_target_pairs={{0,2},{1,3},{2,0},{3,1},{4,6},{5,7},{6,4},{7,5},{8,10},{9,11},{10,... | collective-permute-start | bytes 393224 | tf_op jit(solution)/shard_map/ppermute | solution.py:23
  36.5 5.7 %collective-permute-start.4 = (bf16[512,128]{1,0:T(8,128)(2,1)S(1)}, bf16[512,128]{1,0:T(8,128)(2,1)S(1)}, u32[]{:S(2)}, u32[]{:S(2)}) collective-permute-start(bf16[512,128]{1,0:T(8,128)(2,1)S(1)} %join.1.y0), channel_id=1, source_target_pairs={{0,3},{1,0},{2,1},{3,2},{4,7},{5,4},{6,5},{7,6},{8,11},{9,8},{10,9... | collective-permute-start | bytes 393224 | tf_op jit(solution)/shard_map/ppermute | solution.py:23
  43.3 2.0 %collective-permute-start.7 = (bf16[1024,256]{1,0:T(8,128)(2,1)S(1)}, bf16[1024,256]{1,0:T(8,128)(2,1)S(1)}, u32[]{:S(2)}, u32[]{:S(2)}) collective-permute-start(bf16[1024,256]{1,0:T(8,128)(2,1)S(1)} %rotate.1.rows.mine), channel_id=1, source_target_pairs={{0,4},{4,0},{8,12},{12,8},{16,20},{20,16},{24,28},{28,24},{32,36},... | collective-permute-start | bytes 1572872 | tf_op jit(solution)/shard_map/ppermute | solution.py:39
  47.2 13.9 %collective-permute-start.9 = (bf16[128,1536]{1,0:T(8,128)(2,1)S(1)}, bf16[128,1536]{1,0:T(8,128)(2,1)S(1)}, u32[]{:S(2)}, u32[]{:S(2)}) collective-permute-start(bf16[128,1536]{1,0:T(8,128)(2,1)S(1)} %attend1.1), channel_id=1, source_target_pairs={{0,1},{1,2},{2,3},{3,0},{4,7},{5,4},{6,5},{7,6},{8,9},{9,10},{10,1... | collective-permute-start | bytes 1179656 | tf_op jit(solution)/shard_map/ppermute | solution.py:34
  49.1 9.0 %collective-permute-start.8 = (bf16[512,256]{1,0:T(8,128)(2,1)S(1)}, bf16[512,256]{1,0:T(8,128)(2,1)S(1)}, u32[]{:S(2)}, u32[]{:S(2)}) collective-permute-start(bf16[512,256]{1,0:T(8,128)(2,1)S(1)} %get-tuple-element.59), channel_id=1, source_target_pairs={{0,32},{4,36},{8,40},{12,44},{16,48},{20,52},{24,56},{28,60},{32,0... | collective-permute-start | bytes 786440 | tf_op jit(solution)/shard_map/ppermute | solution.py:39
  51.3 14.6 %collective-permute-start.10 = (bf16[128,1536]{1,0:T(8,128)(2,1)S(1)}, bf16[128,1536]{1,0:T(8,128)(2,1)S(1)}, u32[]{:S(2)}, u32[]{:S(2)}) collective-permute-start(bf16[128,1536]{1,0:T(8,128)(2,1)S(1)} %attend2.1), channel_id=1, source_target_pairs={{0,2},{1,3},{2,0},{3,1},{4,6},{5,7},{6,4},{7,5},{8,10},{9,11},{10,... | collective-permute-start | bytes 1179656 | tf_op jit(solution)/shard_map/ppermute | solution.py:23
  56.5 10.9 %collective-permute-start.11 = (bf16[128,1536]{1,0:T(8,128)(2,1)S(1)}, bf16[128,1536]{1,0:T(8,128)(2,1)S(1)}, u32[]{:S(2)}, u32[]{:S(2)}) collective-permute-start(bf16[128,1536]{1,0:T(8,128)(2,1)S(1)} %attend3.1), channel_id=1, source_target_pairs={{0,3},{1,0},{2,1},{3,2},{4,5},{5,6},{6,7},{7,4},{8,11},{9,8},{10,9... | collective-permute-start | bytes 1179656 | tf_op jit(solution)/shard_map/ppermute | solution.py:34
  58.1 17.5 %copy-start.2 = (bf16[1152,1536]{1,0:T(8,128)(2,1)S(1)}, bf16[1152,1536]{1,0:T(8,128)(2,1)}, u32[]{:S(2)}) copy-start(bf16[1152,1536]{1,0:T(8,128)(2,1)} %refs_5_.3) | copy-start | bytes 10616836
  60.0 7.3 %collective-permute-start.12 = (bf16[256,256]{1,0:T(8,128)(2,1)S(1)}, bf16[256,256]{1,0:T(8,128)(2,1)S(1)}, u32[]{:S(2)}, u32[]{:S(2)}) collective-permute-start(bf16[256,256]{1,0:T(8,128)(2,1)S(1)} %get-tuple-element.63), channel_id=1, source_target_pairs={{0,96},{4,100},{8,104},{12,108},{16,112},{20,116},{24,120},{28,124... | collective-permute-start | bytes 393224 | tf_op jit(solution)/shard_map/ppermute | solution.py:39
  67.8 11.6 %collective-permute-start.14 = (bf16[128,1536]{1,0:T(8,128)(2,1)S(1)}, bf16[128,1536]{1,0:T(8,128)(2,1)S(1)}, u32[]{:S(2)}, u32[]{:S(2)}) collective-permute-start(bf16[128,1536]{1,0:T(8,128)(2,1)S(1)} %get-tuple-element.64.refs_1_), channel_id=1, source_target_pairs={{0,1},{1,2},{2,3},{3,0},{4,7},{5,4},{6,5},{7,6},{8,9},{9,10},{10,1... | collective-permute-start | bytes 1179656 | tf_op jit(solution)/shard_map/ppermute | solution.py:34
  69.4 13.8 %collective-permute-start.15 = (bf16[128,1536]{1,0:T(8,128)(2,1)S(1)}, bf16[128,1536]{1,0:T(8,128)(2,1)S(1)}, u32[]{:S(2)}, u32[]{:S(2)}) collective-permute-start(bf16[128,1536]{1,0:T(8,128)(2,1)S(1)} %get-tuple-element.64.refs_1_), channel_id=1, source_target_pairs={{0,3},{1,0},{2,1},{3,2},{4,5},{5,6},{6,7},{7,4},{8,11},{9,8},{10,9... | collective-permute-start | bytes 1179656 | tf_op jit(solution)/shard_map/ppermute | solution.py:34
  71.3 4.3 %collective-permute-start.13 = (bf16[128,256]{1,0:T(8,128)(2,1)S(1)}, bf16[128,256]{1,0:T(8,128)(2,1)S(1)}, u32[]{:S(2)}, u32[]{:S(2)}) collective-permute-start(bf16[128,256]{1,0:T(8,128)(2,1)S(1)} %get-tuple-element.66), channel_id=1, source_target_pairs={{0,8},{4,12},{8,0},{12,4},{16,24},{20,28},{24,16},{28,20},{32,40},... | collective-permute-start | bytes 196616 | tf_op jit(solution)/shard_map/ppermute | solution.py:39
  78.0 5.2 %collective-permute-start.16 = (bf16[64,256]{1,0:T(8,128)(2,1)S(1)}, bf16[64,256]{1,0:T(8,128)(2,1)S(1)}, u32[]{:S(2)}, u32[]{:S(2)}) collective-permute-start(bf16[64,256]{1,0:T(8,128)(2,1)S(1)} %get-tuple-element.71), channel_id=1, source_target_pairs={{0,24},{4,28},{8,16},{12,20},{16,8},{20,12},{24,0},{28,4},{32,56},... | collective-permute-start | bytes 98312 | tf_op jit(solution)/shard_map/ppermute | solution.py:39
  79.4 11.6 %collective-permute-start.17 = (bf16[128,1536]{1,0:T(8,128)(2,1)S(1)}, bf16[128,1536]{1,0:T(8,128)(2,1)S(1)}, u32[]{:S(2)}, u32[]{:S(2)}) collective-permute-start(bf16[128,1536]{1,0:T(8,128)(2,1)S(1)} %collective-permute-done.14.refs_1_), channel_id=1, source_target_pairs={{0,1},{1,2},{2,3},{3,0},{4,7},{5,4},{6,5},{7,6},{8,9},{9,10},{10,1... | collective-permute-start | bytes 1179656 | tf_op jit(solution)/shard_map/ppermute | solution.py:34
  88.0 10.2 %collective-permute-start.18 = (bf16[384,384]{1,0:T(8,128)(2,1)S(1)}, bf16[384,384]{1,0:T(8,128)(2,1)S(1)}, u32[]{:S(2)}, u32[]{:S(2)}) collective-permute-start(bf16[384,384]{1,0:T(8,128)(2,1)S(1)} %get-tuple-element.78), channel_id=1, source_target_pairs={{0,2},{1,3},{2,0},{3,1},{4,6},{5,7},{6,4},{7,5},{8,10},{9,11},{10,... | collective-permute-start | bytes 884744 | tf_op jit(solution)/shard_map/ppermute | solution.py:23
  89.3 15.0 %collective-permute-start.19 = (bf16[384,384]{1,0:T(8,128)(2,1)S(1)}, bf16[384,384]{1,0:T(8,128)(2,1)S(1)}, u32[]{:S(2)}, u32[]{:S(2)}) collective-permute-start(bf16[384,384]{1,0:T(8,128)(2,1)S(1)} %get-tuple-element.79), channel_id=1, source_target_pairs={{0,1},{1,2},{2,3},{3,0},{4,7},{5,4},{6,5},{7,6},{8,9},{9,10},{10,1... | collective-permute-start | bytes 884744 | tf_op jit(solution)/shard_map/ppermute | solution.py:34
  93.4 12.7 %collective-permute-start.20 = (bf16[128,384]{1,0:T(8,128)(2,1)S(1)}, bf16[128,384]{1,0:T(8,128)(2,1)S(1)}, u32[]{:S(2)}, u32[]{:S(2)}) collective-permute-start(bf16[128,384]{1,0:T(8,128)(2,1)S(1)} %get-tuple-element.80), channel_id=1, source_target_pairs={{0,2},{1,3},{2,0},{3,1},{4,6},{5,7},{6,4},{7,5},{8,10},{9,11},{10,... | collective-permute-start | bytes 294920 | tf_op jit(solution)/shard_map/ppermute | solution.py:23
  94.9 12.4 %collective-permute-start.21 = (bf16[128,384]{1,0:T(8,128)(2,1)S(1)}, bf16[128,384]{1,0:T(8,128)(2,1)S(1)}, u32[]{:S(2)}, u32[]{:S(2)}) collective-permute-start(bf16[128,384]{1,0:T(8,128)(2,1)S(1)} %get-tuple-element.81), channel_id=1, source_target_pairs={{0,1},{1,2},{2,3},{3,0},{4,7},{5,4},{6,5},{7,6},{8,9},{9,10},{10,1... | collective-permute-start | bytes 294920 | tf_op jit(solution)/shard_map/ppermute | solution.py:34
  96.0 11.4 %collective-permute-start.22 = (bf16[512,384]{1,0:T(8,128)(2,1)S(1)}, bf16[512,384]{1,0:T(8,128)(2,1)S(1)}, u32[]{:S(2)}, u32[]{:S(2)}) collective-permute-start(bf16[512,384]{1,0:T(8,128)(2,1)S(1)} %get-tuple-element.82), channel_id=1, source_target_pairs={{0,3},{1,0},{2,1},{3,2},{4,5},{5,6},{6,7},{7,4},{8,11},{9,8},{10,9... | collective-permute-start | bytes 1179656 | tf_op jit(solution)/shard_map/ppermute | solution.py:34
  (5 other events, 51.9 us)

commit v8 on v7

--- a/solution.py
+++ b/solution.py
@@ -249,8 +249,9 @@
         o[lead:, :] = hold[lax.rem(f + target, 4)].astype(o.dtype)
 
 
-def early_sum_body(place, own, both, far, early2, early1, out):
+def early_sum_body(place, own, both, far, early2, early1, stay, landed, out, cache):
     step = own.shape[0]
+    cache[...] = (stay[...].astype(f32) + landed[...].astype(f32)).astype(bf16)
     core = place[2]
     near, other = lag(1, core), lag(3, core)
     out[0] = own[...]
@@ -452,15 +453,15 @@
             [*blocks, *cached, *res, *(b for _, b in before), gate_weight, up_weight, down_weight],
             [pltpu.VMEM((rows, hidden_units), bf16), pltpu.VMEM((4, rows, width), f32)],
             vmem=24 << 20,
-            flops=20_000_000_000 if before and cached else 2_000_000_000,
+            flops=20_000_000_000 if len(before) == 3 else 2_000_000_000,
         )
 
     own0, *own_sent, stay, go = feed("feed_own", [normed2], res=[residual], cached=[stay, landed])
     landed = from_partner(go, 6)
     m1, _ = lax.optimization_barrier((m1, own0))
     m2 = to_side(m1, (1, 3))
-    both0, early1, early2, early3, cache = feed(
-        "feed_near", [m1, m3], before=list(zip((1, 2, 3), own_sent)), cached=[stay, landed]
+    both0, early1, early2, early3 = feed(
+        "feed_near", [m1, m3], before=list(zip((1, 2, 3), own_sent))
     )
     early2 = from_peer(early2, 2)
     early1 = to_side(early1, (1, 3))
@@ -468,12 +469,12 @@
     whole = to_side(whole, (3, 1))
     late2 = from_peer(late2, 2)
     late1 = to_side(late1, (1, 3))
-    some = run(
+    some, cache = run(
         early_sum_body,
-        sds((4, step, width), f32),
+        [sds((4, step, width), f32), sds((held_rows, 2 * HD), bf16)],
         "early_sum",
         [place],
-        [own0, both0, far0, early2, early1],
+        [own0, both0, far0, early2, early1, stay, landed],
         flops=10_000_000_000,
     )
     output = run(

time: 110 us -> 109 us (level)
    ppermute x10, waiting for transfers between devices: 13.5 us -> 17.2 us  [to_side(): return lax.ppermute(block, ('seq', 'feat'), route)]
    ppermute x5, waiting for transfers between devices: 9.77 us -> 6.4 us  [from_partner(): return lax.ppermute(block, 'seq', [(i, i ^ bits) for i in range(n)])]
    ppermute x7, starting transfers between devices: 15.1 us -> 16.3 us  [from_peer(): lax.ppermute(block, 'feat', [(i, (i - distance) % n) for i in range(n)])]
  transfers between devices with their start and end apart: 23 -> 23, of which waited for: 15 -> 14; matrix products, arithmetic and copies ran while one was open for 9% -> 10% of each run, Pallas kernels for 17% -> 17%
where the time goes in v8:
time: 109 us; the launch traced here: 108 us
  starting transfers between devices  36.2 us (33%)
  waiting for transfers between devices  35.5 us (33%)
  Pallas kernels  24.9 us (23%)
  other arithmetic  7.72 us (7%)
  local copies, waits for them, and re-layouts  2.61 us (2%)
    pallas_call x16, Pallas kernels, run(): pl.pallas_call(body, out_shape=outs, in_specs=[SM] * len(scalars) + [VM]...  24.9 us
    ppermute x10, waiting for transfers between devices, to_side(): return lax.ppermute(block, ('seq', 'feat'), route)  17.2 us
    ppermute x7, starting transfers between devices, from_peer(): lax.ppermute(block, 'feat', [(i, (i - distance) % n) for i in range(n)])  16.3 us
    ppermute x10, starting transfers between devices, to_side(): return lax.ppermute(block, ('seq', 'feat'), route)  13.7 us
    ppermute x7, waiting for transfers between devices, from_peer(): lax.ppermute(block, 'feat', [(i, (i - distance) % n) for i in range(n)])  9.16 us
    ppermute x5, waiting for transfers between devices, from_partner(): return lax.ppermute(block, 'seq', [(i, i ^ bits) for i in range(n)])  6.4 us
    ppermute x1, starting transfers between devices, from_earlier(): lax.ppermute(block, 'seq', [(i - distance, i) for i in range(distance, n)])  3.83 us
    neg x1, other arithmetic, shards(): sine = jnp.concatenate([-sine, sine], axis=1)  2.95 us
  transfers between devices with their start and end apart: 23, of which 14 were waited for; matrix products, arithmetic and copies ran while one was open for 10% of the time, Pallas kernels for 17%

profile of v8, /device:TPU:6, one launch (start us, length us, event | category | flops | bytes accessed | tf_op | source)
XLA Modules:
  0.0 107.8 jit_solution(6201029567164444002)
XLA Ops:
  0.6 3.3 %collective-permute-start.1 = (bf16[512,384]{1,0:T(8,128)(2,1)}, bf16[512,384]{1,0:T(8,128)(2,1)S(1)}, u32[]{:S(2)}, u32[]{:S(2)}) collective-permute-start(bf16[512,384]{1,0:T(8,128)(2,1)} %source.1), channel_id=1, source_target_pairs={{0,2},{1,3},{2,0},{3,1},{4,6},{5,7},{6,4},{7,5},{8,10},{9,11},{10,... | collective-permute-start | bytes 1179656 | tf_op jit(solution)/shard_map/ppermute | solution.py:23
  4.6 2.6 %collective-permute-start.2 = (bf16[512,384]{1,0:T(8,128)(2,1)}, bf16[512,384]{1,0:T(8,128)(2,1)S(1)}, u32[]{:S(2)}, u32[]{:S(2)}) collective-permute-start(bf16[512,384]{1,0:T(8,128)(2,1)} %source.1), channel_id=1, source_target_pairs={{0,3},{1,0},{2,1},{3,2},{4,5},{5,6},{6,7},{7,4},{8,11},{9,8},{10,9... | collective-permute-start | bytes 1179656 | tf_op jit(solution)/shard_map/ppermute | solution.py:34
  12.2 3.0 %fusion = (f32[1024,64]{1,0:T(8,128)S(1)}, f32[1024,64]{1,0:T(8,128)}, f32[1024,64]{1,0:T(8,128)S(1)}) fusion(f32[64]{0:T(128)S(1)} %multiply_exponential_fusion, f32[1024]{0:T(1024)S(1)} %slice_convert_fusion), kind=kLoop, calls=%fused_computation.6 | loop fusion | flops 131072 | bytes 790784 | tf_op jit(solution)/shard_map/neg | solution.py:331
  17.6 4.1 %collective-permute-done.x1 = bf16[512,384]{1,0:T(8,128)(2,1)S(1)} collective-permute-done((bf16[512,384]{1,0:T(8,128)(2,1)}, bf16[512,384]{1,0:T(8,128)(2,1)S(1)}, u32[]{:S(2)}, u32[]{:S(2)}) %collective-permute-start) | collective-permute-done | bytes 393248 | tf_op jit(solution)/shard_map/ppermute | solution.py:34
  23.8 3.8 %collective-permute-start.3 = (bf16[256,128]{1,0:T(8,128)(2,1)S(1)}, bf16[256,128]{1,0:T(8,128)(2,1)S(1)}, u32[]{:S(2)}, u32[]{:S(2)}) collective-permute-start(bf16[256,128]{1,0:T(8,128)(2,1)S(1)} %get-tuple-element.51.a), channel_id=1, source_target_pairs={{0,8},{4,12},{8,16},{12,20},{16,24},{20,28},{24,32},{28,36},{32,40... | collective-permute-start | bytes 196616 | tf_op jit(solution)/shard_map/ppermute | solution.py:28
  27.6 1.8 %queries.1.q = bf16[512,384]{1,0:T(8,128)(2,1)S(1)} custom-call(s32[3]{0:T(128)S(1)} %pad_add_fusion.1.place.refs_0_, bf16[4,512,384]{2,1,0:T(8,128)(2,1)S(1)} %get-tuple-element.52.n_in, bf16[1536,384]{1,0:T(8,128)(2,1)S(1)} %copy-done.3, f32[1024,128]{1,0:T(8,128)S(1)} %pad_maximum_fusion.cosine, f32[1024,128]{1,0:T(8,128)S(1)} %pad_maximum_fusion.1.sine), custom_call_target="tpu_custom_call" | custom-call | flops 2000000000 | bytes 10000000 | tf_op jit(solution)/shard_map/queries/pallas_call | solution.py:48
  29.5 2.8 %collective-permute-done.3.b = bf16[256,128]{1,0:T(8,128)(2,1)S(1)} collective-permute-done((bf16[256,128]{1,0:T(8,128)(2,1)S(1)}, bf16[256,128]{1,0:T(8,128)(2,1)S(1)}, u32[]{:S(2)}, u32[]{:S(2)}) %collective-permute-start.3) | collective-permute-done | bytes 65568 | tf_op jit(solution)/shard_map/ppermute | solution.py:28
  33.7 2.8 %collective-permute-start.5 = (bf16[512,128]{1,0:T(8,128)(2,1)S(1)}, bf16[512,128]{1,0:T(8,128)(2,1)S(1)}, u32[]{:S(2)}, u32[]{:S(2)}) collective-permute-start(bf16[512,128]{1,0:T(8,128)(2,1)S(1)} %join.1.y0), channel_id=1, source_target_pairs={{0,2},{1,3},{2,0},{3,1},{4,6},{5,7},{6,4},{7,5},{8,10},{9,11},{10,... | collective-permute-start | bytes 393224 | tf_op jit(solution)/shard_map/ppermute | solution.py:23
  39.2 2.9 %collective-permute-done.5.y2 = bf16[512,128]{1,0:T(8,128)(2,1)S(1)} collective-permute-done((bf16[512,128]{1,0:T(8,128)(2,1)S(1)}, bf16[512,128]{1,0:T(8,128)(2,1)S(1)}, u32[]{:S(2)}, u32[]{:S(2)}) %collective-permute-start.5) | collective-permute-done | bytes 131104 | tf_op jit(solution)/shard_map/ppermute | solution.py:23
  43.4 1.9 %collective-permute-done.7.sibling.theirs = bf16[1024,256]{1,0:T(8,128)(2,1)S(1)} collective-permute-done((bf16[1024,256]{1,0:T(8,128)(2,1)S(1)}, bf16[1024,256]{1,0:T(8,128)(2,1)S(1)}, u32[]{:S(2)}, u32[]{:S(2)}) %collective-permute-start.7) | collective-permute-done | bytes 524320 | tf_op jit(solution)/shard_map/ppermute | solution.py:39
  45.3 1.9 %attend1.1 = bf16[128,1536]{1,0:T(8,128)(2,1)S(1)} custom-call(s32[3]{0:T(128)S(1)} %pad_add_fusion.1.place.refs_0_, s32[8]{0:T(128)S(1)} %bitcast_subtract_fusion.offsets, bf16[512,384]{1,0:T(8,128)(2,1)S(1)} %queries.1.q, bf16[1024,256]{1,0:T(8,128)(2,1)S(1)} %rotate.1.rows.mine, bf16[1024,256]{1,0:T(8,128)(2,1)S(1)} %collective-permute-done.7.sibling.theirs, ...), custom_call_target="tpu_custom_call" | custom-call | flops 2000000000 | bytes 10000000 | tf_op jit(solution)/shard_map/attend1/pallas_call | solution.py:48
  49.4 1.9 %attend2.1 = bf16[128,1536]{1,0:T(8,128)(2,1)S(1)} custom-call(s32[3]{0:T(128)S(1)} %pad_add_fusion.1.place.refs_0_, s32[8]{0:T(128)S(1)} %bitcast_subtract_fusion.offsets, bf16[512,384]{1,0:T(8,128)(2,1)S(1)} %queries.1.q, bf16[1024,256]{1,0:T(8,128)(2,1)S(1)} %rotate.1.rows.mine, bf16[1024,256]{1,0:T(8,128)(2,1)S(1)} %collective-permute-done.7.sibling.theirs, ...), custom_call_target="tpu_custom_call" | custom-call | flops 2000000000 | bytes 10000000 | tf_op jit(solution)/shard_map/attend2/pallas_call | solution.py:48
  51.3 3.3 %collective-permute-start.10 = (bf16[128,1536]{1,0:T(8,128)(2,1)S(1)}, bf16[128,1536]{1,0:T(8,128)(2,1)S(1)}, u32[]{:S(2)}, u32[]{:S(2)}) collective-permute-start(bf16[128,1536]{1,0:T(8,128)(2,1)S(1)} %attend2.1), channel_id=1, source_target_pairs={{0,2},{1,3},{2,0},{3,1},{4,6},{5,7},{6,4},{7,5},{8,10},{9,11},{10,... | collective-permute-start | bytes 1179656 | tf_op jit(solution)/shard_map/ppermute | solution.py:23
  54.6 1.9 %attend3.1 = bf16[128,1536]{1,0:T(8,128)(2,1)S(1)} custom-call(s32[3]{0:T(128)S(1)} %pad_add_fusion.1.place.refs_0_, s32[8]{0:T(128)S(1)} %bitcast_subtract_fusion.offsets, bf16[512,384]{1,0:T(8,128)(2,1)S(1)} %queries.1.q, bf16[1024,256]{1,0:T(8,128)(2,1)S(1)} %rotate.1.rows.mine, bf16[1024,256]{1,0:T(8,128)(2,1)S(1)} %collective-permute-done.7.sibling.theirs, ...), custom_call_target="tpu_custom_call" | custom-call | flops 2000000000 | bytes 10000000 | tf_op jit(solution)/shard_map/attend3/pallas_call | solution.py:48
  58.1 1.9 %attend0.1 = (f32[128,1536]{1,0:T(8,128)S(1)}, bf16[256,256]{1,0:T(8,128)(2,1)S(1)}, bf16[256,256]{1,0:T(8,128)(2,1)S(1)}) custom-call(s32[3]{0:T(128)S(1)} %pad_add_fusion.1.place.refs_0_, s32[8]{0:T(128)S(1)} %bitcast_subtract_fusion.offsets, bf16[512,384]{1,0:T(8,128)(2,1)S(1)} %queries.1.q, bf16[1024,256]{1,0:T(8,128)(2,1)S(1)} %rotate.1.rows.mine, ...), custom_call_target="tpu_custom_call" | custom-call | flops 2000000000 | bytes 10000000 | tf_op jit(solution)/shard_map/attend0/pallas_call | solution.py:48
  61.0 4.9 %collective-permute-done.10.p2 = bf16[128,1536]{1,0:T(8,128)(2,1)S(1)} collective-permute-done((bf16[128,1536]{1,0:T(8,128)(2,1)S(1)}, bf16[128,1536]{1,0:T(8,128)(2,1)S(1)}, u32[]{:S(2)}, u32[]{:S(2)}) %collective-permute-start.10) | collective-permute-done | bytes 393248 | tf_op jit(solution)/shard_map/ppermute | solution.py:23
  69.4 1.9 %collective-permute-start.15 = (bf16[128,1536]{1,0:T(8,128)(2,1)S(1)}, bf16[128,1536]{1,0:T(8,128)(2,1)S(1)}, u32[]{:S(2)}, u32[]{:S(2)}) collective-permute-start(bf16[128,1536]{1,0:T(8,128)(2,1)S(1)} %get-tuple-element.65.refs_1_), channel_id=1, source_target_pairs={{0,3},{1,0},{2,1},{3,2},{4,5},{5,6},{6,7},{7,4},{8,11},{9,8},{10,9... | collective-permute-start | bytes 1179656 | tf_op jit(solution)/shard_map/ppermute | solution.py:34
  71.3 4.3 %collective-permute-done.13.refs_3_ = bf16[128,256]{1,0:T(8,128)(2,1)S(1)} collective-permute-done((bf16[128,256]{1,0:T(8,128)(2,1)S(1)}, bf16[128,256]{1,0:T(8,128)(2,1)S(1)}, u32[]{:S(2)}, u32[]{:S(2)}) %collective-permute-start.13) | collective-permute-done | bytes 65568 | tf_op jit(solution)/shard_map/ppermute | solution.py:39
  75.6 2.4 %feed_own.1 = (f32[128,384]{1,0:T(8,128)S(1)}, bf16[128,384]{1,0:T(8,128)(2,1)S(1)}, bf16[128,384]{1,0:T(8,128)(2,1)S(1)}, bf16[128,384]{1,0:T(8,128)(2,1)S(1)},...) custom-call(s32[3]{0:T(128)S(1)} %pad_add_fusion.1.place.refs_0_, ...), custom_call_target="tpu_custom_call" | custom-call | flops 2000000000 | bytes 10000000 | tf_op jit(solution)/shard_map/feed_own/pallas_call | solution.py:48
  81.1 4.1 %feed_near.1 = (f32[256,384]{1,0:T(8,128)S(1)}, bf16[384,384]{1,0:T(8,128)(2,1)S(1)}, bf16[384,384]{1,0:T(8,128)(2,1)S(1)}, bf16[384,384]{1,0:T(8,128)(2,1)S(1)}) custom-call(s32[3]{0:T(128)S(1)} %pad_add_fusion.1.place.refs_0_, bf16[128,1536]{1,0:T(8,128)(2,1)S(1)} %collective-permute-done.14.refs_1_, ...), custom_call_target="tpu_custom_call" | custom-call | flops 20000000000 | bytes 100000000 | tf_op jit(solution)/shard_map/feed_near/pallas_call | solution.py:48
  85.2 2.5 %collective-permute-start.17 = (bf16[384,384]{1,0:T(8,128)(2,1)S(1)}, bf16[384,384]{1,0:T(8,128)(2,1)S(1)}, u32[]{:S(2)}, u32[]{:S(2)}) collective-permute-start(bf16[384,384]{1,0:T(8,128)(2,1)S(1)} %get-tuple-element.77), channel_id=1, source_target_pairs={{0,2},{1,3},{2,0},{3,1},{4,6},{5,7},{6,4},{7,5},{8,10},{9,11},{10,... | collective-permute-start | bytes 884744 | tf_op jit(solution)/shard_map/ppermute | solution.py:23
  89.4 2.4 %feed_far.1 = (f32[128,384]{1,0:T(8,128)S(1)}, bf16[128,384]{1,0:T(8,128)(2,1)S(1)}, bf16[128,384]{1,0:T(8,128)(2,1)S(1)}, bf16[512,384]{1,0:T(8,128)(2,1)S(1)}) custom-call(s32[3]{0:T(128)S(1)} %pad_add_fusion.1.place.refs_0_, bf16[128,1536]{1,0:T(8,128)(2,1)S(1)} %collective-permute-done.16.refs_1_, bf16[384,384]{1,0:T(8,128)(2,1)S(1)} %get-tuple-element.75.refs_2_, ...), custom_call_target="tpu_custom_call" | custom-call | flops 2000000000 | bytes 10000000 | tf_op jit(solution)/shard_map/feed_far/pallas_call | solution.py:48
  93.3 2.1 %collective-permute-start.21 = (bf16[128,384]{1,0:T(8,128)(2,1)S(1)}, bf16[128,384]{1,0:T(8,128)(2,1)S(1)}, u32[]{:S(2)}, u32[]{:S(2)}) collective-permute-start(bf16[128,384]{1,0:T(8,128)(2,1)S(1)} %get-tuple-element.83), channel_id=1, source_target_pairs={{0,1},{1,2},{2,3},{3,0},{4,7},{5,4},{6,5},{7,6},{8,9},{9,10},{10,1... | collective-permute-start | bytes 294920 | tf_op jit(solution)/shard_map/ppermute | solution.py:34
  96.6 7.2 %collective-permute-done.18.early1 = bf16[384,384]{1,0:T(8,128)(2,1)S(1)} collective-permute-done((bf16[384,384]{1,0:T(8,128)(2,1)S(1)}, bf16[384,384]{1,0:T(8,128)(2,1)S(1)}, u32[]{:S(2)}, u32[]{:S(2)}) %collective-permute-start.18) | collective-permute-done | bytes 294944 | tf_op jit(solution)/shard_map/ppermute | solution.py:34
  (71 shorter events, 35.3 us)
Async XLA Ops:
  0.6 17.0 %collective-permute-start.1 = (bf16[512,384]{1,0:T(8,128)(2,1)}, bf16[512,384]{1,0:T(8,128)(2,1)S(1)}, u32[]{:S(2)}, u32[]{:S(2)}) collective-permute-start(bf16[512,384]{1,0:T(8,128)(2,1)} %source.1), channel_id=1, source_target_pairs={{0,2},{1,3},{2,0},{3,1},{4,6},{5,7},{6,4},{7,5},{8,10},{9,11},{10,... | collective-permute-start | bytes 1179656 | tf_op jit(solution)/shard_map/ppermute | solution.py:23
  3.9 17.8 %collective-permute-start = (bf16[512,384]{1,0:T(8,128)(2,1)}, bf16[512,384]{1,0:T(8,128)(2,1)S(1)}, u32[]{:S(2)}, u32[]{:S(2)}) collective-permute-start(bf16[512,384]{1,0:T(8,128)(2,1)} %source.1), channel_id=1, source_target_pairs={{0,1},{1,2},{2,3},{3,0},{4,7},{5,4},{6,5},{7,6},{8,9},{9,10},{10,1... | collective-permute-start | bytes 1179656 | tf_op jit(solution)/shard_map/ppermute | solution.py:34
  4.6 17.5 %collective-permute-start.2 = (bf16[512,384]{1,0:T(8,128)(2,1)}, bf16[512,384]{1,0:T(8,128)(2,1)S(1)}, u32[]{:S(2)}, u32[]{:S(2)}) collective-permute-start(bf16[512,384]{1,0:T(8,128)(2,1)} %source.1), channel_id=1, source_target_pairs={{0,3},{1,0},{2,1},{3,2},{4,5},{5,6},{6,7},{7,4},{8,11},{9,8},{10,9... | collective-permute-start | bytes 1179656 | tf_op jit(solution)/shard_map/ppermute | solution.py:34
  23.8 8.4 %collective-permute-start.3 = (bf16[256,128]{1,0:T(8,128)(2,1)S(1)}, bf16[256,128]{1,0:T(8,128)(2,1)S(1)}, u32[]{:S(2)}, u32[]{:S(2)}) collective-permute-start(bf16[256,128]{1,0:T(8,128)(2,1)S(1)} %get-tuple-element.51.a), channel_id=1, source_target_pairs={{0,8},{4,12},{8,16},{12,20},{16,24},{20,28},{24,32},{28,36},{32,40... | collective-permute-start | bytes 196616 | tf_op jit(solution)/shard_map/ppermute | solution.py:28
  32.3 7.0 %collective-permute-start.6 = (bf16[512,128]{1,0:T(8,128)(2,1)S(1)}, bf16[512,128]{1,0:T(8,128)(2,1)S(1)}, u32[]{:S(2)}, u32[]{:S(2)}) collective-permute-start(bf16[512,128]{1,0:T(8,128)(2,1)S(1)} %join.1.y0), channel_id=1, source_target_pairs={{0,1},{1,2},{2,3},{3,0},{4,5},{5,6},{6,7},{7,4},{8,9},{9,10},{10,1... | collective-permute-start | bytes 393224 | tf_op jit(solution)/shard_map/ppermute | solution.py:23
  33.7 8.5 %collective-permute-start.5 = (bf16[512,128]{1,0:T(8,128)(2,1)S(1)}, bf16[512,128]{1,0:T(8,128)(2,1)S(1)}, u32[]{:S(2)}, u32[]{:S(2)}) collective-permute-start(bf16[512,128]{1,0:T(8,128)(2,1)S(1)} %join.1.y0), channel_id=1, source_target_pairs={{0,2},{1,3},{2,0},{3,1},{4,6},{5,7},{6,4},{7,5},{8,10},{9,11},{10,... | collective-permute-start | bytes 393224 | tf_op jit(solution)/shard_map/ppermute | solution.py:23
  36.5 5.7 %collective-permute-start.4 = (bf16[512,128]{1,0:T(8,128)(2,1)S(1)}, bf16[512,128]{1,0:T(8,128)(2,1)S(1)}, u32[]{:S(2)}, u32[]{:S(2)}) collective-permute-start(bf16[512,128]{1,0:T(8,128)(2,1)S(1)} %join.1.y0), channel_id=1, source_target_pairs={{0,3},{1,0},{2,1},{3,2},{4,7},{5,4},{6,5},{7,6},{8,11},{9,8},{10,9... | collective-permute-start | bytes 393224 | tf_op jit(solution)/shard_map/ppermute | solution.py:23
  43.3 2.0 %collective-permute-start.7 = (bf16[1024,256]{1,0:T(8,128)(2,1)S(1)}, bf16[1024,256]{1,0:T(8,128)(2,1)S(1)}, u32[]{:S(2)}, u32[]{:S(2)}) collective-permute-start(bf16[1024,256]{1,0:T(8,128)(2,1)S(1)} %rotate.1.rows.mine), channel_id=1, source_target_pairs={{0,4},{4,0},{8,12},{12,8},{16,20},{20,16},{24,28},{28,24},{32,36},... | collective-permute-start | bytes 1572872 | tf_op jit(solution)/shard_map/ppermute | solution.py:39
  47.2 13.9 %collective-permute-start.9 = (bf16[128,1536]{1,0:T(8,128)(2,1)S(1)}, bf16[128,1536]{1,0:T(8,128)(2,1)S(1)}, u32[]{:S(2)}, u32[]{:S(2)}) collective-permute-start(bf16[128,1536]{1,0:T(8,128)(2,1)S(1)} %attend1.1), channel_id=1, source_target_pairs={{0,1},{1,2},{2,3},{3,0},{4,7},{5,4},{6,5},{7,6},{8,9},{9,10},{10,1... | collective-permute-start | bytes 1179656 | tf_op jit(solution)/shard_map/ppermute | solution.py:34
  49.1 9.0 %collective-permute-start.8 = (bf16[512,256]{1,0:T(8,128)(2,1)S(1)}, bf16[512,256]{1,0:T(8,128)(2,1)S(1)}, u32[]{:S(2)}, u32[]{:S(2)}) collective-permute-start(bf16[512,256]{1,0:T(8,128)(2,1)S(1)} %get-tuple-element.60), channel_id=1, source_target_pairs={{0,32},{4,36},{8,40},{12,44},{16,48},{20,52},{24,56},{28,60},{32,0... | collective-permute-start | bytes 786440 | tf_op jit(solution)/shard_map/ppermute | solution.py:39
  51.3 14.6 %collective-permute-start.10 = (bf16[128,1536]{1,0:T(8,128)(2,1)S(1)}, bf16[128,1536]{1,0:T(8,128)(2,1)S(1)}, u32[]{:S(2)}, u32[]{:S(2)}) collective-permute-start(bf16[128,1536]{1,0:T(8,128)(2,1)S(1)} %attend2.1), channel_id=1, source_target_pairs={{0,2},{1,3},{2,0},{3,1},{4,6},{5,7},{6,4},{7,5},{8,10},{9,11},{10,... | collective-permute-start | bytes 1179656 | tf_op jit(solution)/shard_map/ppermute | solution.py:23
  56.5 10.9 %collective-permute-start.11 = (bf16[128,1536]{1,0:T(8,128)(2,1)S(1)}, bf16[128,1536]{1,0:T(8,128)(2,1)S(1)}, u32[]{:S(2)}, u32[]{:S(2)}) collective-permute-start(bf16[128,1536]{1,0:T(8,128)(2,1)S(1)} %attend3.1), channel_id=1, source_target_pairs={{0,3},{1,0},{2,1},{3,2},{4,5},{5,6},{6,7},{7,4},{8,11},{9,8},{10,9... | collective-permute-start | bytes 1179656 | tf_op jit(solution)/shard_map/ppermute | solution.py:34
  58.1 17.5 %copy-start.2 = (bf16[1152,1536]{1,0:T(8,128)(2,1)S(1)}, bf16[1152,1536]{1,0:T(8,128)(2,1)}, u32[]{:S(2)}) copy-start(bf16[1152,1536]{1,0:T(8,128)(2,1)} %refs_5_.3) | copy-start | bytes 10616836
  60.0 7.3 %collective-permute-start.12 = (bf16[256,256]{1,0:T(8,128)(2,1)S(1)}, bf16[256,256]{1,0:T(8,128)(2,1)S(1)}, u32[]{:S(2)}, u32[]{:S(2)}) collective-permute-start(bf16[256,256]{1,0:T(8,128)(2,1)S(1)} %get-tuple-element.64), channel_id=1, source_target_pairs={{0,96},{4,100},{8,104},{12,108},{16,112},{20,116},{24,120},{28,124... | collective-permute-start | bytes 393224 | tf_op jit(solution)/shard_map/ppermute | solution.py:39
  67.8 11.6 %collective-permute-start.14 = (bf16[128,1536]{1,0:T(8,128)(2,1)S(1)}, bf16[128,1536]{1,0:T(8,128)(2,1)S(1)}, u32[]{:S(2)}, u32[]{:S(2)}) collective-permute-start(bf16[128,1536]{1,0:T(8,128)(2,1)S(1)} %get-tuple-element.65.refs_1_), channel_id=1, source_target_pairs={{0,1},{1,2},{2,3},{3,0},{4,7},{5,4},{6,5},{7,6},{8,9},{9,10},{10,1... | collective-permute-start | bytes 1179656 | tf_op jit(solution)/shard_map/ppermute | solution.py:34
  69.4 11.7 %collective-permute-start.15 = (bf16[128,1536]{1,0:T(8,128)(2,1)S(1)}, bf16[128,1536]{1,0:T(8,128)(2,1)S(1)}, u32[]{:S(2)}, u32[]{:S(2)}) collective-permute-start(bf16[128,1536]{1,0:T(8,128)(2,1)S(1)} %get-tuple-element.65.refs_1_), channel_id=1, source_target_pairs={{0,3},{1,0},{2,1},{3,2},{4,5},{5,6},{6,7},{7,4},{8,11},{9,8},{10,9... | collective-permute-start | bytes 1179656 | tf_op jit(solution)/shard_map/ppermute | solution.py:34
  71.3 4.3 %collective-permute-start.13 = (bf16[128,256]{1,0:T(8,128)(2,1)S(1)}, bf16[128,256]{1,0:T(8,128)(2,1)S(1)}, u32[]{:S(2)}, u32[]{:S(2)}) collective-permute-start(bf16[128,256]{1,0:T(8,128)(2,1)S(1)} %get-tuple-element.67), channel_id=1, source_target_pairs={{0,8},{4,12},{8,0},{12,4},{16,24},{20,28},{24,16},{28,20},{32,40},... | collective-permute-start | bytes 196616 | tf_op jit(solution)/shard_map/ppermute | solution.py:39
  79.4 10.0 %collective-permute-start.16 = (bf16[128,1536]{1,0:T(8,128)(2,1)S(1)}, bf16[128,1536]{1,0:T(8,128)(2,1)S(1)}, u32[]{:S(2)}, u32[]{:S(2)}) collective-permute-start(bf16[128,1536]{1,0:T(8,128)(2,1)S(1)} %collective-permute-done.14.refs_1_), channel_id=1, source_target_pairs={{0,1},{1,2},{2,3},{3,0},{4,7},{5,4},{6,5},{7,6},{8,9},{9,10},{10,1... | collective-permute-start | bytes 1179656 | tf_op jit(solution)/shard_map/ppermute | solution.py:34
  85.2 11.4 %collective-permute-start.17 = (bf16[384,384]{1,0:T(8,128)(2,1)S(1)}, bf16[384,384]{1,0:T(8,128)(2,1)S(1)}, u32[]{:S(2)}, u32[]{:S(2)}) collective-permute-start(bf16[384,384]{1,0:T(8,128)(2,1)S(1)} %get-tuple-element.77), channel_id=1, source_target_pairs={{0,2},{1,3},{2,0},{3,1},{4,6},{5,7},{6,4},{7,5},{8,10},{9,11},{10,... | collective-permute-start | bytes 884744 | tf_op jit(solution)/shard_map/ppermute | solution.py:23
  87.7 16.0 %collective-permute-start.18 = (bf16[384,384]{1,0:T(8,128)(2,1)S(1)}, bf16[384,384]{1,0:T(8,128)(2,1)S(1)}, u32[]{:S(2)}, u32[]{:S(2)}) collective-permute-start(bf16[384,384]{1,0:T(8,128)(2,1)S(1)} %get-tuple-element.78), channel_id=1, source_target_pairs={{0,1},{1,2},{2,3},{3,0},{4,7},{5,4},{6,5},{7,6},{8,9},{9,10},{10,1... | collective-permute-start | bytes 884744 | tf_op jit(solution)/shard_map/ppermute | solution.py:34
  88.3 7.2 %collective-permute-start.19 = (bf16[64,256]{1,0:T(8,128)(2,1)S(1)}, bf16[64,256]{1,0:T(8,128)(2,1)S(1)}, u32[]{:S(2)}, u32[]{:S(2)}) collective-permute-start(bf16[64,256]{1,0:T(8,128)(2,1)S(1)} %get-tuple-element.80), channel_id=1, source_target_pairs={{0,24},{4,28},{8,16},{12,20},{16,8},{20,12},{24,0},{28,4},{32,56},... | collective-permute-start | bytes 98312 | tf_op jit(solution)/shard_map/ppermute | solution.py:39
  91.8 13.1 %collective-permute-start.20 = (bf16[128,384]{1,0:T(8,128)(2,1)S(1)}, bf16[128,384]{1,0:T(8,128)(2,1)S(1)}, u32[]{:S(2)}, u32[]{:S(2)}) collective-permute-start(bf16[128,384]{1,0:T(8,128)(2,1)S(1)} %get-tuple-element.82), channel_id=1, source_target_pairs={{0,2},{1,3},{2,0},{3,1},{4,6},{5,7},{6,4},{7,5},{8,10},{9,11},{10,... | collective-permute-start | bytes 294920 | tf_op jit(solution)/shard_map/ppermute | solution.py:23
  93.3 13.1 %collective-permute-start.21 = (bf16[128,384]{1,0:T(8,128)(2,1)S(1)}, bf16[128,384]{1,0:T(8,128)(2,1)S(1)}, u32[]{:S(2)}, u32[]{:S(2)}) collective-permute-start(bf16[128,384]{1,0:T(8,128)(2,1)S(1)} %get-tuple-element.83), channel_id=1, source_target_pairs={{0,1},{1,2},{2,3},{3,0},{4,7},{5,4},{6,5},{7,6},{8,9},{9,10},{10,1... | collective-permute-start | bytes 294920 | tf_op jit(solution)/shard_map/ppermute | solution.py:34
  95.5 10.9 %collective-permute-start.22 = (bf16[512,384]{1,0:T(8,128)(2,1)S(1)}, bf16[512,384]{1,0:T(8,128)(2,1)S(1)}, u32[]{:S(2)}, u32[]{:S(2)}) collective-permute-start(bf16[512,384]{1,0:T(8,128)(2,1)S(1)} %get-tuple-element.84), channel_id=1, source_target_pairs={{0,3},{1,0},{2,1},{3,2},{4,5},{5,6},{6,7},{7,4},{8,11},{9,8},{10,9... | collective-permute-start | bytes 1179656 | tf_op jit(solution)/shard_map/ppermute | solution.py:34
  (5 other events, 51.9 us)

commit v9 on v8

--- a/solution.py
+++ b/solution.py
@@ -357,8 +357,8 @@
 
     gain1 = first_gain.reshape(4, width)
     gain2 = second_gain.reshape(1, full)
-    x1, x2, x3, target, other, cosine, sine, offsets, place, gain1, gain2 = lax.optimization_barrier(
-        (x1, x2, x3, target, other, cosine, sine, offsets, place, gain1, gain2)
+    x1, x3, x2, target, other, cosine, sine, offsets, place, gain1, gain2 = lax.optimization_barrier(
+        (x1, x3, x2, target, other, cosine, sine, offsets, place, gain1, gain2)
     )
     step = tokens // 4
 

time: 109 us -> 109 us (level)
  the two profiles are of different devices: /device:TPU:6 before, /device:TPU:1 now
where the time goes in v9:
time: 109 us; the launch traced here: 108 us
  waiting for transfers between devices  36.8 us (34%)
  starting transfers between devices  35.3 us (32%)
  Pallas kernels  24.9 us (23%)
  other arithmetic  7.72 us (7%)
  local copies, waits for them, and re-layouts  2.61 us (2%)
    pallas_call x16, Pallas kernels, run(): pl.pallas_call(body, out_shape=outs, in_specs=[SM] * len(scalars) + [VM]...  24.9 us
    ppermute x10, waiting for transfers between devices, to_side(): return lax.ppermute(block, ('seq', 'feat'), route)  16.3 us
    ppermute x7, waiting for transfers between devices, from_peer(): lax.ppermute(block, 'feat', [(i, (i - distance) % n) for i in range(n)])  13.6 us
    ppermute x10, starting transfers between devices, to_side(): return lax.ppermute(block, ('seq', 'feat'), route)  12.7 us
    ppermute x5, starting transfers between devices, from_partner(): return lax.ppermute(block, 'seq', [(i, i ^ bits) for i in range(n)])  11 us
    ppermute x7, starting transfers between devices, from_peer(): lax.ppermute(block, 'feat', [(i, (i - distance) % n) for i in range(n)])  8.13 us
    ppermute x5, waiting for transfers between devices, from_partner(): return lax.ppermute(block, 'seq', [(i, i ^ bits) for i in range(n)])  6.82 us
    ppermute x1, starting transfers between devices, from_earlier(): lax.ppermute(block, 'seq', [(i - distance, i) for i in range(distance, n)])  3.54 us
  transfers between devices with their start and end apart: 23, of which 14 were waited for; matrix products, arithmetic and copies ran while one was open for 10% of the time, Pallas kernels for 17%

profile of v9, /device:TPU:1, one launch (start us, length us, event | category | flops | bytes accessed | tf_op | source)
XLA Modules:
  0.0 108.2 jit_solution(14489090402804373386)
XLA Ops:
  0.6 2.2 %collective-permute-start.1 = (bf16[512,384]{1,0:T(8,128)(2,1)}, bf16[512,384]{1,0:T(8,128)(2,1)S(1)}, u32[]{:S(2)}, u32[]{:S(2)}) collective-permute-start(bf16[512,384]{1,0:T(8,128)(2,1)} %source.1), channel_id=1, source_target_pairs={{0,3},{1,0},{2,1},{3,2},{4,5},{5,6},{6,7},{7,4},{8,11},{9,8},{10,9... | collective-permute-start | bytes 1179656 | tf_op jit(solution)/shard_map/ppermute | solution.py:34
  10.9 3.0 %fusion = (f32[1024,64]{1,0:T(8,128)S(1)}, f32[1024,64]{1,0:T(8,128)}, f32[1024,64]{1,0:T(8,128)S(1)}) fusion(f32[64]{0:T(128)S(1)} %multiply_exponential_fusion, f32[1024]{0:T(1024)S(1)} %slice_convert_fusion), kind=kLoop, calls=%fused_computation.6 | loop fusion | flops 131072 | bytes 790784 | tf_op jit(solution)/shard_map/neg | solution.py:331
  16.4 5.4 %collective-permute-done.2.x2 = bf16[512,384]{1,0:T(8,128)(2,1)S(1)} collective-permute-done((bf16[512,384]{1,0:T(8,128)(2,1)}, bf16[512,384]{1,0:T(8,128)(2,1)S(1)}, u32[]{:S(2)}, u32[]{:S(2)}) %collective-permute-start.2) | collective-permute-done | bytes 393248 | tf_op jit(solution)/shard_map/ppermute | solution.py:23
  23.5 3.5 %collective-permute-start.3 = (bf16[256,128]{1,0:T(8,128)(2,1)S(1)}, bf16[256,128]{1,0:T(8,128)(2,1)S(1)}, u32[]{:S(2)}, u32[]{:S(2)}) collective-permute-start(bf16[256,128]{1,0:T(8,128)(2,1)S(1)} %get-tuple-element.51.a), channel_id=1, source_target_pairs={{0,8},{4,12},{8,16},{12,20},{16,24},{20,28},{24,32},{28,36},{32,40... | collective-permute-start | bytes 196616 | tf_op jit(solution)/shard_map/ppermute | solution.py:28
  28.9 2.7 %collective-permute-start.6 = (bf16[512,128]{1,0:T(8,128)(2,1)S(1)}, bf16[512,128]{1,0:T(8,128)(2,1)S(1)}, u32[]{:S(2)}, u32[]{:S(2)}) collective-permute-start(bf16[512,128]{1,0:T(8,128)(2,1)S(1)} %join.1.y0), channel_id=1, source_target_pairs={{0,1},{1,2},{2,3},{3,0},{4,5},{5,6},{6,7},{7,4},{8,9},{9,10},{10,1... | collective-permute-start | bytes 393224 | tf_op jit(solution)/shard_map/ppermute | solution.py:23
  34.3 3.9 %collective-permute-done.5.y2 = bf16[512,128]{1,0:T(8,128)(2,1)S(1)} collective-permute-done((bf16[512,128]{1,0:T(8,128)(2,1)S(1)}, bf16[512,128]{1,0:T(8,128)(2,1)S(1)}, u32[]{:S(2)}, u32[]{:S(2)}) %collective-permute-start.5) | collective-permute-done | bytes 131104 | tf_op jit(solution)/shard_map/ppermute | solution.py:23
  39.3 2.4 %collective-permute-start.7 = (bf16[1024,256]{1,0:T(8,128)(2,1)S(1)}, bf16[1024,256]{1,0:T(8,128)(2,1)S(1)}, u32[]{:S(2)}, u32[]{:S(2)}) collective-permute-start(bf16[1024,256]{1,0:T(8,128)(2,1)S(1)} %rotate.1.rows.mine), channel_id=1, source_target_pairs={{0,4},{4,0},{8,12},{12,8},{16,20},{20,16},{24,28},{28,24},{32,36},... | collective-permute-start | bytes 1572872 | tf_op jit(solution)/shard_map/ppermute | solution.py:39
  43.2 1.9 %attend1.1 = bf16[128,1536]{1,0:T(8,128)(2,1)S(1)} custom-call(s32[3]{0:T(128)S(1)} %pad_add_fusion.1.place.refs_0_, s32[8]{0:T(128)S(1)} %bitcast_subtract_fusion.offsets, bf16[512,384]{1,0:T(8,128)(2,1)S(1)} %queries.1.q, bf16[1024,256]{1,0:T(8,128)(2,1)S(1)} %rotate.1.rows.mine, bf16[1024,256]{1,0:T(8,128)(2,1)S(1)} %collective-permute-done.7.sibling.theirs, ...), custom_call_target="tpu_custom_call" | custom-call | flops 2000000000 | bytes 10000000 | tf_op jit(solution)/shard_map/attend1/pallas_call | solution.py:48
  45.1 2.3 %collective-permute-start.9 = (bf16[128,1536]{1,0:T(8,128)(2,1)S(1)}, bf16[128,1536]{1,0:T(8,128)(2,1)S(1)}, u32[]{:S(2)}, u32[]{:S(2)}) collective-permute-start(bf16[128,1536]{1,0:T(8,128)(2,1)S(1)} %attend1.1), channel_id=1, source_target_pairs={{0,1},{1,2},{2,3},{3,0},{4,7},{5,4},{6,5},{7,6},{8,9},{9,10},{10,1... | collective-permute-start | bytes 1179656 | tf_op jit(solution)/shard_map/ppermute | solution.py:34
  48.1 3.6 %collective-permute-start.8 = (bf16[512,256]{1,0:T(8,128)(2,1)S(1)}, bf16[512,256]{1,0:T(8,128)(2,1)S(1)}, u32[]{:S(2)}, u32[]{:S(2)}) collective-permute-start(bf16[512,256]{1,0:T(8,128)(2,1)S(1)} %get-tuple-element.60), channel_id=1, source_target_pairs={{0,32},{4,36},{8,40},{12,44},{16,48},{20,52},{24,56},{28,60},{32,0... | collective-permute-start | bytes 786440 | tf_op jit(solution)/shard_map/ppermute | solution.py:39
  51.7 1.9 %attend2.1 = bf16[128,1536]{1,0:T(8,128)(2,1)S(1)} custom-call(s32[3]{0:T(128)S(1)} %pad_add_fusion.1.place.refs_0_, s32[8]{0:T(128)S(1)} %bitcast_subtract_fusion.offsets, bf16[512,384]{1,0:T(8,128)(2,1)S(1)} %queries.1.q, bf16[1024,256]{1,0:T(8,128)(2,1)S(1)} %rotate.1.rows.mine, bf16[1024,256]{1,0:T(8,128)(2,1)S(1)} %collective-permute-done.7.sibling.theirs, ...), custom_call_target="tpu_custom_call" | custom-call | flops 2000000000 | bytes 10000000 | tf_op jit(solution)/shard_map/attend2/pallas_call | solution.py:48
  54.2 1.9 %attend3.1 = bf16[128,1536]{1,0:T(8,128)(2,1)S(1)} custom-call(s32[3]{0:T(128)S(1)} %pad_add_fusion.1.place.refs_0_, s32[8]{0:T(128)S(1)} %bitcast_subtract_fusion.offsets, bf16[512,384]{1,0:T(8,128)(2,1)S(1)} %queries.1.q, bf16[1024,256]{1,0:T(8,128)(2,1)S(1)} %rotate.1.rows.mine, bf16[1024,256]{1,0:T(8,128)(2,1)S(1)} %collective-permute-done.7.sibling.theirs, ...), custom_call_target="tpu_custom_call" | custom-call | flops 2000000000 | bytes 10000000 | tf_op jit(solution)/shard_map/attend3/pallas_call | solution.py:48
  58.1 1.9 %attend0.1 = (f32[128,1536]{1,0:T(8,128)S(1)}, bf16[256,256]{1,0:T(8,128)(2,1)S(1)}, bf16[256,256]{1,0:T(8,128)(2,1)S(1)}) custom-call(s32[3]{0:T(128)S(1)} %pad_add_fusion.1.place.refs_0_, s32[8]{0:T(128)S(1)} %bitcast_subtract_fusion.offsets, bf16[512,384]{1,0:T(8,128)(2,1)S(1)} %queries.1.q, bf16[1024,256]{1,0:T(8,128)(2,1)S(1)} %rotate.1.rows.mine, ...), custom_call_target="tpu_custom_call" | custom-call | flops 2000000000 | bytes 10000000 | tf_op jit(solution)/shard_map/attend0/pallas_call | solution.py:48
  60.1 3.3 %collective-permute-start.12 = (bf16[256,256]{1,0:T(8,128)(2,1)S(1)}, bf16[256,256]{1,0:T(8,128)(2,1)S(1)}, u32[]{:S(2)}, u32[]{:S(2)}) collective-permute-start(bf16[256,256]{1,0:T(8,128)(2,1)S(1)} %get-tuple-element.64), channel_id=1, source_target_pairs={{0,96},{4,100},{8,104},{12,108},{16,112},{20,116},{24,120},{28,124... | collective-permute-start | bytes 393224 | tf_op jit(solution)/shard_map/ppermute | solution.py:39
  63.3 2.9 %collective-permute-done.10.p2 = bf16[128,1536]{1,0:T(8,128)(2,1)S(1)} collective-permute-done((bf16[128,1536]{1,0:T(8,128)(2,1)S(1)}, bf16[128,1536]{1,0:T(8,128)(2,1)S(1)}, u32[]{:S(2)}, u32[]{:S(2)}) %collective-permute-start.10) | collective-permute-done | bytes 393248 | tf_op jit(solution)/shard_map/ppermute | solution.py:23
  66.3 4.0 %collective-permute-done.11.p3 = bf16[128,1536]{1,0:T(8,128)(2,1)S(1)} collective-permute-done((bf16[128,1536]{1,0:T(8,128)(2,1)S(1)}, bf16[128,1536]{1,0:T(8,128)(2,1)S(1)}, u32[]{:S(2)}, u32[]{:S(2)}) %collective-permute-start.11) | collective-permute-done | bytes 393248 | tf_op jit(solution)/shard_map/ppermute | solution.py:34
  72.2 3.6 %collective-permute-done.13.refs_3_ = bf16[128,256]{1,0:T(8,128)(2,1)S(1)} collective-permute-done((bf16[128,256]{1,0:T(8,128)(2,1)S(1)}, bf16[128,256]{1,0:T(8,128)(2,1)S(1)}, u32[]{:S(2)}, u32[]{:S(2)}) %collective-permute-start.13) | collective-permute-done | bytes 65568 | tf_op jit(solution)/shard_map/ppermute | solution.py:39
  75.8 2.4 %feed_own.1 = (f32[128,384]{1,0:T(8,128)S(1)}, bf16[128,384]{1,0:T(8,128)(2,1)S(1)}, bf16[128,384]{1,0:T(8,128)(2,1)S(1)}, bf16[128,384]{1,0:T(8,128)(2,1)S(1)},...) custom-call(s32[3]{0:T(128)S(1)} %pad_add_fusion.1.place.refs_0_, ...), custom_call_target="tpu_custom_call" | custom-call | flops 2000000000 | bytes 10000000 | tf_op jit(solution)/shard_map/feed_own/pallas_call | solution.py:48
  78.2 3.2 %collective-permute-done.14.refs_1_ = bf16[128,1536]{1,0:T(8,128)(2,1)S(1)} collective-permute-done((bf16[128,1536]{1,0:T(8,128)(2,1)S(1)}, bf16[128,1536]{1,0:T(8,128)(2,1)S(1)}, u32[]{:S(2)}, u32[]{:S(2)}) %collective-permute-start.14) | collective-permute-done | bytes 393248 | tf_op jit(solution)/shard_map/ppermute | solution.py:34
  81.9 4.1 %feed_near.1 = (f32[256,384]{1,0:T(8,128)S(1)}, bf16[384,384]{1,0:T(8,128)(2,1)S(1)}, bf16[384,384]{1,0:T(8,128)(2,1)S(1)}, bf16[384,384]{1,0:T(8,128)(2,1)S(1)}) custom-call(s32[3]{0:T(128)S(1)} %pad_add_fusion.1.place.refs_0_, bf16[128,1536]{1,0:T(8,128)(2,1)S(1)} %collective-permute-done.14.refs_1_, ...), custom_call_target="tpu_custom_call" | custom-call | flops 20000000000 | bytes 100000000 | tf_op jit(solution)/shard_map/feed_near/pallas_call | solution.py:48
  86.7 2.8 %collective-permute-start.18 = (bf16[384,384]{1,0:T(8,128)(2,1)S(1)}, bf16[384,384]{1,0:T(8,128)(2,1)S(1)}, u32[]{:S(2)}, u32[]{:S(2)}) collective-permute-start(bf16[384,384]{1,0:T(8,128)(2,1)S(1)} %get-tuple-element.78), channel_id=1, source_target_pairs={{0,1},{1,2},{2,3},{3,0},{4,7},{5,4},{6,5},{7,6},{8,9},{9,10},{10,1... | collective-permute-start | bytes 884744 | tf_op jit(solution)/shard_map/ppermute | solution.py:34
  91.1 2.4 %feed_far.1 = (f32[128,384]{1,0:T(8,128)S(1)}, bf16[128,384]{1,0:T(8,128)(2,1)S(1)}, bf16[128,384]{1,0:T(8,128)(2,1)S(1)}, bf16[512,384]{1,0:T(8,128)(2,1)S(1)}) custom-call(s32[3]{0:T(128)S(1)} %pad_add_fusion.1.place.refs_0_, bf16[128,1536]{1,0:T(8,128)(2,1)S(1)} %collective-permute-done.16.refs_1_, bf16[384,384]{1,0:T(8,128)(2,1)S(1)} %get-tuple-element.75.refs_2_, ...), custom_call_target="tpu_custom_call" | custom-call | flops 2000000000 | bytes 10000000 | tf_op jit(solution)/shard_map/feed_far/pallas_call | solution.py:48
  95.8 2.0 %collective-permute-done.18.early1 = bf16[384,384]{1,0:T(8,128)(2,1)S(1)} collective-permute-done((bf16[384,384]{1,0:T(8,128)(2,1)S(1)}, bf16[384,384]{1,0:T(8,128)(2,1)S(1)}, u32[]{:S(2)}, u32[]{:S(2)}) %collective-permute-start.18) | collective-permute-done | bytes 294944 | tf_op jit(solution)/shard_map/ppermute | solution.py:34
  101.2 5.6 %collective-permute-done.22.whole = bf16[512,384]{1,0:T(8,128)(2,1)S(1)} collective-permute-done((bf16[512,384]{1,0:T(8,128)(2,1)S(1)}, bf16[512,384]{1,0:T(8,128)(2,1)S(1)}, u32[]{:S(2)}, u32[]{:S(2)}) %collective-permute-start.22) | collective-permute-done | bytes 393248 | tf_op jit(solution)/shard_map/ppermute | solution.py:34
  (71 shorter events, 34.4 us)
Async XLA Ops:
  0.6 15.7 %collective-permute-start.1 = (bf16[512,384]{1,0:T(8,128)(2,1)}, bf16[512,384]{1,0:T(8,128)(2,1)S(1)}, u32[]{:S(2)}, u32[]{:S(2)}) collective-permute-start(bf16[512,384]{1,0:T(8,128)(2,1)} %source.1), channel_id=1, source_target_pairs={{0,3},{1,0},{2,1},{3,2},{4,5},{5,6},{6,7},{7,4},{8,11},{9,8},{10,9... | collective-permute-start | bytes 1179656 | tf_op jit(solution)/shard_map/ppermute | solution.py:34
  2.8 13.5 %collective-permute-start = (bf16[512,384]{1,0:T(8,128)(2,1)}, bf16[512,384]{1,0:T(8,128)(2,1)S(1)}, u32[]{:S(2)}, u32[]{:S(2)}) collective-permute-start(bf16[512,384]{1,0:T(8,128)(2,1)} %source.1), channel_id=1, source_target_pairs={{0,1},{1,2},{2,3},{3,0},{4,7},{5,4},{6,5},{7,6},{8,9},{9,10},{10,1... | collective-permute-start | bytes 1179656 | tf_op jit(solution)/shard_map/ppermute | solution.py:34
  4.4 17.5 %collective-permute-start.2 = (bf16[512,384]{1,0:T(8,128)(2,1)}, bf16[512,384]{1,0:T(8,128)(2,1)S(1)}, u32[]{:S(2)}, u32[]{:S(2)}) collective-permute-start(bf16[512,384]{1,0:T(8,128)(2,1)} %source.1), channel_id=1, source_target_pairs={{0,2},{1,3},{2,0},{3,1},{4,6},{5,7},{6,4},{7,5},{8,10},{9,11},{10,... | collective-permute-start | bytes 1179656 | tf_op jit(solution)/shard_map/ppermute | solution.py:23
  23.5 5.4 %collective-permute-start.3 = (bf16[256,128]{1,0:T(8,128)(2,1)S(1)}, bf16[256,128]{1,0:T(8,128)(2,1)S(1)}, u32[]{:S(2)}, u32[]{:S(2)}) collective-permute-start(bf16[256,128]{1,0:T(8,128)(2,1)S(1)} %get-tuple-element.51.a), channel_id=1, source_target_pairs={{0,8},{4,12},{8,16},{12,20},{16,24},{20,28},{24,32},{28,36},{32,40... | collective-permute-start | bytes 196616 | tf_op jit(solution)/shard_map/ppermute | solution.py:28
  28.9 5.3 %collective-permute-start.6 = (bf16[512,128]{1,0:T(8,128)(2,1)S(1)}, bf16[512,128]{1,0:T(8,128)(2,1)S(1)}, u32[]{:S(2)}, u32[]{:S(2)}) collective-permute-start(bf16[512,128]{1,0:T(8,128)(2,1)S(1)} %join.1.y0), channel_id=1, source_target_pairs={{0,1},{1,2},{2,3},{3,0},{4,5},{5,6},{6,7},{7,4},{8,9},{9,10},{10,1... | collective-permute-start | bytes 393224 | tf_op jit(solution)/shard_map/ppermute | solution.py:23
  31.7 6.5 %collective-permute-start.5 = (bf16[512,128]{1,0:T(8,128)(2,1)S(1)}, bf16[512,128]{1,0:T(8,128)(2,1)S(1)}, u32[]{:S(2)}, u32[]{:S(2)}) collective-permute-start(bf16[512,128]{1,0:T(8,128)(2,1)S(1)} %join.1.y0), channel_id=1, source_target_pairs={{0,2},{1,3},{2,0},{3,1},{4,6},{5,7},{6,4},{7,5},{8,10},{9,11},{10,... | collective-permute-start | bytes 393224 | tf_op jit(solution)/shard_map/ppermute | solution.py:23
  33.1 5.1 %collective-permute-start.4 = (bf16[512,128]{1,0:T(8,128)(2,1)S(1)}, bf16[512,128]{1,0:T(8,128)(2,1)S(1)}, u32[]{:S(2)}, u32[]{:S(2)}) collective-permute-start(bf16[512,128]{1,0:T(8,128)(2,1)S(1)} %join.1.y0), channel_id=1, source_target_pairs={{0,3},{1,0},{2,1},{3,2},{4,7},{5,4},{6,5},{7,6},{8,11},{9,8},{10,9... | collective-permute-start | bytes 393224 | tf_op jit(solution)/shard_map/ppermute | solution.py:23
  39.3 3.9 %collective-permute-start.7 = (bf16[1024,256]{1,0:T(8,128)(2,1)S(1)}, bf16[1024,256]{1,0:T(8,128)(2,1)S(1)}, u32[]{:S(2)}, u32[]{:S(2)}) collective-permute-start(bf16[1024,256]{1,0:T(8,128)(2,1)S(1)} %rotate.1.rows.mine), channel_id=1, source_target_pairs={{0,4},{4,0},{8,12},{12,8},{16,20},{20,16},{24,28},{28,24},{32,36},... | collective-permute-start | bytes 1572872 | tf_op jit(solution)/shard_map/ppermute | solution.py:39
  45.1 18.2 %collective-permute-start.9 = (bf16[128,1536]{1,0:T(8,128)(2,1)S(1)}, bf16[128,1536]{1,0:T(8,128)(2,1)S(1)}, u32[]{:S(2)}, u32[]{:S(2)}) collective-permute-start(bf16[128,1536]{1,0:T(8,128)(2,1)S(1)} %attend1.1), channel_id=1, source_target_pairs={{0,1},{1,2},{2,3},{3,0},{4,7},{5,4},{6,5},{7,6},{8,9},{9,10},{10,1... | collective-permute-start | bytes 1179656 | tf_op jit(solution)/shard_map/ppermute | solution.py:34
  48.1 10.0 %collective-permute-start.8 = (bf16[512,256]{1,0:T(8,128)(2,1)S(1)}, bf16[512,256]{1,0:T(8,128)(2,1)S(1)}, u32[]{:S(2)}, u32[]{:S(2)}) collective-permute-start(bf16[512,256]{1,0:T(8,128)(2,1)S(1)} %get-tuple-element.60), channel_id=1, source_target_pairs={{0,32},{4,36},{8,40},{12,44},{16,48},{20,52},{24,56},{28,60},{32,0... | collective-permute-start | bytes 786440 | tf_op jit(solution)/shard_map/ppermute | solution.py:39
  53.6 12.7 %collective-permute-start.10 = (bf16[128,1536]{1,0:T(8,128)(2,1)S(1)}, bf16[128,1536]{1,0:T(8,128)(2,1)S(1)}, u32[]{:S(2)}, u32[]{:S(2)}) collective-permute-start(bf16[128,1536]{1,0:T(8,128)(2,1)S(1)} %attend2.1), channel_id=1, source_target_pairs={{0,2},{1,3},{2,0},{3,1},{4,6},{5,7},{6,4},{7,5},{8,10},{9,11},{10,... | collective-permute-start | bytes 1179656 | tf_op jit(solution)/shard_map/ppermute | solution.py:23
  56.1 14.2 %collective-permute-start.11 = (bf16[128,1536]{1,0:T(8,128)(2,1)S(1)}, bf16[128,1536]{1,0:T(8,128)(2,1)S(1)}, u32[]{:S(2)}, u32[]{:S(2)}) collective-permute-start(bf16[128,1536]{1,0:T(8,128)(2,1)S(1)} %attend3.1), channel_id=1, source_target_pairs={{0,3},{1,0},{2,1},{3,2},{4,5},{5,6},{6,7},{7,4},{8,11},{9,8},{10,9... | collective-permute-start | bytes 1179656 | tf_op jit(solution)/shard_map/ppermute | solution.py:34
  58.1 17.6 %copy-start.2 = (bf16[1152,1536]{1,0:T(8,128)(2,1)S(1)}, bf16[1152,1536]{1,0:T(8,128)(2,1)}, u32[]{:S(2)}) copy-start(bf16[1152,1536]{1,0:T(8,128)(2,1)} %refs_5_.3) | copy-start | bytes 10616836
  60.1 10.2 %collective-permute-start.12 = (bf16[256,256]{1,0:T(8,128)(2,1)S(1)}, bf16[256,256]{1,0:T(8,128)(2,1)S(1)}, u32[]{:S(2)}, u32[]{:S(2)}) collective-permute-start(bf16[256,256]{1,0:T(8,128)(2,1)S(1)} %get-tuple-element.64), channel_id=1, source_target_pairs={{0,96},{4,100},{8,104},{12,108},{16,112},{20,116},{24,120},{28,124... | collective-permute-start | bytes 393224 | tf_op jit(solution)/shard_map/ppermute | solution.py:39
  70.7 10.8 %collective-permute-start.14 = (bf16[128,1536]{1,0:T(8,128)(2,1)S(1)}, bf16[128,1536]{1,0:T(8,128)(2,1)S(1)}, u32[]{:S(2)}, u32[]{:S(2)}) collective-permute-start(bf16[128,1536]{1,0:T(8,128)(2,1)S(1)} %get-tuple-element.65.refs_1_), channel_id=1, source_target_pairs={{0,1},{1,2},{2,3},{3,0},{4,7},{5,4},{6,5},{7,6},{8,9},{9,10},{10,1... | collective-permute-start | bytes 1179656 | tf_op jit(solution)/shard_map/ppermute | solution.py:34
  71.1 10.8 %collective-permute-start.15 = (bf16[128,1536]{1,0:T(8,128)(2,1)S(1)}, bf16[128,1536]{1,0:T(8,128)(2,1)S(1)}, u32[]{:S(2)}, u32[]{:S(2)}) collective-permute-start(bf16[128,1536]{1,0:T(8,128)(2,1)S(1)} %get-tuple-element.65.refs_1_), channel_id=1, source_target_pairs={{0,3},{1,0},{2,1},{3,2},{4,5},{5,6},{6,7},{7,4},{8,11},{9,8},{10,9... | collective-permute-start | bytes 1179656 | tf_op jit(solution)/shard_map/ppermute | solution.py:34
  72.2 3.6 %collective-permute-start.13 = (bf16[128,256]{1,0:T(8,128)(2,1)S(1)}, bf16[128,256]{1,0:T(8,128)(2,1)S(1)}, u32[]{:S(2)}, u32[]{:S(2)}) collective-permute-start(bf16[128,256]{1,0:T(8,128)(2,1)S(1)} %get-tuple-element.67), channel_id=1, source_target_pairs={{0,8},{4,12},{8,0},{12,4},{16,24},{20,28},{24,16},{28,20},{32,40},... | collective-permute-start | bytes 196616 | tf_op jit(solution)/shard_map/ppermute | solution.py:39
  81.4 9.7 %collective-permute-start.16 = (bf16[128,1536]{1,0:T(8,128)(2,1)S(1)}, bf16[128,1536]{1,0:T(8,128)(2,1)S(1)}, u32[]{:S(2)}, u32[]{:S(2)}) collective-permute-start(bf16[128,1536]{1,0:T(8,128)(2,1)S(1)} %collective-permute-done.14.refs_1_), channel_id=1, source_target_pairs={{0,1},{1,2},{2,3},{3,0},{4,7},{5,4},{6,5},{7,6},{8,9},{9,10},{10,1... | collective-permute-start | bytes 1179656 | tf_op jit(solution)/shard_map/ppermute | solution.py:34
  86.0 9.8 %collective-permute-start.17 = (bf16[384,384]{1,0:T(8,128)(2,1)S(1)}, bf16[384,384]{1,0:T(8,128)(2,1)S(1)}, u32[]{:S(2)}, u32[]{:S(2)}) collective-permute-start(bf16[384,384]{1,0:T(8,128)(2,1)S(1)} %get-tuple-element.77), channel_id=1, source_target_pairs={{0,2},{1,3},{2,0},{3,1},{4,6},{5,7},{6,4},{7,5},{8,10},{9,11},{10,... | collective-permute-start | bytes 884744 | tf_op jit(solution)/shard_map/ppermute | solution.py:23
  86.7 11.2 %collective-permute-start.18 = (bf16[384,384]{1,0:T(8,128)(2,1)S(1)}, bf16[384,384]{1,0:T(8,128)(2,1)S(1)}, u32[]{:S(2)}, u32[]{:S(2)}) collective-permute-start(bf16[384,384]{1,0:T(8,128)(2,1)S(1)} %get-tuple-element.78), channel_id=1, source_target_pairs={{0,1},{1,2},{2,3},{3,0},{4,7},{5,4},{6,5},{7,6},{8,9},{9,10},{10,1... | collective-permute-start | bytes 884744 | tf_op jit(solution)/shard_map/ppermute | solution.py:34
  89.5 5.3 %collective-permute-start.19 = (bf16[64,256]{1,0:T(8,128)(2,1)S(1)}, bf16[64,256]{1,0:T(8,128)(2,1)S(1)}, u32[]{:S(2)}, u32[]{:S(2)}) collective-permute-start(bf16[64,256]{1,0:T(8,128)(2,1)S(1)} %get-tuple-element.80), channel_id=1, source_target_pairs={{0,24},{4,28},{8,16},{12,20},{16,8},{20,12},{24,0},{28,4},{32,56},... | collective-permute-start | bytes 98312 | tf_op jit(solution)/shard_map/ppermute | solution.py:39
  93.6 6.2 %collective-permute-start.20 = (bf16[128,384]{1,0:T(8,128)(2,1)S(1)}, bf16[128,384]{1,0:T(8,128)(2,1)S(1)}, u32[]{:S(2)}, u32[]{:S(2)}) collective-permute-start(bf16[128,384]{1,0:T(8,128)(2,1)S(1)} %get-tuple-element.82), channel_id=1, source_target_pairs={{0,2},{1,3},{2,0},{3,1},{4,6},{5,7},{6,4},{7,5},{8,10},{9,11},{10,... | collective-permute-start | bytes 294920 | tf_op jit(solution)/shard_map/ppermute | solution.py:23
  93.7 7.6 %collective-permute-start.21 = (bf16[128,384]{1,0:T(8,128)(2,1)S(1)}, bf16[128,384]{1,0:T(8,128)(2,1)S(1)}, u32[]{:S(2)}, u32[]{:S(2)}) collective-permute-start(bf16[128,384]{1,0:T(8,128)(2,1)S(1)} %get-tuple-element.83), channel_id=1, source_target_pairs={{0,1},{1,2},{2,3},{3,0},{4,7},{5,4},{6,5},{7,6},{8,9},{9,10},{10,1... | collective-permute-start | bytes 294920 | tf_op jit(solution)/shard_map/ppermute | solution.py:34
  94.7 12.1 %collective-permute-start.22 = (bf16[512,384]{1,0:T(8,128)(2,1)S(1)}, bf16[512,384]{1,0:T(8,128)(2,1)S(1)}, u32[]{:S(2)}, u32[]{:S(2)}) collective-permute-start(bf16[512,384]{1,0:T(8,128)(2,1)S(1)} %get-tuple-element.84), channel_id=1, source_target_pairs={{0,3},{1,0},{2,1},{3,2},{4,5},{5,6},{6,7},{7,4},{8,11},{9,8},{10,9... | collective-permute-start | bytes 1179656 | tf_op jit(solution)/shard_map/ppermute | solution.py:34
  (5 other events, 46.3 us)
